TPU v7x, 512 devices: a whole 4x4x16 slice. The times are simulated.
512 devices in a mesh: field: 16 (over y_hi, x, core), space: 32 (over y_lo, z).
Axes of the slice: x: 4, y: 4 (y_hi: 2, y_lo: 2; y = y_hi * 2 + y_lo), z: 16, core: 2. Of those that a mesh axis runs over, the one named last changes fastest.
Arguments:
- scalars: float32 [16, 32, 64, 16, 128], P('field', None, 'space'), may hold values from 0.02 to 1
- diffusivity: float32 [64, 16, 128], P('space'), may hold values from 0.02 to 0.1
- velocity: float32 [64, 16, 128], P('space'), may hold values from 0 to 0.35
- mixing: float32 [64, 16, 128], P('space'), may hold values from 0.1 to 0.6
- rates: float32 [256], replicated, may hold values from 0.05 to 2
- stoich: int32 [4, 256], replicated, may hold values from 0 to 31
- burn_tile: int32 [16, 32, 32], P('field'), may hold values from -1 to 31, as said below
- helper_slot: int32 [16, 32, 32], P('field'), may hold values from -1 to 127, as said below
Outputs:
- updated: float32 [16, 32, 64, 16, 128], P('field', None, 'space')
Inputs may be any that keep to these rules, and one draw needn't show every extreme that they name: Entries of burn_tile for one field and block are distinct tile numbers 0 to 31, live ones first and -1 after; one block lists at most 32, and some block of every field lists exactly 32. helper_slot is -1 exactly where burn_tile is -1; a live entry's slot h * 4 + p names helper block h and place p. In every field each slot 0 to 127 is used by exactly one live entry. The number of tiles that one block sends to one helper is at most 1, and equals 1 for some pair in every field.
All inputs are finite; a program needn't handle non-finite values.
Results may differ from a plain program's by a relative error of at most 0.0003.
Values sent between devices are 32-bit elements; how exact they have to be, the bound alone decides.
No kernel may reach another device: no remote copies, remote signals or barrier semaphores. Data moves between devices by JAX's collectives and lax.ppermute only.
A program may use at most 64 MiB of HBM per device.

v0:
```python
import functools

import jax
import jax.numpy as jnp
from jax import lax
from jax.experimental import pallas as pl
from jax.experimental.pallas import tpu as pltpu
from jax.sharding import PartitionSpec as P

NSUB = 4
LANES = 128
GROUP = 8
F32 = jnp.float32
BF16 = jnp.bfloat16
VMEM = pl.BlockSpec(memory_space=pltpu.VMEM)
SMEM = pl.BlockSpec(memory_space=pltpu.SMEM)
LIMIT = pltpu.CompilerParams(vmem_limit_bytes=24 << 20)


def shape(*dims):
    return jax.ShapeDtypeStruct(dims, F32)


def transport_kernel(parity_ref, tiles_ref, cells_ref, near_ref, far_ref, dif_ref, vel_ref, out_ref, rows_ref):
    species, planes, rows, _ = cells_ref.shape
    odd = parity_ref[0] == 1
    dif = [dif_ref[z] for z in range(planes)]
    vel = [vel_ref[z] for z in range(planes)]

    def one_species(s, carry):
        near, far = near_ref[s, 0], far_ref[s, 0]
        below = jnp.where(odd, near, far)
        above = jnp.where(odd, far, near)
        cells = [cells_ref[s, z] for z in range(planes)]
        column = [below, *cells, above]
        for z in range(planes):
            center, under, over = column[z + 1], column[z], column[z + 2]
            lateral = (
                pltpu.roll(center, 1, 1)
                + pltpu.roll(center, LANES - 1, 1)
                + pltpu.roll(center, 1, 0)
                + pltpu.roll(center, rows - 1, 0)
            )
            moved = center + dif[z] * (over + under + lateral - 6.0 * center) + vel[z] * (under - center)
            start = pl.multiple_of((s * planes + z) * rows, rows)
            rows_ref[pl.ds(start, rows), :] = moved
        return carry

    lax.fori_loop(0, species, one_species, 0, unroll=4)
    data = species * planes
    for y in range(rows):
        out_ref[y, 0:data, :] = rows_ref[pl.ds(y, data, stride=rows), :]
        out_ref[y, data : data + 8, :] = jnp.zeros((8, LANES), F32)
    for entry in range(tiles_ref.shape[0]):
        tile = tiles_ref[entry]

        @pl.when(tile >= 0)
        def _():
            y, z = lax.rem(tile, rows), lax.div(tile, rows)
            out_ref[y, pl.ds(data + z, 1), :] = jnp.ones((1, LANES), F32)


def in_parts(x, count):
    parts = []
    for part in range(count):
        parts.append(x.astype(BF16))
        if part + 1 < count:
            x = x - parts[-1].astype(F32)
    return parts


def chemistry(concent, pick, partner, produced, rates):
    substep = 1.0 / NSUB
    reactions = rates.shape[0]
    for repeat in range(NSUB):
        high, low = in_parts(concent, 2)
        picked = jnp.dot(pick, jnp.concatenate([high, low], 0), preferred_element_type=F32)
        losing = jnp.dot(partner, jnp.concatenate([high, high, low], 0), preferred_element_type=F32)
        progress = picked[:reactions] * picked[reactions:] * rates
        high, low = in_parts(progress, 2)
        making = jnp.dot(produced, high, preferred_element_type=F32) + jnp.dot(
            produced, low, preferred_element_type=F32
        )
        concent = (concent + substep * making) / (1.0 + substep * losing)
    return concent


def react_kernel(row_ref, in_ref, mix_ref, pick_ref, partner_ref, produced_ref, rates_ref, out_ref, list_ref):
    fields, data, _ = out_ref.shape
    planes = mix_ref.shape[0]
    species = data // planes
    row = row_ref[0]
    even = lax.broadcasted_iota(jnp.int32, (8, LANES), 0) % planes == 0
    mixing = jnp.where(even, mix_ref[0, pl.ds(row, 1), :], mix_ref[1, pl.ds(row, 1), :])

    def one_block(block, carry):
        at = pl.ds(pl.multiple_of(block * 8, 8), 8)
        cells = [in_ref[f, at, :] for f in range(fields)]
        total = cells[0]
        for f in range(1, fields):
            total = total + cells[f]
        ensemble = total * (1.0 / fields)
        for f in range(fields):
            out_ref[f, at, :] = cells[f] - mixing * (cells[f] - ensemble)
        return carry

    lax.fori_loop(0, data // 8, one_block, 0)
    marks = jnp.zeros((8, LANES), F32)
    for f in range(fields):
        marks = marks + in_ref[f, data : data + 8, :] * float(2**f)
    code = [jnp.max(marks[z : z + 1, :]).astype(jnp.int32) for z in range(planes)]
    count = jnp.int32(0)
    for z in range(planes):
        for f in range(fields):
            list_ref[count] = f * planes + z
            count = count + ((code[z] >> f) & 1)
    rates = jnp.concatenate([rates_ref[...]] * GROUP, 1)
    pick, partner, produced = pick_ref[...], partner_ref[...], produced_ref[...]

    @pl.loop(0, pl.cdiv(count, GROUP))
    def _(group):
        first = group * GROUP
        entries = [list_ref[jnp.minimum(first + j, count - 1)] for j in range(GROUP)]
        places = [(lax.div(e, planes), lax.rem(e, planes)) for e in entries]
        concent = jnp.concatenate([out_ref[f, pl.ds(z, species, stride=planes), :] for f, z in places], 1)
        concent = chemistry(concent, pick, partner, produced, rates)
        for j, (f, z) in enumerate(places):

            @pl.when(first + j < count)
            def _():
                out_ref[f, pl.ds(z, species, stride=planes), :] = concent[:, j * LANES : (j + 1) * LANES]


def home_kernel(in_ref, out_ref, rows_ref):
    pieces, data, _ = in_ref.shape
    for y in range(pieces):
        rows_ref[pl.ds(y, data, stride=pieces), :] = in_ref[y]
    out_ref[...] = rows_ref[...].reshape(out_ref.shape)


def one_hot_rows(indices, count):
    return (indices[:, None] == jnp.arange(count, dtype=jnp.int32)[None, :]).astype(F32)


def reaction_tables(stoich, rates, species):
    one, two = one_hot_rows(stoich[0], species), one_hot_rows(stoich[1], species)
    produced = one_hot_rows(stoich[2], species) + one_hot_rows(stoich[3], species)
    pick = jnp.concatenate([one, two], 0).astype(BF16)
    partner = jnp.dot((one * rates[:, None]).T, two, precision=lax.Precision.HIGHEST)
    partner = partner + partner.T
    high = lax.reduce_precision(partner, 8, 7)
    low = partner - high
    return (
        jnp.concatenate([pick, pick], 1),
        jnp.concatenate([high, low, high], 1).astype(BF16),
        produced.T.astype(BF16),
        jnp.broadcast_to(rates[:, None], (rates.shape[0], LANES)),
    )


def per_device(scalars, diffusivity, velocity, mixing, rates, stoich, burn_tile, helper_slot):
    block = lax.axis_index("space")
    blocks = lax.axis_size("space")
    fields = lax.axis_size("field")
    cells = scalars[0]
    species, planes, rows, width = cells.shape
    data = species * planes
    parity = block % 2
    near_pairs = [(i, i ^ 1) for i in range(blocks)]
    far_pairs = [(i, (i + 1 if i % 2 else i - 1) % blocks) for i in range(blocks)]
    far = lax.ppermute(lax.dynamic_slice_in_dim(cells, parity, 1, 1), "space", far_pairs)
    near = lax.ppermute(lax.dynamic_slice_in_dim(cells, 1 - parity, 1, 1), "space", near_pairs)
    tables = reaction_tables(stoich, rates, species)
    pieces = pl.pallas_call(
        transport_kernel,
        out_shape=shape(rows, data + 8, width),
        in_specs=[SMEM, SMEM] + [VMEM] * 5,
        out_specs=VMEM,
        scratch_shapes=[pltpu.VMEM((data * rows, width), F32)],
        compiler_params=LIMIT,
        name="transport",
    )(parity.reshape(1), burn_tile[0, block], cells, near, far, diffusivity, velocity)
    pieces = lax.all_to_all(pieces, "field", 0, 0, tiled=True)
    pieces = pl.pallas_call(
        react_kernel,
        out_shape=shape(fields, data, width),
        in_specs=[SMEM] + [VMEM] * 6,
        out_specs=VMEM,
        scratch_shapes=[pltpu.SMEM((fields * planes + 1,), jnp.int32)],
        compiler_params=LIMIT,
        name="react",
    )(lax.axis_index("field").reshape(1), pieces, mixing, *tables)
    pieces = lax.all_to_all(pieces, "field", 0, 0, tiled=True)
    updated = pl.pallas_call(
        home_kernel,
        out_shape=shape(species, planes, rows, width),
        in_specs=[VMEM],
        out_specs=VMEM,
        scratch_shapes=[pltpu.VMEM((data * rows, width), F32)],
        compiler_params=LIMIT,
        name="home",
    )(pieces)
    return updated[None]


def solution(mesh):
    return jax.shard_map(
        per_device,
        mesh=mesh,
        in_specs=(
            P("field", None, "space", None, None),
            P("space", None, None),
            P("space", None, None),
            P("space", None, None),
            P(),
            P(),
            P("field", None, None),
            P("field", None, None),
        ),
        out_specs=P("field", None, "space", None, None),
        check_vma=False,
    )
```

profile of v0, /device:TPU:1, one launch (start us, length us, event | category | flops | bytes accessed | tf_op | source)
XLA Modules:
  0.0 64.8 jit_solution(16560508558844966912)
XLA Ops:
  0.0 0.0 copy-start
  0.0 1.1 %dynamic-slice_bitcast_fusion = (f32[32,1,16,128]{3,2,1,0:T(8,128)S(1)}, f32[32,1,16,128]{3,2,1,0:T(8,128)S(1)}) fusion(f32[1,32,2,16,128]{4,3,2,1,0:T(8,128)} %param.8, s32[]{:T(128)S(6)} %select_n.19, s32[]{:T(128)S(6)} %select_n.18), kind=kLoop, calls=%fused_computation | loop fusion | bytes 1048584 | tf_op jit(solution)/shard_map/dynamic_slice | solution.py:171
  1.1 0.0 copy-start.5
  1.1 4.4 %collective-permute-start = (f32[32,1,16,128]{3,2,1,0:T(8,128)S(1)}, f32[32,1,16,128]{3,2,1,0:T(8,128)S(1)}, u32[]{:S(2)}, u32[]{:S(2)}) collective-permute-start(f32[32,1,16,128]{3,2,1,0:T(8,128)S(1)} %get-tuple-element.6), channel_id=1, source_target_pairs={{0,1},{1,0},{2,3},{3,2},{4,5},{5,4},{6,7},{7,6},{8,9},{9,8},{10,11... | collective-permute-start | bytes 786440 | tf_op jit(solution)/shard_map/ppermute | solution.py:172
  5.5 11.2 %collective-permute-start.1 = (f32[32,1,16,128]{3,2,1,0:T(8,128)S(1)}, f32[32,1,16,128]{3,2,1,0:T(8,128)S(1)}, u32[]{:S(2)}, u32[]{:S(2)}) collective-permute-start(f32[32,1,16,128]{3,2,1,0:T(8,128)S(1)} %get-tuple-element.5), channel_id=1, source_target_pairs={{0,31},{1,2},{2,1},{3,4},{4,3},{5,6},{6,5},{7,8},{8,7},{9,10},{10,... | collective-permute-start | bytes 786440 | tf_op jit(solution)/shard_map/ppermute | solution.py:171
  16.8 0.0 copy-done.5
  16.8 0.0 copy-start.6
  16.8 0.6 %copy-done.6 = f32[256]{0:T(256)S(1)} copy-done((f32[256]{0:T(256)S(1)}, f32[256]{0:T(256)}, u32[]{:S(2)}) %copy-start.6) | copy-done | bytes 1048
  17.5 0.1 fusion
  17.6 0.0 copy-done
  17.6 0.1 copy.12
  17.7 0.0 collective-permute-done.near_ref
  17.7 4.7 %collective-permute-done.1.far_ref = f32[32,1,16,128]{3,2,1,0:T(8,128)S(1)} collective-permute-done((f32[32,1,16,128]{3,2,1,0:T(8,128)S(1)}, f32[32,1,16,128]{3,2,1,0:T(8,128)S(1)}, u32[]{:S(2)}, u32[]{:S(2)}) %collective-permute-start.1) | collective-permute-done | bytes 262176 | tf_op jit(solution)/shard_map/ppermute | solution.py:171
  22.5 2.7 %transport.1 = f32[16,72,128]{2,1,0:T(8,128)} custom-call(s32[1]{0:T(128)} %bitcast.1.parity_ref, s32[32]{0:T(128)S(1)} %fusion.5.tiles_ref, f32[32,2,16,128]{3,2,1,0:T(8,128)S(1)} %bitcast.20, f32[32,1,16,128]{3,2,1,0:T(8,128)S(1)} %collective-permute-done.near_ref, f32[32,1,16,128]{3,2,1,0:T(8,128)S(1)} %collective-permute-done.1.far_ref, ...), custom_call_target="tpu_custom_call" | custom-call | tf_op jit(solution)/shard_map/transport/pallas_call | solution.py:174
  25.1 8.2 %all-to-all-start = ((f32[16,72,128]{2,1,0:T(8,128)}), f32[16,72,128]{2,1,0:T(8,128)S(1)}, u32[]{:S(2)}, u32[]{:S(2)}) async-start(f32[16,72,128]{2,1,0:T(8,128)} %transport.1), calls=%async_computation | async-start | bytes 1179648 | tf_op jit(solution)/shard_map/all_to_all | solution.py:183
  33.3 0.1 copy.11
  33.5 0.1 pad_maximum_fusion.1.partner_ref
  33.5 0.1 pad_maximum_fusion.pick_ref
  33.7 11.3 %all-to-all-done.in_ref = f32[16,72,128]{2,1,0:T(8,128)S(1)} async-done(((f32[16,72,128]{2,1,0:T(8,128)}), f32[16,72,128]{2,1,0:T(8,128)S(1)}, u32[]{:S(2)}, u32[]{:S(2)}) %all-to-all-start) | async-done | bytes 589856 | tf_op jit(solution)/shard_map/all_to_all | solution.py:183
  45.0 0.1 broadcast_in_dim.4.rates_ref
  45.1 0.6 copy-done.4
  45.7 2.9 %react.1 = f32[16,64,128]{2,1,0:T(8,128)S(1)} custom-call(s32[1]{0:T(128)} %bitcast.row_ref, f32[16,72,128]{2,1,0:T(8,128)S(1)} %all-to-all-done.in_ref, f32[2,16,128]{2,1,0:T(8,128)S(1)} %copy-done.4, bf16[512,64]{1,0:T(8,128)(2,1)S(1)} %pad_maximum_fusion.pick_ref, bf16[32,96]{1,0:T(8,128)(2,1)S(1)} %pad_maximum_fusion.1.partner_ref, ...), custom_call_target="tpu_custom_call" | custom-call | tf_op jit(solution)/shard_map/react/pallas_call | solution.py:184
  48.6 15.0 %all_to_all.10.in_ref = f32[16,64,128]{2,1,0:T(8,128)S(1)} all-to-all(f32[16,64,128]{2,1,0:T(8,128)S(1)} %react.1), channel_id=1, replica_groups=mesh['field'=16,'space'=32] {'field'}, dimensions={0} | all-to-all | bytes 1048576 | tf_op jit(solution)/shard_map/all_to_all | solution.py:193
  63.7 1.1 %home.1 = f32[32,2,16,128]{3,2,1,0:T(8,128)} custom-call(f32[16,64,128]{2,1,0:T(8,128)S(1)} %all_to_all.10.in_ref), custom_call_target="tpu_custom_call" | custom-call | tf_op jit(solution)/shard_map/home/pallas_call | solution.py:194
  (13 shorter events, 0.1 us)
Async XLA Ops:
  0.0 17.6 %copy-start = (s32[1,32,32]{2,1,0:T(8,128)S(1)}, s32[1,32,32]{2,1,0:T(8,128)}, u32[]{:S(2)}) copy-start(s32[1,32,32]{2,1,0:T(8,128)} %param.14) | copy-start | bytes 12292
  0.0 22.5 %copy-start.1 = (f32[1,32,2,16,128]{4,3,2,1,0:T(8,128)S(1)}, f32[1,32,2,16,128]{4,3,2,1,0:T(8,128)}, u32[]{:S(2)}) copy-start(f32[1,32,2,16,128]{4,3,2,1,0:T(8,128)} %param.8) | copy-start | bytes 1572868
  1.1 15.6 %copy-start.5 = (s32[4,256]{1,0:T(4,128)S(1)}, s32[4,256]{1,0:T(4,128)}, u32[]{:S(2)}) copy-start(s32[4,256]{1,0:T(4,128)} %param.13) | copy-start | bytes 12292
  1.1 16.6 %collective-permute-start = (f32[32,1,16,128]{3,2,1,0:T(8,128)S(1)}, f32[32,1,16,128]{3,2,1,0:T(8,128)S(1)}, u32[]{:S(2)}, u32[]{:S(2)}) collective-permute-start(f32[32,1,16,128]{3,2,1,0:T(8,128)S(1)} %get-tuple-element.6), channel_id=1, source_target_pairs={{0,1},{1,0},{2,3},{3,2},{4,5},{5,4},{6,7},{7,6},{8,9},{9,8},{10,11... | collective-permute-start | bytes 786440 | tf_op jit(solution)/shard_map/ppermute | solution.py:172
  5.5 16.9 %collective-permute-start.1 = (f32[32,1,16,128]{3,2,1,0:T(8,128)S(1)}, f32[32,1,16,128]{3,2,1,0:T(8,128)S(1)}, u32[]{:S(2)}, u32[]{:S(2)}) collective-permute-start(f32[32,1,16,128]{3,2,1,0:T(8,128)S(1)} %get-tuple-element.5), channel_id=1, source_target_pairs={{0,31},{1,2},{2,1},{3,4},{4,3},{5,6},{6,5},{7,8},{8,7},{9,10},{10,... | collective-permute-start | bytes 786440 | tf_op jit(solution)/shard_map/ppermute | solution.py:171
  16.8 0.7 %copy-start.6 = (f32[256]{0:T(256)S(1)}, f32[256]{0:T(256)}, u32[]{:S(2)}) copy-start(f32[256]{0:T(256)} %param.12) | copy-start | bytes 3076
  17.7 4.8 %copy-start.2 = (f32[2,16,128]{2,1,0:T(8,128)S(1)}, f32[2,16,128]{2,1,0:T(8,128)}, u32[]{:S(2)}) copy-start(f32[2,16,128]{2,1,0:T(8,128)} %dif_ref.1) | copy-start | bytes 49156
  17.7 4.8 %copy-start.3 = (f32[2,16,128]{2,1,0:T(8,128)S(1)}, f32[2,16,128]{2,1,0:T(8,128)}, u32[]{:S(2)}) copy-start(f32[2,16,128]{2,1,0:T(8,128)} %vel_ref.1) | copy-start | bytes 49156
  25.1 19.8 %all-to-all-start = ((f32[16,72,128]{2,1,0:T(8,128)}), f32[16,72,128]{2,1,0:T(8,128)S(1)}, u32[]{:S(2)}, u32[]{:S(2)}) async-start(f32[16,72,128]{2,1,0:T(8,128)} %transport.1), calls=%async_computation | async-start | bytes 1179648 | tf_op jit(solution)/shard_map/all_to_all | solution.py:183
  45.0 0.7 %copy-start.4 = (f32[2,16,128]{2,1,0:T(8,128)S(1)}, f32[2,16,128]{2,1,0:T(8,128)}, u32[]{:S(2)}) copy-start(f32[2,16,128]{2,1,0:T(8,128)} %mix_ref.1) | copy-start | bytes 49156
where the time goes:
time: 65.1 us; the launch traced here: 64.8 us
  starting transfers between devices  23.8 us (37%)
  waiting for transfers between devices  16 us (25%)
  blocking collectives  15 us (23%)
  Pallas kernels  6.69 us (10%)
  local copies, waits for them, and re-layouts  2.72 us (4%)
    all_to_all x1, blocking collectives, per_device(): pieces = lax.all_to_all(pieces, 'field', 0, 0, tiled=True)  15 us
    all_to_all x1, waiting for transfers between devices, per_device(): pieces = lax.all_to_all(pieces, 'field', 0, 0, tiled=True)  11.3 us
    ppermute x1, starting transfers between devices, per_device(): lax.ppermute(lax.dynamic_slice_in_dim(cells, parity, 1, 1), 'space', far_...  11.2 us
    all_to_all x1, starting transfers between devices, per_device(): pieces = lax.all_to_all(pieces, 'field', 0, 0, tiled=True)  8.18 us
    ppermute x1, waiting for transfers between devices, per_device(): lax.ppermute(lax.dynamic_slice_in_dim(cells, parity, 1, 1), 'space', far_...  4.73 us
    ppermute x1, starting transfers between devices, per_device(): lax.ppermute(lax.dynamic_slice_in_dim(cells, 1 - parity, 1, 1), 'space',...  4.36 us
    pallas_call x1, Pallas kernels, per_device(): pl.pallas_call(react_kernel, out_shape=shape(fields, data, width), in_spe...  2.94 us
    pallas_call x1, Pallas kernels, per_device(): pl.pallas_call(transport_kernel, out_shape=shape(rows, data + 8, width),...  2.67 us
  transfers between devices with their start and end apart: 3, of which 2 were waited for; matrix products, arithmetic and copies ran while one was open for 1% of the time, Pallas kernels for 0%

commit v1 on v0

--- a/solution.py
+++ b/solution.py
@@ -21,29 +21,49 @@
     return jax.ShapeDtypeStruct(dims, F32)
 
 
-def transport_kernel(parity_ref, tiles_ref, cells_ref, near_ref, far_ref, dif_ref, vel_ref, out_ref, rows_ref):
+def plane_kernel(plane, cells_ref, out_ref, sem):
+    copy = pltpu.make_async_copy(cells_ref.at[:, plane], out_ref, sem)
+    copy.start()
+    copy.wait()
+
+
+def plane_of(cells, plane):
+    species, _, rows, width = cells.shape
+    return pl.pallas_call(
+        functools.partial(plane_kernel, plane),
+        out_shape=shape(species, rows, width),
+        in_specs=[pl.BlockSpec(memory_space=pltpu.HBM)],
+        out_specs=VMEM,
+        scratch_shapes=[pltpu.SemaphoreType.DMA],
+        compiler_params=LIMIT,
+        name="plane",
+    )(pltpu.with_memory_space_constraint(cells, pltpu.HBM))
+
+
+def local_kernel(tiles_ref, cells_ref, dif_ref, vel_ref, out_ref, rows_ref):
     species, planes, rows, _ = cells_ref.shape
-    odd = parity_ref[0] == 1
+    last = planes - 1
     dif = [dif_ref[z] for z in range(planes)]
     vel = [vel_ref[z] for z in range(planes)]
 
     def one_species(s, carry):
-        near, far = near_ref[s, 0], far_ref[s, 0]
-        below = jnp.where(odd, near, far)
-        above = jnp.where(odd, far, near)
         cells = [cells_ref[s, z] for z in range(planes)]
-        column = [below, *cells, above]
         for z in range(planes):
-            center, under, over = column[z + 1], column[z], column[z + 2]
-            lateral = (
+            center = cells[z]
+            around = (
                 pltpu.roll(center, 1, 1)
                 + pltpu.roll(center, LANES - 1, 1)
                 + pltpu.roll(center, 1, 0)
                 + pltpu.roll(center, rows - 1, 0)
+                - 6.0 * center
             )
-            moved = center + dif[z] * (over + under + lateral - 6.0 * center) + vel[z] * (under - center)
+            if z > 0:
+                around = around + cells[z - 1]
+            if z < last:
+                around = around + cells[z + 1]
+            drift = cells[z - 1] - center if z > 0 else -center
             start = pl.multiple_of((s * planes + z) * rows, rows)
-            rows_ref[pl.ds(start, rows), :] = moved
+            rows_ref[pl.ds(start, rows), :] = center + dif[z] * around + vel[z] * drift
         return carry
 
     lax.fori_loop(0, species, one_species, 0, unroll=4)
@@ -58,6 +78,18 @@
         def _():
             y, z = lax.rem(tile, rows), lax.div(tile, rows)
             out_ref[y, pl.ds(data + z, 1), :] = jnp.ones((1, LANES), F32)
+
+
+def halo_kernel(pieces_ref, below_ref, above_ref, dif_ref, vel_ref, out_ref):
+    planes, rows, _ = dif_ref.shape
+    species = below_ref.shape[0] // rows
+    for y in range(rows):
+        at = pl.ds(y, species, stride=rows)
+        low = dif_ref[0, y : y + 1, :] + vel_ref[0, y : y + 1, :]
+        high = dif_ref[planes - 1, y : y + 1, :]
+        first, last = pl.ds(0, species, stride=planes), pl.ds(planes - 1, species, stride=planes)
+        out_ref[y, first, :] = pieces_ref[y, first, :] + low * below_ref[at, :]
+        out_ref[y, last, :] = pieces_ref[y, last, :] + high * above_ref[at, :]
 
 
 def in_parts(x, count):
@@ -85,13 +117,12 @@
     return concent
 
 
-def react_kernel(row_ref, in_ref, mix_ref, pick_ref, partner_ref, produced_ref, rates_ref, out_ref, list_ref):
+def react_kernel(in_ref, mix_ref, pick_ref, partner_ref, produced_ref, rates_ref, out_ref, list_ref):
     fields, data, _ = out_ref.shape
     planes = mix_ref.shape[0]
     species = data // planes
-    row = row_ref[0]
     even = lax.broadcasted_iota(jnp.int32, (8, LANES), 0) % planes == 0
-    mixing = jnp.where(even, mix_ref[0, pl.ds(row, 1), :], mix_ref[1, pl.ds(row, 1), :])
+    mixing = jnp.where(even, mix_ref[0:1, :], mix_ref[1:2, :])
 
     def one_block(block, carry):
         at = pl.ds(pl.multiple_of(block * 8, 8), 8)
@@ -131,11 +162,10 @@
                 out_ref[f, pl.ds(z, species, stride=planes), :] = concent[:, j * LANES : (j + 1) * LANES]
 
 
-def home_kernel(in_ref, out_ref, rows_ref):
+def home_kernel(in_ref, out_ref):
     pieces, data, _ = in_ref.shape
     for y in range(pieces):
-        rows_ref[pl.ds(y, data, stride=pieces), :] = in_ref[y]
-    out_ref[...] = rows_ref[...].reshape(out_ref.shape)
+        out_ref[pl.ds(y, data, stride=pieces), :] = in_ref[y]
 
 
 def one_hot_rows(indices, count):
@@ -165,42 +195,53 @@
     cells = scalars[0]
     species, planes, rows, width = cells.shape
     data = species * planes
-    parity = block % 2
-    near_pairs = [(i, i ^ 1) for i in range(blocks)]
-    far_pairs = [(i, (i + 1 if i % 2 else i - 1) % blocks) for i in range(blocks)]
-    far = lax.ppermute(lax.dynamic_slice_in_dim(cells, parity, 1, 1), "space", far_pairs)
-    near = lax.ppermute(lax.dynamic_slice_in_dim(cells, 1 - parity, 1, 1), "space", near_pairs)
+    up = [(i, (i + 1) % blocks) for i in range(blocks)]
+    down = [((i + 1) % blocks, i) for i in range(blocks)]
+    below = lax.ppermute(plane_of(cells, planes - 1), "space", up).reshape(species * rows, width)
+    above = lax.ppermute(plane_of(cells, 0), "space", down).reshape(species * rows, width)
     tables = reaction_tables(stoich, rates, species)
+    mixing_row = lax.dynamic_index_in_dim(mixing, lax.axis_index("field"), 1, False)
     pieces = pl.pallas_call(
-        transport_kernel,
+        local_kernel,
         out_shape=shape(rows, data + 8, width),
-        in_specs=[SMEM, SMEM] + [VMEM] * 5,
+        in_specs=[SMEM] + [VMEM] * 3,
         out_specs=VMEM,
         scratch_shapes=[pltpu.VMEM((data * rows, width), F32)],
         compiler_params=LIMIT,
-        name="transport",
-    )(parity.reshape(1), burn_tile[0, block], cells, near, far, diffusivity, velocity)
+        name="local",
+    )(burn_tile[0, block], cells, diffusivity, velocity)
+    pieces = pl.pallas_call(
+        halo_kernel,
+        out_shape=shape(rows, data + 8, width),
+        in_specs=[VMEM] * 5,
+        out_specs=VMEM,
+        input_output_aliases={0: 0},
+        compiler_params=LIMIT,
+        name="halo",
+    )(pieces, below, above, diffusivity, velocity)
+    pieces, tables, mixing_row = lax.optimization_barrier((pieces, tables, mixing_row))
     pieces = lax.all_to_all(pieces, "field", 0, 0, tiled=True)
     pieces = pl.pallas_call(
         react_kernel,
         out_shape=shape(fields, data, width),
-        in_specs=[SMEM] + [VMEM] * 6,
+        in_specs=[VMEM] * 6,
         out_specs=VMEM,
         scratch_shapes=[pltpu.SMEM((fields * planes + 1,), jnp.int32)],
         compiler_params=LIMIT,
         name="react",
-    )(lax.axis_index("field").reshape(1), pieces, mixing, *tables)
+    )(pieces, mixing_row, *tables)
     pieces = lax.all_to_all(pieces, "field", 0, 0, tiled=True)
+    steps = 4
     updated = pl.pallas_call(
         home_kernel,
-        out_shape=shape(species, planes, rows, width),
-        in_specs=[VMEM],
-        out_specs=VMEM,
-        scratch_shapes=[pltpu.VMEM((data * rows, width), F32)],
+        grid=(steps,),
+        out_shape=shape(data * rows, width),
+        in_specs=[pl.BlockSpec((rows, data // steps, width), lambda i: (0, i, 0))],
+        out_specs=pl.BlockSpec((data * rows // steps, width), lambda i: (i, 0)),
         compiler_params=LIMIT,
         name="home",
     )(pieces)
-    return updated[None]
+    return updated.reshape(1, species, planes, rows, width)
 
 
 def solution(mesh):

time: 65.1 us -> 61.8 us (0.949)
  blocking collectives: 15 us -> 34.6 us
  waiting for transfers between devices: 16 us -> 1.7 us
  starting transfers between devices: 23.8 us -> 15 us
  Pallas kernels: 6.69 us -> 8.58 us
  local copies, waits for them, and re-layouts: 2.72 us -> 1.03 us
    all_to_all x1 -> x2, blocking collectives: 15 us -> 34.6 us  [per_device(): pieces = lax.all_to_all(pieces, 'field', 0, 0, tiled=True)]
    all_to_all x1 -> x0, waiting for transfers between devices: 11.3 us -> none  [per_device(): pieces = lax.all_to_all(pieces, 'field', 0, 0, tiled=True)]
    all_to_all x1 -> x0, starting transfers between devices: 8.18 us -> none  [per_device(): pieces = lax.all_to_all(pieces, 'field', 0, 0, tiled=True)]
    ppermute x2, waiting for transfers between devices: 4.73 us -> 1.7 us  [the longest x1 1.7 us: per_device(): lax.ppermute(plane_of(cells, 0), 'space', down)]
    pallas_call x2 -> x5, Pallas kernels: 3.75 us -> 5.62 us  [the longest x2 1.93 us: plane_of(): pl.pallas_call(functools.partial(plane_kernel, plane), out_shape=shape(sp...]
    unnamed x14 -> x12, local copies, waits for them, and re-layouts: 1.3 us -> 0.04 us
    dynamic_slice x1, local copies, waits for them, and re-layouts: 1.13 us -> 0.01 us  [per_device(): lax.dynamic_index_in_dim(mixing, lax.axis_index('field'), 1, False)]
    squeeze x1, local copies, waits for them, and re-layouts: 0.01 us -> 0.7 us  [per_device(): burn_tile[0, block]]
  transfers between devices with their start and end apart: 3 -> 2, of which waited for: 2 -> 1; matrix products, arithmetic and copies ran while one was open for 1% -> 2% of each run, Pallas kernels for 0% -> 5%
where the time goes in v1:
time: 61.8 us; the launch traced here: 61.5 us
  blocking collectives  34.6 us (56%)
  starting transfers between devices  15 us (24%)
  Pallas kernels  8.58 us (14%)
  waiting for transfers between devices  1.7 us (3%)
  local copies, waits for them, and re-layouts  1.03 us (2%)
    all_to_all x2, blocking collectives, per_device(): pieces = lax.all_to_all(pieces, 'field', 0, 0, tiled=True)  34.6 us
    ppermute x1, starting transfers between devices, per_device(): lax.ppermute(plane_of(cells, 0), 'space', down)  10.6 us
    ppermute x1, starting transfers between devices, per_device(): lax.ppermute(plane_of(cells, planes - 1), 'space', up)  4.36 us
    pallas_call x1, Pallas kernels, per_device(): pl.pallas_call(react_kernel, out_shape=shape(fields, data, width), in_spe...  2.96 us
    pallas_call x2, Pallas kernels, plane_of(): pl.pallas_call(functools.partial(plane_kernel, plane), out_shape=shape(sp...  1.93 us
    pallas_call x1, Pallas kernels, per_device(): pl.pallas_call(local_kernel, out_shape=shape(rows, data + 8, width), in_s...  1.84 us
    ppermute x1, waiting for transfers between devices, per_device(): lax.ppermute(plane_of(cells, 0), 'space', down)  1.7 us
    pallas_call x1, Pallas kernels, per_device(): pl.pallas_call(home_kernel, grid=(steps,), out_shape=shape(data * rows, w...  1.49 us
  transfers between devices with their start and end apart: 2, of which 1 were waited for; matrix products, arithmetic and copies ran while one was open for 2% of the time, Pallas kernels for 5%

profile of v1, /device:TPU:1, one launch (start us, length us, event | category | flops | bytes accessed | tf_op | source)
XLA Modules:
  0.0 61.5 jit_solution(17518108351081117013)
XLA Ops:
  0.0 1.0 %plane.2 = f32[32,16,128]{2,1,0:T(8,128)S(1)} custom-call(f32[32,2,16,128]{3,2,1,0:T(8,128)} %bitcast.17), custom_call_target="tpu_custom_call" | custom-call | tf_op jit(solution)/shard_map/plane/pallas_call | solution.py:32
  1.0 4.4 %collective-permute-start = (f32[32,16,128]{2,1,0:T(8,128)S(1)}, f32[32,16,128]{2,1,0:T(8,128)S(1)}, u32[]{:S(2)}, u32[]{:S(2)}) collective-permute-start(f32[32,16,128]{2,1,0:T(8,128)S(1)} %plane.2), channel_id=1, source_target_pairs={{0,1},{1,2},{2,3},{3,4},{4,5},{5,6},{6,7},{7,8},{8,9},{9,10},{10,1... | collective-permute-start | bytes 786440 | tf_op jit(solution)/shard_map/ppermute | solution.py:200
  5.3 0.0 copy-start.4
  5.4 0.0 copy-start.5
  5.4 1.0 %plane.3 = f32[32,16,128]{2,1,0:T(8,128)S(1)} custom-call(f32[32,2,16,128]{3,2,1,0:T(8,128)} %bitcast.18), custom_call_target="tpu_custom_call" | custom-call | tf_op jit(solution)/shard_map/plane/pallas_call | solution.py:32
  6.3 0.0 copy-start.1
  6.4 10.6 %collective-permute-start.1 = (f32[32,16,128]{2,1,0:T(8,128)S(1)}, f32[32,16,128]{2,1,0:T(8,128)S(1)}, u32[]{:S(2)}, u32[]{:S(2)}) collective-permute-start(f32[32,16,128]{2,1,0:T(8,128)S(1)} %plane.3), channel_id=1, source_target_pairs={{1,0},{2,1},{3,2},{4,3},{5,4},{6,5},{7,6},{8,7},{9,8},{10,9},{11,1... | collective-permute-start | bytes 786440 | tf_op jit(solution)/shard_map/ppermute | solution.py:201
  17.1 0.1 copy.12
  17.2 0.1 pad_maximum_fusion.pick_ref
  17.3 0.1 fusion
  17.5 0.1 copy.13
  17.6 0.0 copy-start.2
  17.6 0.0 copy-start.3
  17.6 0.1 pad_maximum_fusion.1.partner_ref
  17.7 0.7 %dynamic-slice_bitcast_fusion.tiles_ref = s32[32]{0:T(128)S(1)} fusion(s32[1,32,32]{2,1,0:T(8,128)} %param.14, s32[]{:T(128)S(6)} %select_n.7), kind=kLoop, calls=%fused_computation.16 | loop fusion | bytes 260 | tf_op jit(solution)/shard_map/squeeze | solution.py:212
  18.4 1.8 %local.1.pieces_ref = f32[16,72,128]{2,1,0:T(8,128)S(1)} custom-call(s32[32]{0:T(128)S(1)} %dynamic-slice_bitcast_fusion.tiles_ref, f32[32,2,16,128]{3,2,1,0:T(8,128)S(1)} %bitcast.19, f32[2,16,128]{2,1,0:T(8,128)S(1)} %copy-done.2, f32[2,16,128]{2,1,0:T(8,128)S(1)} %copy-done.3), custom_call_target="tpu_custom_call" | custom-call | tf_op jit(solution)/shard_map/local/pallas_call | solution.py:204
  20.3 0.0 collective-permute-done
  20.3 1.7 %collective-permute-done.1 = f32[32,16,128]{2,1,0:T(8,128)S(1)} collective-permute-done((f32[32,16,128]{2,1,0:T(8,128)S(1)}, f32[32,16,128]{2,1,0:T(8,128)S(1)}, u32[]{:S(2)}, u32[]{:S(2)}) %collective-permute-start.1) | collective-permute-done | bytes 262176 | tf_op jit(solution)/shard_map/ppermute | solution.py:201
  22.0 0.4 halo.1
  22.3 0.1 broadcast_in_dim.2.rates_ref
  22.4 20.7 %all_to_all.10.in_ref = f32[16,72,128]{2,1,0:T(8,128)S(1)} all-to-all(f32[16,72,128]{2,1,0:T(8,128)S(1)} %halo.1), channel_id=1, replica_groups=mesh['field'=16,'space'=32] {'field'}, dimensions={0} | all-to-all | bytes 1179648 | tf_op jit(solution)/shard_map/all_to_all | solution.py:223
  43.1 3.0 %react.1 = f32[16,64,128]{2,1,0:T(8,128)S(1)} custom-call(f32[16,72,128]{2,1,0:T(8,128)S(1)} %all_to_all.10.in_ref, f32[2,128]{1,0:T(2,128)S(1)} %bitcast.22, bf16[512,64]{1,0:T(8,128)(2,1)S(1)} %pad_maximum_fusion.pick_ref, bf16[32,96]{1,0:T(8,128)(2,1)S(1)} %pad_maximum_fusion.1.partner_ref, bf16[32,256]{1,0:T(8,128)(2,1)S(1)} %add_convert_fusion.1.produced_ref, ...), custom_call_target="tpu_custom_call" | custom-call | tf_op jit(solution)/shard_map/react/pallas_call | solution.py:224
  46.1 13.9 %all_to_all.11.in_ref = f32[16,64,128]{2,1,0:T(8,128)S(1)} all-to-all(f32[16,64,128]{2,1,0:T(8,128)S(1)} %react.1), channel_id=1, replica_groups=mesh['field'=16,'space'=32] {'field'}, dimensions={0} | all-to-all | bytes 1048576 | tf_op jit(solution)/shard_map/all_to_all | solution.py:233
  60.0 1.5 %home.1 = f32[1024,128]{1,0:T(8,128)} custom-call(f32[16,64,128]{2,1,0:T(8,128)S(1)} %all_to_all.11.in_ref), custom_call_target="tpu_custom_call" | custom-call | tf_op jit(solution)/shard_map/home/pallas_call | solution.py:235
  (13 shorter events, 0.1 us)
Async XLA Ops:
  0.0 17.7 %copy-start = (f32[2,16,128]{2,1,0:T(8,128)S(1)}, f32[2,16,128]{2,1,0:T(8,128)}, u32[]{:S(2)}) copy-start(f32[2,16,128]{2,1,0:T(8,128)} %param.11) | copy-start | bytes 49156
  1.0 19.3 %collective-permute-start = (f32[32,16,128]{2,1,0:T(8,128)S(1)}, f32[32,16,128]{2,1,0:T(8,128)S(1)}, u32[]{:S(2)}, u32[]{:S(2)}) collective-permute-start(f32[32,16,128]{2,1,0:T(8,128)S(1)} %plane.2), channel_id=1, source_target_pairs={{0,1},{1,2},{2,3},{3,4},{4,5},{5,6},{6,7},{7,8},{8,9},{9,10},{10,1... | collective-permute-start | bytes 786440 | tf_op jit(solution)/shard_map/ppermute | solution.py:200
  5.3 11.7 %copy-start.4 = (s32[4,256]{1,0:T(4,128)S(1)}, s32[4,256]{1,0:T(4,128)}, u32[]{:S(2)}) copy-start(s32[4,256]{1,0:T(4,128)} %param.13) | copy-start | bytes 12292
  5.4 12.0 %copy-start.5 = (f32[256]{0:T(256)S(1)}, f32[256]{0:T(256)}, u32[]{:S(2)}) copy-start(f32[256]{0:T(256)} %param.12) | copy-start | bytes 3076
  6.3 12.0 %copy-start.1 = (f32[1,32,2,16,128]{4,3,2,1,0:T(8,128)S(1)}, f32[1,32,2,16,128]{4,3,2,1,0:T(8,128)}, u32[]{:S(2)}) copy-start(f32[1,32,2,16,128]{4,3,2,1,0:T(8,128)} %param.8) | copy-start | bytes 1572868
  6.4 15.6 %collective-permute-start.1 = (f32[32,16,128]{2,1,0:T(8,128)S(1)}, f32[32,16,128]{2,1,0:T(8,128)S(1)}, u32[]{:S(2)}, u32[]{:S(2)}) collective-permute-start(f32[32,16,128]{2,1,0:T(8,128)S(1)} %plane.3), channel_id=1, source_target_pairs={{1,0},{2,1},{3,2},{4,3},{5,4},{6,5},{7,6},{8,7},{9,8},{10,9},{11,1... | collective-permute-start | bytes 786440 | tf_op jit(solution)/shard_map/ppermute | solution.py:201
  17.6 0.8 %copy-start.2 = (f32[2,16,128]{2,1,0:T(8,128)S(1)}, f32[2,16,128]{2,1,0:T(8,128)}, u32[]{:S(2)}) copy-start(f32[2,16,128]{2,1,0:T(8,128)} %dif_ref.3) | copy-start | bytes 49156
  17.6 0.8 %copy-start.3 = (f32[2,16,128]{2,1,0:T(8,128)S(1)}, f32[2,16,128]{2,1,0:T(8,128)}, u32[]{:S(2)}) copy-start(f32[2,16,128]{2,1,0:T(8,128)} %vel_ref.3) | copy-start | bytes 49156

commit v2 on v1

--- a/solution.py
+++ b/solution.py
@@ -9,7 +9,7 @@
 
 NSUB = 4
 LANES = 128
-GROUP = 8
+GROUP = 12
 F32 = jnp.float32
 BF16 = jnp.bfloat16
 VMEM = pl.BlockSpec(memory_space=pltpu.VMEM)
@@ -19,25 +19,6 @@
 
 def shape(*dims):
     return jax.ShapeDtypeStruct(dims, F32)
-
-
-def plane_kernel(plane, cells_ref, out_ref, sem):
-    copy = pltpu.make_async_copy(cells_ref.at[:, plane], out_ref, sem)
-    copy.start()
-    copy.wait()
-
-
-def plane_of(cells, plane):
-    species, _, rows, width = cells.shape
-    return pl.pallas_call(
-        functools.partial(plane_kernel, plane),
-        out_shape=shape(species, rows, width),
-        in_specs=[pl.BlockSpec(memory_space=pltpu.HBM)],
-        out_specs=VMEM,
-        scratch_shapes=[pltpu.SemaphoreType.DMA],
-        compiler_params=LIMIT,
-        name="plane",
-    )(pltpu.with_memory_space_constraint(cells, pltpu.HBM))
 
 
 def local_kernel(tiles_ref, cells_ref, dif_ref, vel_ref, out_ref, rows_ref):
@@ -92,32 +73,36 @@
         out_ref[y, last, :] = pieces_ref[y, last, :] + high * above_ref[at, :]
 
 
-def in_parts(x, count):
-    parts = []
-    for part in range(count):
-        parts.append(x.astype(BF16))
-        if part + 1 < count:
-            x = x - parts[-1].astype(F32)
-    return parts
-
-
-def chemistry(concent, pick, partner, produced, rates):
+def in_parts(x):
+    high = x.astype(BF16)
+    return high, (x - high.astype(F32)).astype(BF16)
+
+
+def factors(x):
+    high, low = in_parts(x)
+    return jnp.concatenate([high, low, high], 0)
+
+
+def weights(w):
+    high = lax.reduce_precision(w, 8, 7)
+    return jnp.concatenate([high, high, w - high], 1).astype(BF16)
+
+
+def dot(a, b):
+    return jnp.dot(a, b, preferred_element_type=F32)
+
+
+def chemistry(concent, pairs, partner, squares, produced):
     substep = 1.0 / NSUB
-    reactions = rates.shape[0]
     for repeat in range(NSUB):
-        high, low = in_parts(concent, 2)
-        picked = jnp.dot(pick, jnp.concatenate([high, low], 0), preferred_element_type=F32)
-        losing = jnp.dot(partner, jnp.concatenate([high, high, low], 0), preferred_element_type=F32)
-        progress = picked[:reactions] * picked[reactions:] * rates
-        high, low = in_parts(progress, 2)
-        making = jnp.dot(produced, high, preferred_element_type=F32) + jnp.dot(
-            produced, low, preferred_element_type=F32
-        )
-        concent = (concent + substep * making) / (1.0 + substep * losing)
+        current = factors(concent)
+        pair = dot(pairs, current)
+        making = dot(produced, jnp.concatenate(in_parts(pair * pair), 0)) - dot(squares, factors(concent * concent))
+        concent = (concent + substep * making) / (1.0 + substep * dot(partner, current))
     return concent
 
 
-def react_kernel(in_ref, mix_ref, pick_ref, partner_ref, produced_ref, rates_ref, out_ref, list_ref):
+def react_kernel(in_ref, mix_ref, pairs_ref, partner_ref, squares_ref, produced_ref, out_ref, list_ref):
     fields, data, _ = out_ref.shape
     planes = mix_ref.shape[0]
     species = data // planes
@@ -145,8 +130,7 @@
         for f in range(fields):
             list_ref[count] = f * planes + z
             count = count + ((code[z] >> f) & 1)
-    rates = jnp.concatenate([rates_ref[...]] * GROUP, 1)
-    pick, partner, produced = pick_ref[...], partner_ref[...], produced_ref[...]
+    tables = [ref[...] for ref in (pairs_ref, partner_ref, squares_ref, produced_ref)]
 
     @pl.loop(0, pl.cdiv(count, GROUP))
     def _(group):
@@ -154,7 +138,7 @@
         entries = [list_ref[jnp.minimum(first + j, count - 1)] for j in range(GROUP)]
         places = [(lax.div(e, planes), lax.rem(e, planes)) for e in entries]
         concent = jnp.concatenate([out_ref[f, pl.ds(z, species, stride=planes), :] for f, z in places], 1)
-        concent = chemistry(concent, pick, partner, produced, rates)
+        concent = chemistry(concent, *tables)
         for j, (f, z) in enumerate(places):
 
             @pl.when(first + j < count)
@@ -162,10 +146,21 @@
                 out_ref[f, pl.ds(z, species, stride=planes), :] = concent[:, j * LANES : (j + 1) * LANES]
 
 
-def home_kernel(in_ref, out_ref):
+def home_kernel(in_ref, out_ref, rows_ref, sems):
     pieces, data, _ = in_ref.shape
-    for y in range(pieces):
-        out_ref[pl.ds(y, data, stride=pieces), :] = in_ref[y]
+    steps = sems.shape[0]
+    part = data // steps
+    copies = []
+    for step in range(steps):
+        size = part * pieces
+        for y in range(pieces):
+            at = pl.ds(step * size + y, part, stride=pieces)
+            rows_ref[at, :] = in_ref[y, step * part : (step + 1) * part, :]
+        at = pl.ds(step * size, size)
+        copies.append(pltpu.make_async_copy(rows_ref.at[at], out_ref.at[at], sems.at[step]))
+        copies[-1].start()
+    for copy in copies:
+        copy.wait()
 
 
 def one_hot_rows(indices, count):
@@ -173,18 +168,19 @@
 
 
 def reaction_tables(stoich, rates, species):
+    highest = lax.Precision.HIGHEST
+    rate = rates[:, None]
     one, two = one_hot_rows(stoich[0], species), one_hot_rows(stoich[1], species)
     produced = one_hot_rows(stoich[2], species) + one_hot_rows(stoich[3], species)
-    pick = jnp.concatenate([one, two], 0).astype(BF16)
-    partner = jnp.dot((one * rates[:, None]).T, two, precision=lax.Precision.HIGHEST)
-    partner = partner + partner.T
-    high = lax.reduce_precision(partner, 8, 7)
-    low = partner - high
+    both = one + two
+    partner = jnp.dot((one * rate).T, two, precision=highest)
+    squares = jnp.dot(produced.T, (0.5 * rate) * both, precision=highest)
+    produced = (0.5 * produced).T.astype(BF16)
     return (
-        jnp.concatenate([pick, pick], 1),
-        jnp.concatenate([high, low, high], 1).astype(BF16),
-        produced.T.astype(BF16),
-        jnp.broadcast_to(rates[:, None], (rates.shape[0], LANES)),
+        weights(jnp.sqrt(rate) * both),
+        weights(partner + partner.T),
+        weights(squares),
+        jnp.concatenate([produced, produced], 1),
     )
 
 
@@ -197,8 +193,8 @@
     data = species * planes
     up = [(i, (i + 1) % blocks) for i in range(blocks)]
     down = [((i + 1) % blocks, i) for i in range(blocks)]
-    below = lax.ppermute(plane_of(cells, planes - 1), "space", up).reshape(species * rows, width)
-    above = lax.ppermute(plane_of(cells, 0), "space", down).reshape(species * rows, width)
+    below = lax.ppermute(cells[:, planes - 1], "space", up).reshape(species * rows, width)
+    above = lax.ppermute(cells[:, 0], "space", down).reshape(species * rows, width)
     tables = reaction_tables(stoich, rates, species)
     mixing_row = lax.dynamic_index_in_dim(mixing, lax.axis_index("field"), 1, False)
     pieces = pl.pallas_call(
@@ -231,13 +227,12 @@
         name="react",
     )(pieces, mixing_row, *tables)
     pieces = lax.all_to_all(pieces, "field", 0, 0, tiled=True)
-    steps = 4
     updated = pl.pallas_call(
         home_kernel,
-        grid=(steps,),
         out_shape=shape(data * rows, width),
-        in_specs=[pl.BlockSpec((rows, data // steps, width), lambda i: (0, i, 0))],
-        out_specs=pl.BlockSpec((data * rows // steps, width), lambda i: (i, 0)),
+        in_specs=[VMEM],
+        out_specs=pl.BlockSpec(memory_space=pltpu.HBM),
+        scratch_shapes=[pltpu.VMEM((data * rows, width), F32), pltpu.SemaphoreType.DMA((4,))],
         compiler_params=LIMIT,
         name="home",
     )(pieces)

time: 61.8 us -> 60.5 us (0.979)
  Pallas kernels: 8.58 us -> 6.24 us
  local copies, waits for them, and re-layouts: 1.03 us -> 1.93 us
  waiting for transfers between devices: 1.7 us -> 0.82 us
  matrix products: 0.14 us -> 0.95 us
    pallas_call x3 -> x1, Pallas kernels: 3.42 us -> 0.86 us  [per_device(): pl.pallas_call(home_kernel, out_shape=shape(data * rows, width), in_specs...]
    squeeze x0 -> x1, local copies, waits for them, and re-layouts: none -> 1.11 us  [per_device(): cells[:, 0]]
    ppermute x2, waiting for transfers between devices: 1.7 us -> 0.82 us  [the longest x1 0.82 us: per_device(): lax.ppermute(cells[:, 0], 'space', down).reshape(species * rows, width)]
    dot_general x1 -> x2, matrix products: 0.14 us -> 0.95 us  [the longest x1 0.57 us: reaction_tables(): squares = jnp.dot(produced.T, 0.5 * rate * both, precision=highest)]
  transfers between devices with their start and end apart: 2 -> 2, of which waited for: 1 -> 1; matrix products, arithmetic and copies ran while one was open for 2% -> 4% of each run, Pallas kernels for 5% -> 3%
where the time goes in v2:
time: 60.5 us; the launch traced here: 60.2 us
  blocking collectives  34.6 us (57%)
  starting transfers between devices  15 us (25%)
  Pallas kernels  6.24 us (10%)
  local copies, waits for them, and re-layouts  1.93 us (3%)
  matrix products  0.95 us (2%)
  waiting for transfers between devices  0.82 us (1%)
    all_to_all x2, blocking collectives, per_device(): pieces = lax.all_to_all(pieces, 'field', 0, 0, tiled=True)  34.6 us
    ppermute x1, starting transfers between devices, per_device(): lax.ppermute(cells[:, 0], 'space', down).reshape(species * rows, width)  10.5 us
    ppermute x1, starting transfers between devices, per_device(): lax.ppermute(cells[:, planes - 1], 'space', up)  4.5 us
    pallas_call x1, Pallas kernels, per_device(): pl.pallas_call(react_kernel, out_shape=shape(fields, data, width), in_spe...  3.18 us
    pallas_call x1, Pallas kernels, per_device(): pl.pallas_call(local_kernel, out_shape=shape(rows, data + 8, width), in_s...  1.84 us
  transfers between devices with their start and end apart: 2, of which 1 were waited for; matrix products, arithmetic and copies ran while one was open for 4% of the time, Pallas kernels for 3%

profile of v2, /device:TPU:1, one launch (start us, length us, event | category | flops | bytes accessed | tf_op | source)
XLA Modules:
  0.0 60.2 jit_solution(9256685607694085349)
XLA Ops:
  0.0 1.1 %slice_bitcast_fusion = (f32[32,16,128]{2,1,0:T(8,128)S(1)}, f32[32,16,128]{2,1,0:T(8,128)S(1)}) fusion(f32[32,2,16,128]{3,2,1,0:T(8,128)} %bitcast.21), kind=kLoop, calls=%fused_computation | loop fusion | bytes 1048576 | tf_op jit(solution)/shard_map/squeeze | solution.py:197
  1.1 0.0 copy-start.1
  1.1 4.5 %collective-permute-start = (f32[32,16,128]{2,1,0:T(8,128)S(1)}, f32[32,16,128]{2,1,0:T(8,128)S(1)}, u32[]{:S(2)}, u32[]{:S(2)}) collective-permute-start(f32[32,16,128]{2,1,0:T(8,128)S(1)} %get-tuple-element.18), channel_id=1, source_target_pairs={{0,1},{1,2},{2,3},{3,4},{4,5},{5,6},{6,7},{7,8},{8,9},{9,10},{10,1... | collective-permute-start | bytes 786440 | tf_op jit(solution)/shard_map/ppermute | solution.py:196
  5.6 10.5 %collective-permute-start.1 = (f32[32,16,128]{2,1,0:T(8,128)S(1)}, f32[32,16,128]{2,1,0:T(8,128)S(1)}, u32[]{:S(2)}, u32[]{:S(2)}) collective-permute-start(f32[32,16,128]{2,1,0:T(8,128)S(1)} %get-tuple-element.17), channel_id=1, source_target_pairs={{1,0},{2,1},{3,2},{4,3},{5,4},{6,5},{7,6},{8,7},{9,8},{10,9},{11,1... | collective-permute-start | bytes 786440 | tf_op jit(solution)/shard_map/ppermute | solution.py:197
  16.2 0.0 copy-done.5
  16.2 0.4 fusion.6
  16.6 0.2 reduce-precision_convert_fusion
  16.8 0.1 copy.9
  16.9 0.6 reduce-precision_convert_fusion.1
  17.5 0.0 copy-done
  17.5 0.0 copy-start.2
  17.5 0.0 copy-start.3
  17.5 0.1 pad_maximum_fusion.2
  17.6 0.7 %dynamic-slice_bitcast_fusion.tiles_ref = s32[32]{0:T(128)S(1)} fusion(s32[1,32,32]{2,1,0:T(8,128)} %param.14, s32[]{:T(128)S(6)} %select_n.7), kind=kLoop, calls=%fused_computation.42 | loop fusion | bytes 260 | tf_op jit(solution)/shard_map/squeeze | solution.py:208
  18.3 0.0 copy-done.1
  18.3 1.8 %local.1.pieces_ref = f32[16,72,128]{2,1,0:T(8,128)S(1)} custom-call(s32[32]{0:T(128)S(1)} %dynamic-slice_bitcast_fusion.tiles_ref, f32[32,2,16,128]{3,2,1,0:T(8,128)S(1)} %bitcast.22, f32[2,16,128]{2,1,0:T(8,128)S(1)} %copy-done.2, f32[2,16,128]{2,1,0:T(8,128)S(1)} %copy-done.3), custom_call_target="tpu_custom_call" | custom-call | tf_op jit(solution)/shard_map/local/pallas_call | solution.py:200
  20.2 0.1 pad_maximum_fusion.pairs_ref
  20.3 0.0 collective-permute-done
  20.3 0.8 %collective-permute-done.1 = f32[32,16,128]{2,1,0:T(8,128)S(1)} collective-permute-done((f32[32,16,128]{2,1,0:T(8,128)S(1)}, f32[32,16,128]{2,1,0:T(8,128)S(1)}, u32[]{:S(2)}, u32[]{:S(2)}) %collective-permute-start.1) | collective-permute-done | bytes 262176 | tf_op jit(solution)/shard_map/ppermute | solution.py:197
  21.1 0.4 halo.1
  21.5 20.7 %all_to_all.10.in_ref = f32[16,72,128]{2,1,0:T(8,128)S(1)} all-to-all(f32[16,72,128]{2,1,0:T(8,128)S(1)} %halo.1), channel_id=1, replica_groups=mesh['field'=16,'space'=32] {'field'}, dimensions={0} | all-to-all | bytes 1179648 | tf_op jit(solution)/shard_map/all_to_all | solution.py:219
  42.2 3.2 %react.1 = f32[16,64,128]{2,1,0:T(8,128)S(1)} custom-call(f32[16,72,128]{2,1,0:T(8,128)S(1)} %all_to_all.10.in_ref, f32[2,128]{1,0:T(2,128)S(1)} %bitcast.25, bf16[256,96]{1,0:T(8,128)(2,1)S(1)} %pad_maximum_fusion.pairs_ref, bf16[32,96]{1,0:T(8,128)(2,1)S(1)} %get-tuple-element.14.partner_ref, bf16[32,96]{1,0:T(8,128)(2,1)S(1)} %get-tuple-element.15.squares_ref, ...), custom_call_target="tpu_custom_call" | custom-call | tf_op jit(solution)/shard_map/react/pallas_call | solution.py:220
  45.4 13.9 %all_to_all.11.in_ref = f32[16,64,128]{2,1,0:T(8,128)S(1)} all-to-all(f32[16,64,128]{2,1,0:T(8,128)S(1)} %react.1), channel_id=1, replica_groups=mesh['field'=16,'space'=32] {'field'}, dimensions={0} | all-to-all | bytes 1048576 | tf_op jit(solution)/shard_map/all_to_all | solution.py:229
  59.3 0.9 %home.1 = f32[1024,128]{1,0:T(8,128)} custom-call(f32[16,64,128]{2,1,0:T(8,128)S(1)} %all_to_all.11.in_ref), custom_call_target="tpu_custom_call" | custom-call | tf_op jit(solution)/shard_map/home/pallas_call | solution.py:230
  (12 shorter events, 0.1 us)
Async XLA Ops:
  0.0 17.5 %copy-start = (f32[2,16,128]{2,1,0:T(8,128)S(1)}, f32[2,16,128]{2,1,0:T(8,128)}, u32[]{:S(2)}) copy-start(f32[2,16,128]{2,1,0:T(8,128)} %param.11) | copy-start | bytes 49156
  0.0 16.2 %copy-start.4 = (s32[4,256]{1,0:T(4,128)S(1)}, s32[4,256]{1,0:T(4,128)}, u32[]{:S(2)}) copy-start(s32[4,256]{1,0:T(4,128)} %param.13) | copy-start | bytes 12292
  0.0 16.2 %copy-start.5 = (f32[256]{0:T(256)S(1)}, f32[256]{0:T(256)}, u32[]{:S(2)}) copy-start(f32[256]{0:T(256)} %param.12) | copy-start | bytes 3076
  1.1 17.2 %copy-start.1 = (f32[1,32,2,16,128]{4,3,2,1,0:T(8,128)S(1)}, f32[1,32,2,16,128]{4,3,2,1,0:T(8,128)}, u32[]{:S(2)}) copy-start(f32[1,32,2,16,128]{4,3,2,1,0:T(8,128)} %param.8) | copy-start | bytes 1572868
  1.1 19.2 %collective-permute-start = (f32[32,16,128]{2,1,0:T(8,128)S(1)}, f32[32,16,128]{2,1,0:T(8,128)S(1)}, u32[]{:S(2)}, u32[]{:S(2)}) collective-permute-start(f32[32,16,128]{2,1,0:T(8,128)S(1)} %get-tuple-element.18), channel_id=1, source_target_pairs={{0,1},{1,2},{2,3},{3,4},{4,5},{5,6},{6,7},{7,8},{8,9},{9,10},{10,1... | collective-permute-start | bytes 786440 | tf_op jit(solution)/shard_map/ppermute | solution.py:196
  5.6 15.5 %collective-permute-start.1 = (f32[32,16,128]{2,1,0:T(8,128)S(1)}, f32[32,16,128]{2,1,0:T(8,128)S(1)}, u32[]{:S(2)}, u32[]{:S(2)}) collective-permute-start(f32[32,16,128]{2,1,0:T(8,128)S(1)} %get-tuple-element.17), channel_id=1, source_target_pairs={{1,0},{2,1},{3,2},{4,3},{5,4},{6,5},{7,6},{8,7},{9,8},{10,9},{11,1... | collective-permute-start | bytes 786440 | tf_op jit(solution)/shard_map/ppermute | solution.py:197
  17.5 0.8 %copy-start.2 = (f32[2,16,128]{2,1,0:T(8,128)S(1)}, f32[2,16,128]{2,1,0:T(8,128)}, u32[]{:S(2)}) copy-start(f32[2,16,128]{2,1,0:T(8,128)} %dif_ref.3) | copy-start | bytes 49156
  17.5 0.8 %copy-start.3 = (f32[2,16,128]{2,1,0:T(8,128)S(1)}, f32[2,16,128]{2,1,0:T(8,128)}, u32[]{:S(2)}) copy-start(f32[2,16,128]{2,1,0:T(8,128)} %vel_ref.3) | copy-start | bytes 49156

commit v3 on v2

--- a/solution.py
+++ b/solution.py
@@ -61,16 +61,26 @@
             out_ref[y, pl.ds(data + z, 1), :] = jnp.ones((1, LANES), F32)
 
 
-def halo_kernel(pieces_ref, below_ref, above_ref, dif_ref, vel_ref, out_ref):
+def halo_kernel(core_ref, pieces_ref, first_ref, second_ref, dif_ref, vel_ref, out_ref):
     planes, rows, _ = dif_ref.shape
-    species = below_ref.shape[0] // rows
-    for y in range(rows):
-        at = pl.ds(y, species, stride=rows)
-        low = dif_ref[0, y : y + 1, :] + vel_ref[0, y : y + 1, :]
-        high = dif_ref[planes - 1, y : y + 1, :]
-        first, last = pl.ds(0, species, stride=planes), pl.ds(planes - 1, species, stride=planes)
-        out_ref[y, first, :] = pieces_ref[y, first, :] + low * below_ref[at, :]
-        out_ref[y, last, :] = pieces_ref[y, last, :] + high * above_ref[at, :]
+    species = first_ref.shape[0] // rows
+    low = dif_ref[0] + vel_ref[0]
+    high = dif_ref[planes - 1]
+
+    def add(below_ref, above_ref):
+        for y in range(rows):
+            at = pl.ds(y, species, stride=rows)
+            bottom, top = pl.ds(0, species, stride=planes), pl.ds(planes - 1, species, stride=planes)
+            out_ref[y, bottom, :] = pieces_ref[y, bottom, :] + low[y : y + 1] * below_ref[at, :]
+            out_ref[y, top, :] = pieces_ref[y, top, :] + high[y : y + 1] * above_ref[at, :]
+
+    @pl.when(core_ref[0] == 0)
+    def _():
+        add(first_ref, second_ref)
+
+    @pl.when(core_ref[0] == 1)
+    def _():
+        add(second_ref, first_ref)
 
 
 def in_parts(x):
@@ -191,12 +201,20 @@
     cells = scalars[0]
     species, planes, rows, width = cells.shape
     data = species * planes
-    up = [(i, (i + 1) % blocks) for i in range(blocks)]
-    down = [((i + 1) % blocks, i) for i in range(blocks)]
-    below = lax.ppermute(cells[:, planes - 1], "space", up).reshape(species * rows, width)
-    above = lax.ppermute(cells[:, 0], "space", down).reshape(species * rows, width)
+    field = lax.axis_index("field")
+    core = field % 2
+
+    def exchanged(ways):
+        pairs = [
+            (f * blocks + i, f * blocks + (i + ways[f % 2]) % blocks) for f in range(fields) for i in range(blocks)
+        ]
+        up = core if ways[1] == 1 else 1 - core
+        plane = lax.dynamic_index_in_dim(cells, up * (planes - 1), 1, False)
+        return lax.ppermute(plane, ("field", "space"), pairs).reshape(species * rows, width)
+
+    first, second = exchanged((1, -1)), exchanged((-1, 1))
     tables = reaction_tables(stoich, rates, species)
-    mixing_row = lax.dynamic_index_in_dim(mixing, lax.axis_index("field"), 1, False)
+    mixing_row = lax.dynamic_index_in_dim(mixing, field, 1, False)
     pieces = pl.pallas_call(
         local_kernel,
         out_shape=shape(rows, data + 8, width),
@@ -209,12 +227,12 @@
     pieces = pl.pallas_call(
         halo_kernel,
         out_shape=shape(rows, data + 8, width),
-        in_specs=[VMEM] * 5,
+        in_specs=[SMEM] + [VMEM] * 5,
         out_specs=VMEM,
-        input_output_aliases={0: 0},
+        input_output_aliases={1: 0},
         compiler_params=LIMIT,
         name="halo",
-    )(pieces, below, above, diffusivity, velocity)
+    )(core.reshape(1), pieces, first, second, diffusivity, velocity)
     pieces, tables, mixing_row = lax.optimization_barrier((pieces, tables, mixing_row))
     pieces = lax.all_to_all(pieces, "field", 0, 0, tiled=True)
     pieces = pl.pallas_call(

time: 60.5 us -> 61.4 us (1.015)
  waiting for transfers between devices: 0.82 us -> 3.1 us
  blocking collectives: 34.6 us -> 33.2 us
    ppermute x2, waiting for transfers between devices: 0.82 us -> 3.1 us  [exchanged(): lax.ppermute(plane, ('field', 'space'), pairs)]
    all_to_all x2, blocking collectives: 34.6 us -> 33.2 us  [per_device(): pieces = lax.all_to_all(pieces, 'field', 0, 0, tiled=True)]
where the time goes in v3:
time: 61.4 us; the launch traced here: 61.1 us
  blocking collectives  33.2 us (54%)
  starting transfers between devices  15 us (24%)
  Pallas kernels  6.3 us (10%)
  waiting for transfers between devices  3.1 us (5%)
  local copies, waits for them, and re-layouts  1.93 us (3%)
  matrix products  0.95 us (2%)
    all_to_all x2, blocking collectives, per_device(): pieces = lax.all_to_all(pieces, 'field', 0, 0, tiled=True)  33.2 us
    ppermute x2, starting transfers between devices, exchanged(): lax.ppermute(plane, ('field', 'space'), pairs)  15 us
    pallas_call x1, Pallas kernels, per_device(): pl.pallas_call(react_kernel, out_shape=shape(fields, data, width), in_spe...  3.18 us
    ppermute x2, waiting for transfers between devices, exchanged(): lax.ppermute(plane, ('field', 'space'), pairs)  3.1 us
    pallas_call x1, Pallas kernels, per_device(): pl.pallas_call(local_kernel, out_shape=shape(rows, data + 8, width), in_s...  1.89 us
  transfers between devices with their start and end apart: 2, of which 1 were waited for; matrix products, arithmetic and copies ran while one was open for 4% of the time, Pallas kernels for 3%

profile of v3, /device:TPU:1, one launch (start us, length us, event | category | flops | bytes accessed | tf_op | source)
XLA Modules:
  0.0 61.1 jit_solution(10930349226522963631)
XLA Ops:
  0.0 0.0 copy-start
  0.0 1.1 %dynamic-slice_bitcast_fusion = (f32[32,16,128]{2,1,0:T(8,128)S(1)}, f32[32,16,128]{2,1,0:T(8,128)S(1)}) fusion(f32[1,32,2,16,128]{4,3,2,1,0:T(8,128)} %param.8, s32[]{:T(128)S(6)} %select_n.24, s32[]{:T(128)S(6)} %select_n.23), kind=kLoop, calls=%fused_computation | loop fusion | bytes 1048584 | tf_op jit(solution)/shard_map/jit(dynamic_index_in_dim)/squeeze | solution.py:212
  1.1 0.0 copy-start.1
  1.1 13.1 %collective-permute-start = (f32[32,16,128]{2,1,0:T(8,128)S(1)}, f32[32,16,128]{2,1,0:T(8,128)S(1)}, u32[]{:S(2)}, u32[]{:S(2)}) collective-permute-start(f32[32,16,128]{2,1,0:T(8,128)S(1)} %get-tuple-element.18), channel_id=1, source_target_pairs={{0,1},{1,2},{2,3},{3,4},{4,5},{5,6},{6,7},{7,8},{8,9},{9,10},{10,1... | collective-permute-start | bytes 786440 | tf_op jit(solution)/shard_map/ppermute | solution.py:213
  14.2 1.9 %collective-permute-start.1 = (f32[32,16,128]{2,1,0:T(8,128)S(1)}, f32[32,16,128]{2,1,0:T(8,128)S(1)}, u32[]{:S(2)}, u32[]{:S(2)}) collective-permute-start(f32[32,16,128]{2,1,0:T(8,128)S(1)} %get-tuple-element.17), channel_id=1, source_target_pairs={{0,31},{1,0},{2,1},{3,2},{4,3},{5,4},{6,5},{7,6},{8,7},{9,8},{10,9... | collective-permute-start | bytes 786440 | tf_op jit(solution)/shard_map/ppermute | solution.py:213
  16.2 0.0 copy-done.5
  16.2 0.4 fusion.6
  16.6 0.1 copy.9
  16.7 0.6 reduce-precision_convert_fusion.1
  17.3 0.2 reduce-precision_convert_fusion
  17.5 0.0 copy-start.2
  17.5 0.0 copy-start.3
  17.5 0.1 pad_maximum_fusion.2
  17.6 0.7 %fusion.20.tiles_ref = s32[32]{0:T(128)S(1)} fusion(s32[1,32,32]{2,1,0:T(8,128)} %param.14, s32[]{:T(128)S(6)} %select_n.22), kind=kLoop, calls=%fused_computation.43 | loop fusion | bytes 260 | tf_op jit(solution)/shard_map/squeeze | solution.py:226
  18.3 0.0 copy-done.2
  18.3 1.9 %local.1.pieces_ref = f32[16,72,128]{2,1,0:T(8,128)S(1)} custom-call(s32[32]{0:T(128)S(1)} %fusion.20.tiles_ref, f32[32,2,16,128]{3,2,1,0:T(8,128)S(1)} %bitcast.22, f32[2,16,128]{2,1,0:T(8,128)S(1)} %copy-done.2, f32[2,16,128]{2,1,0:T(8,128)S(1)} %copy-done.3), custom_call_target="tpu_custom_call" | custom-call | tf_op jit(solution)/shard_map/local/pallas_call | solution.py:218
  20.2 0.1 pad_maximum_fusion.pairs_ref
  20.3 0.0 collective-permute-done
  20.4 3.1 %collective-permute-done.1 = f32[32,16,128]{2,1,0:T(8,128)S(1)} collective-permute-done((f32[32,16,128]{2,1,0:T(8,128)S(1)}, f32[32,16,128]{2,1,0:T(8,128)S(1)}, u32[]{:S(2)}, u32[]{:S(2)}) %collective-permute-start.1) | collective-permute-done | bytes 262176 | tf_op jit(solution)/shard_map/ppermute | solution.py:213
  23.5 0.4 halo.1
  23.8 19.3 %all_to_all.10.in_ref = f32[16,72,128]{2,1,0:T(8,128)S(1)} all-to-all(f32[16,72,128]{2,1,0:T(8,128)S(1)} %halo.1), channel_id=1, replica_groups=mesh['field'=16,'space'=32] {'field'}, dimensions={0} | all-to-all | bytes 1179648 | tf_op jit(solution)/shard_map/all_to_all | solution.py:237
  43.1 3.2 %react.1 = f32[16,64,128]{2,1,0:T(8,128)S(1)} custom-call(f32[16,72,128]{2,1,0:T(8,128)S(1)} %all_to_all.10.in_ref, f32[2,128]{1,0:T(2,128)S(1)} %bitcast.25, bf16[256,96]{1,0:T(8,128)(2,1)S(1)} %pad_maximum_fusion.pairs_ref, bf16[32,96]{1,0:T(8,128)(2,1)S(1)} %get-tuple-element.14.partner_ref, bf16[32,96]{1,0:T(8,128)(2,1)S(1)} %get-tuple-element.15.squares_ref, ...), custom_call_target="tpu_custom_call" | custom-call | tf_op jit(solution)/shard_map/react/pallas_call | solution.py:238
  46.3 13.9 %all_to_all.11.in_ref = f32[16,64,128]{2,1,0:T(8,128)S(1)} all-to-all(f32[16,64,128]{2,1,0:T(8,128)S(1)} %react.1), channel_id=1, replica_groups=mesh['field'=16,'space'=32] {'field'}, dimensions={0} | all-to-all | bytes 1048576 | tf_op jit(solution)/shard_map/all_to_all | solution.py:247
  60.2 0.9 %home.1 = f32[1024,128]{1,0:T(8,128)} custom-call(f32[16,64,128]{2,1,0:T(8,128)S(1)} %all_to_all.11.in_ref), custom_call_target="tpu_custom_call" | custom-call | tf_op jit(solution)/shard_map/home/pallas_call | solution.py:248
  (12 shorter events, 0.1 us)
Async XLA Ops:
  0.0 17.5 %copy-start = (f32[2,16,128]{2,1,0:T(8,128)S(1)}, f32[2,16,128]{2,1,0:T(8,128)}, u32[]{:S(2)}) copy-start(f32[2,16,128]{2,1,0:T(8,128)} %param.11) | copy-start | bytes 49156
  0.0 16.2 %copy-start.4 = (s32[4,256]{1,0:T(4,128)S(1)}, s32[4,256]{1,0:T(4,128)}, u32[]{:S(2)}) copy-start(s32[4,256]{1,0:T(4,128)} %param.13) | copy-start | bytes 12292
  0.0 16.2 %copy-start.5 = (f32[256]{0:T(256)S(1)}, f32[256]{0:T(256)}, u32[]{:S(2)}) copy-start(f32[256]{0:T(256)} %param.12) | copy-start | bytes 3076
  1.1 17.2 %copy-start.1 = (f32[1,32,2,16,128]{4,3,2,1,0:T(8,128)S(1)}, f32[1,32,2,16,128]{4,3,2,1,0:T(8,128)}, u32[]{:S(2)}) copy-start(f32[1,32,2,16,128]{4,3,2,1,0:T(8,128)} %param.8) | copy-start | bytes 1572868
  1.1 19.2 %collective-permute-start = (f32[32,16,128]{2,1,0:T(8,128)S(1)}, f32[32,16,128]{2,1,0:T(8,128)S(1)}, u32[]{:S(2)}, u32[]{:S(2)}) collective-permute-start(f32[32,16,128]{2,1,0:T(8,128)S(1)} %get-tuple-element.18), channel_id=1, source_target_pairs={{0,1},{1,2},{2,3},{3,4},{4,5},{5,6},{6,7},{7,8},{8,9},{9,10},{10,1... | collective-permute-start | bytes 786440 | tf_op jit(solution)/shard_map/ppermute | solution.py:213
  14.2 9.2 %collective-permute-start.1 = (f32[32,16,128]{2,1,0:T(8,128)S(1)}, f32[32,16,128]{2,1,0:T(8,128)S(1)}, u32[]{:S(2)}, u32[]{:S(2)}) collective-permute-start(f32[32,16,128]{2,1,0:T(8,128)S(1)} %get-tuple-element.17), channel_id=1, source_target_pairs={{0,31},{1,0},{2,1},{3,2},{4,3},{5,4},{6,5},{7,6},{8,7},{9,8},{10,9... | collective-permute-start | bytes 786440 | tf_op jit(solution)/shard_map/ppermute | solution.py:213
  17.5 0.8 %copy-start.2 = (f32[2,16,128]{2,1,0:T(8,128)S(1)}, f32[2,16,128]{2,1,0:T(8,128)}, u32[]{:S(2)}) copy-start(f32[2,16,128]{2,1,0:T(8,128)} %dif_ref.3) | copy-start | bytes 49156
  17.5 0.8 %copy-start.3 = (f32[2,16,128]{2,1,0:T(8,128)S(1)}, f32[2,16,128]{2,1,0:T(8,128)}, u32[]{:S(2)}) copy-start(f32[2,16,128]{2,1,0:T(8,128)} %vel_ref.3) | copy-start | bytes 49156

commit v4 on v3

--- a/solution.py
+++ b/solution.py
@@ -21,8 +21,17 @@
     return jax.ShapeDtypeStruct(dims, F32)
 
 
-def local_kernel(tiles_ref, cells_ref, dif_ref, vel_ref, out_ref, rows_ref):
+def local_kernel(
+    block_ref, cells_ref, dif_ref, vel_ref, burn_ref, stoich_ref, rates_ref,
+    out_ref, pairs_ref, partner_ref, squares_ref, produced_ref, rows_ref, flags_ref,
+):
     species, planes, rows, _ = cells_ref.shape
+    reaction_tables(stoich_ref, rates_ref, pairs_ref, partner_ref, squares_ref, produced_ref, species)
+    tiles = planes * rows
+    listed = burn_ref[pl.ds(block_ref[0], 1), :]
+    match = lax.broadcasted_iota(jnp.int32, (tiles, listed.shape[1]), 0) == listed
+    burning = jnp.max(jnp.where(match, 1.0, 0.0), axis=1, keepdims=True)
+    flags_ref[...] = jnp.broadcast_to(burning, flags_ref.shape)
     last = planes - 1
     dif = [dif_ref[z] for z in range(planes)]
     vel = [vel_ref[z] for z in range(planes)]
@@ -52,16 +61,10 @@
     for y in range(rows):
         out_ref[y, 0:data, :] = rows_ref[pl.ds(y, data, stride=rows), :]
         out_ref[y, data : data + 8, :] = jnp.zeros((8, LANES), F32)
-    for entry in range(tiles_ref.shape[0]):
-        tile = tiles_ref[entry]
-
-        @pl.when(tile >= 0)
-        def _():
-            y, z = lax.rem(tile, rows), lax.div(tile, rows)
-            out_ref[y, pl.ds(data + z, 1), :] = jnp.ones((1, LANES), F32)
-
-
-def halo_kernel(core_ref, pieces_ref, first_ref, second_ref, dif_ref, vel_ref, out_ref):
+        out_ref[y, data : data + planes, :] = flags_ref[pl.ds(y, planes, stride=rows), :]
+
+
+def halo_kernel(up_ref, pieces_ref, first_ref, second_ref, dif_ref, vel_ref, out_ref):
     planes, rows, _ = dif_ref.shape
     species = first_ref.shape[0] // rows
     low = dif_ref[0] + vel_ref[0]
@@ -74,11 +77,11 @@
             out_ref[y, bottom, :] = pieces_ref[y, bottom, :] + low[y : y + 1] * below_ref[at, :]
             out_ref[y, top, :] = pieces_ref[y, top, :] + high[y : y + 1] * above_ref[at, :]
 
-    @pl.when(core_ref[0] == 0)
+    @pl.when(up_ref[0] == 0)
     def _():
         add(first_ref, second_ref)
 
-    @pl.when(core_ref[0] == 1)
+    @pl.when(up_ref[0] == 1)
     def _():
         add(second_ref, first_ref)
 
@@ -94,8 +97,8 @@
 
 
 def weights(w):
-    high = lax.reduce_precision(w, 8, 7)
-    return jnp.concatenate([high, high, w - high], 1).astype(BF16)
+    high, low = in_parts(w)
+    return jnp.concatenate([high, high, low], 1)
 
 
 def dot(a, b):
@@ -173,25 +176,23 @@
         copy.wait()
 
 
-def one_hot_rows(indices, count):
-    return (indices[:, None] == jnp.arange(count, dtype=jnp.int32)[None, :]).astype(F32)
-
-
-def reaction_tables(stoich, rates, species):
+def reaction_tables(stoich_ref, rates_ref, pairs_ref, partner_ref, squares_ref, produced_ref, species):
+    rates = rates_ref[...]
+    each = lax.broadcasted_iota(jnp.int32, (species, rates.shape[1]), 0)
+    one, two, three, four = [jnp.where(each == stoich_ref[i : i + 1, :], 1.0, 0.0) for i in range(4)]
+    both, produced = one + two, three + four
+    along = (((1,), (1,)), ((), ()))
     highest = lax.Precision.HIGHEST
-    rate = rates[:, None]
-    one, two = one_hot_rows(stoich[0], species), one_hot_rows(stoich[1], species)
-    produced = one_hot_rows(stoich[2], species) + one_hot_rows(stoich[3], species)
-    both = one + two
-    partner = jnp.dot((one * rate).T, two, precision=highest)
-    squares = jnp.dot(produced.T, (0.5 * rate) * both, precision=highest)
-    produced = (0.5 * produced).T.astype(BF16)
-    return (
-        weights(jnp.sqrt(rate) * both),
-        weights(partner + partner.T),
-        weights(squares),
-        jnp.concatenate([produced, produced], 1),
-    )
+    scaled = rates * both
+    partner = lax.dot_general(rates * one, two, along, highest, F32) + lax.dot_general(rates * two, one, along, highest, F32)
+    squares = lax.dot_general(produced, 0.5 * scaled, along, highest, F32)
+    pairs = jnp.sqrt(rates) * both
+    high = pairs.astype(BF16).astype(F32)
+    pairs_ref[...] = jnp.concatenate([high, high, pairs - high], 0).T.astype(BF16)
+    partner_ref[...] = weights(partner)
+    squares_ref[...] = weights(squares)
+    half = (0.5 * produced).astype(BF16)
+    produced_ref[...] = jnp.concatenate([half, half], 1)
 
 
 def per_device(scalars, diffusivity, velocity, mixing, rates, stoich, burn_tile, helper_slot):
@@ -202,28 +203,36 @@
     species, planes, rows, width = cells.shape
     data = species * planes
     field = lax.axis_index("field")
-    core = field % 2
-
-    def exchanged(ways):
-        pairs = [
-            (f * blocks + i, f * blocks + (i + ways[f % 2]) % blocks) for f in range(fields) for i in range(blocks)
-        ]
-        up = core if ways[1] == 1 else 1 - core
+    core, parity = field % 2, block % 2
+    up_first = (parity + core + 1) % 2
+
+    def exchanged(near_core, up):
+        pairs = []
+        for f in range(fields):
+            for i in range(blocks):
+                step = 1 if (i % 2 == 0) == (f % 2 == near_core) else -1
+                pairs.append((f * blocks + i, f * blocks + (i + step) % blocks))
         plane = lax.dynamic_index_in_dim(cells, up * (planes - 1), 1, False)
         return lax.ppermute(plane, ("field", "space"), pairs).reshape(species * rows, width)
 
-    first, second = exchanged((1, -1)), exchanged((-1, 1))
-    tables = reaction_tables(stoich, rates, species)
+    first, second = exchanged(0, up_first), exchanged(1, 1 - up_first)
     mixing_row = lax.dynamic_index_in_dim(mixing, field, 1, False)
-    pieces = pl.pallas_call(
+    reactions = rates.shape[0]
+    pieces, *tables = pl.pallas_call(
         local_kernel,
-        out_shape=shape(rows, data + 8, width),
-        in_specs=[SMEM] + [VMEM] * 3,
-        out_specs=VMEM,
-        scratch_shapes=[pltpu.VMEM((data * rows, width), F32)],
+        out_shape=(
+            shape(rows, data + 8, width),
+            jax.ShapeDtypeStruct((reactions, 3 * species), BF16),
+            jax.ShapeDtypeStruct((species, 3 * species), BF16),
+            jax.ShapeDtypeStruct((species, 3 * species), BF16),
+            jax.ShapeDtypeStruct((species, 2 * reactions), BF16),
+        ),
+        in_specs=[SMEM] + [VMEM] * 6,
+        out_specs=[VMEM] * 5,
+        scratch_shapes=[pltpu.VMEM((data * rows, width), F32), pltpu.VMEM((planes * rows, width), F32)],
         compiler_params=LIMIT,
         name="local",
-    )(burn_tile[0, block], cells, diffusivity, velocity)
+    )(block.reshape(1), cells, diffusivity, velocity, burn_tile[0], stoich, rates[None])
     pieces = pl.pallas_call(
         halo_kernel,
         out_shape=shape(rows, data + 8, width),
@@ -232,7 +241,7 @@
         input_output_aliases={1: 0},
         compiler_params=LIMIT,
         name="halo",
-    )(core.reshape(1), pieces, first, second, diffusivity, velocity)
+    )(up_first.reshape(1), pieces, first, second, diffusivity, velocity)
     pieces, tables, mixing_row = lax.optimization_barrier((pieces, tables, mixing_row))
     pieces = lax.all_to_all(pieces, "field", 0, 0, tiled=True)
     pieces = pl.pallas_call(

time: 61.4 us -> 61.1 us (level)
  blocking collectives: 33.2 us -> 34.9 us
  matrix products: 0.95 us -> 0 us
    all_to_all x2, blocking collectives: 33.2 us -> 34.9 us  [per_device(): pieces = lax.all_to_all(pieces, 'field', 0, 0, tiled=True)]
    dot_general x2 -> x0, matrix products: 0.95 us -> none  [the longest x1 0.57 us: reaction_tables(): squares = jnp.dot(produced.T, 0.5 * rate * both, precision=highest)]
    squeeze x1 -> x0, local copies, waits for them, and re-layouts: 0.7 us -> none  [per_device(): burn_tile[0, block]]
    unnamed x12 -> x14, local copies, waits for them, and re-layouts: 0.03 us -> 0.66 us
  transfers between devices with their start and end apart: 2 -> 2, of which waited for: 1 -> 1; matrix products, arithmetic and copies ran while one was open for 4% -> 0% of each run, Pallas kernels for 3% -> 2%
where the time goes in v4:
time: 61.1 us; the launch traced here: 60.9 us
  blocking collectives  34.9 us (57%)
  starting transfers between devices  15.6 us (26%)
  Pallas kernels  5.82 us (10%)
  waiting for transfers between devices  2.68 us (4%)
  local copies, waits for them, and re-layouts  1.81 us (3%)
    all_to_all x2, blocking collectives, per_device(): pieces = lax.all_to_all(pieces, 'field', 0, 0, tiled=True)  34.9 us
    ppermute x2, starting transfers between devices, exchanged(): lax.ppermute(plane, ('field', 'space'), pairs)  15.6 us
    pallas_call x1, Pallas kernels, per_device(): pl.pallas_call(react_kernel, out_shape=shape(fields, data, width), in_spe...  3.19 us
    ppermute x2, waiting for transfers between devices, exchanged(): lax.ppermute(plane, ('field', 'space'), pairs)  2.68 us
    pallas_call x1, Pallas kernels, per_device(): pl.pallas_call(local_kernel, out_shape=(shape(rows, data + 8, width), jax...  1.34 us
  transfers between devices with their start and end apart: 2, of which 1 were waited for; matrix products, arithmetic and copies ran while one was open for 0% of the time, Pallas kernels for 2%

profile of v4, /device:TPU:1, one launch (start us, length us, event | category | flops | bytes accessed | tf_op | source)
XLA Modules:
  0.0 60.9 jit_solution(11026837658436105752)
XLA Ops:
  0.0 0.0 copy-start
  0.0 0.0 copy-start.1
  0.0 0.0 copy-start.3
  0.0 0.0 copy-start.4
  0.0 1.1 %dynamic-slice_bitcast_fusion = (f32[32,16,128]{2,1,0:T(8,128)S(1)}, f32[32,16,128]{2,1,0:T(8,128)S(1)}) fusion(f32[1,32,2,16,128]{4,3,2,1,0:T(8,128)} %param.8, s32[]{:T(128)S(6)} %select_n.30, s32[]{:T(128)S(6)} %select_n.29), kind=kLoop, calls=%fused_computation | loop fusion | bytes 1048584 | tf_op jit(solution)/shard_map/jit(dynamic_index_in_dim)/squeeze | solution.py:215
  1.2 4.4 %collective-permute-start.1 = (f32[32,16,128]{2,1,0:T(8,128)S(1)}, f32[32,16,128]{2,1,0:T(8,128)S(1)}, u32[]{:S(2)}, u32[]{:S(2)}) collective-permute-start(f32[32,16,128]{2,1,0:T(8,128)S(1)} %get-tuple-element.27), channel_id=1, source_target_pairs={{0,31},{1,2},{2,1},{3,4},{4,3},{5,6},{6,5},{7,8},{8,7},{9,10},{10,... | collective-permute-start | bytes 786440 | tf_op jit(solution)/shard_map/ppermute | solution.py:216
  5.5 11.2 %collective-permute-start = (f32[32,16,128]{2,1,0:T(8,128)S(1)}, f32[32,16,128]{2,1,0:T(8,128)S(1)}, u32[]{:S(2)}, u32[]{:S(2)}) collective-permute-start(f32[32,16,128]{2,1,0:T(8,128)S(1)} %get-tuple-element.28), channel_id=1, source_target_pairs={{0,1},{1,0},{2,3},{3,2},{4,5},{5,4},{6,7},{7,6},{8,9},{9,8},{10,11... | collective-permute-start | bytes 786440 | tf_op jit(solution)/shard_map/ppermute | solution.py:216
  16.8 0.0 copy-start.5
  16.8 0.0 copy-start.6
  16.8 0.0 copy-done.1
  16.8 0.0 copy-done.2
  16.8 0.0 copy-done.3
  16.8 0.0 copy-done.4
  16.8 0.6 %copy-done.5 = s32[4,256]{1,0:T(4,128)S(1)} copy-done((s32[4,256]{1,0:T(4,128)S(1)}, s32[4,256]{1,0:T(4,128)}, u32[]{:S(2)}) %copy-start.5) | copy-done | bytes 4120
  17.5 0.0 copy-done.6
  17.5 1.3 %local.1 = (f32[16,72,128]{2,1,0:T(8,128)S(1)}, bf16[256,96]{1,0:T(8,128)(2,1)S(1)}, bf16[32,96]{1,0:T(8,128)(2,1)S(1)}, bf16[32,96]{1,0:T(8,128)(2,1)S(1)}, bf16[32,512]{1,0:T(8,128)(2,1)S(1)}) custom-call(s32[1]{0:T(128)} %bitcast.1.block_ref, f32[32,2,16,128]{3,2,1,0:T(8,128)S(1)} %bitcast.13, f32[2,16,128]{2,1,0:T(8,128)S(1)} %copy-done.2, ...), custom_call_target="tpu_custom_call" | custom-call | tf_op jit(solution)/shard_map/local/pallas_call | solution.py:221
  18.8 0.0 copy-done
  18.8 0.0 collective-permute-done.1
  18.9 2.7 %collective-permute-done = f32[32,16,128]{2,1,0:T(8,128)S(1)} collective-permute-done((f32[32,16,128]{2,1,0:T(8,128)S(1)}, f32[32,16,128]{2,1,0:T(8,128)S(1)}, u32[]{:S(2)}, u32[]{:S(2)}) %collective-permute-start) | collective-permute-done | bytes 262176 | tf_op jit(solution)/shard_map/ppermute | solution.py:216
  21.5 0.4 halo.1
  22.0 20.9 %all_to_all.10.in_ref = f32[16,72,128]{2,1,0:T(8,128)S(1)} all-to-all(f32[16,72,128]{2,1,0:T(8,128)S(1)} %halo.1), channel_id=1, replica_groups=mesh['field'=16,'space'=32] {'field'}, dimensions={0} | all-to-all | bytes 1179648 | tf_op jit(solution)/shard_map/all_to_all | solution.py:246
  42.9 3.2 %react.1 = f32[16,64,128]{2,1,0:T(8,128)S(1)} custom-call(f32[16,72,128]{2,1,0:T(8,128)S(1)} %all_to_all.10.in_ref, f32[2,128]{1,0:T(2,128)S(1)} %bitcast.17, bf16[256,96]{1,0:T(8,128)(2,1)S(1)} %get-tuple-element.23.pairs_ref, bf16[32,96]{1,0:T(8,128)(2,1)S(1)} %get-tuple-element.24.partner_ref, bf16[32,96]{1,0:T(8,128)(2,1)S(1)} %get-tuple-element.25.squares_ref, ...), custom_call_target="tpu_custom_call" | custom-call | tf_op jit(solution)/shard_map/react/pallas_call | solution.py:247
  46.1 13.9 %all_to_all.11.in_ref = f32[16,64,128]{2,1,0:T(8,128)S(1)} all-to-all(f32[16,64,128]{2,1,0:T(8,128)S(1)} %react.1), channel_id=1, replica_groups=mesh['field'=16,'space'=32] {'field'}, dimensions={0} | all-to-all | bytes 1048576 | tf_op jit(solution)/shard_map/all_to_all | solution.py:256
  60.0 0.9 %home.1 = f32[1024,128]{1,0:T(8,128)} custom-call(f32[16,64,128]{2,1,0:T(8,128)S(1)} %all_to_all.11.in_ref), custom_call_target="tpu_custom_call" | custom-call | tf_op jit(solution)/shard_map/home/pallas_call | solution.py:257
  (2 shorter events, 0.0 us)
Async XLA Ops:
  0.0 18.8 %copy-start = (f32[2,16,128]{2,1,0:T(8,128)S(1)}, f32[2,16,128]{2,1,0:T(8,128)}, u32[]{:S(2)}) copy-start(f32[2,16,128]{2,1,0:T(8,128)} %param.11) | copy-start | bytes 49156
  0.0 16.8 %copy-start.1 = (f32[1,32,2,16,128]{4,3,2,1,0:T(8,128)S(1)}, f32[1,32,2,16,128]{4,3,2,1,0:T(8,128)}, u32[]{:S(2)}) copy-start(f32[1,32,2,16,128]{4,3,2,1,0:T(8,128)} %param.8) | copy-start | bytes 1572868
  0.0 16.8 %copy-start.2 = (f32[2,16,128]{2,1,0:T(8,128)S(1)}, f32[2,16,128]{2,1,0:T(8,128)}, u32[]{:S(2)}) copy-start(f32[2,16,128]{2,1,0:T(8,128)} %dif_ref.3) | copy-start | bytes 49156
  0.0 16.8 %copy-start.3 = (f32[2,16,128]{2,1,0:T(8,128)S(1)}, f32[2,16,128]{2,1,0:T(8,128)}, u32[]{:S(2)}) copy-start(f32[2,16,128]{2,1,0:T(8,128)} %vel_ref.3) | copy-start | bytes 49156
  0.0 16.8 %copy-start.4 = (s32[1,32,32]{2,1,0:T(8,128)S(1)}, s32[1,32,32]{2,1,0:T(8,128)}, u32[]{:S(2)}) copy-start(s32[1,32,32]{2,1,0:T(8,128)} %param.14) | copy-start | bytes 12292
  1.2 17.7 %collective-permute-start.1 = (f32[32,16,128]{2,1,0:T(8,128)S(1)}, f32[32,16,128]{2,1,0:T(8,128)S(1)}, u32[]{:S(2)}, u32[]{:S(2)}) collective-permute-start(f32[32,16,128]{2,1,0:T(8,128)S(1)} %get-tuple-element.27), channel_id=1, source_target_pairs={{0,31},{1,2},{2,1},{3,4},{4,3},{5,6},{6,5},{7,8},{8,7},{9,10},{10,... | collective-permute-start | bytes 786440 | tf_op jit(solution)/shard_map/ppermute | solution.py:216
  5.5 16.0 %collective-permute-start = (f32[32,16,128]{2,1,0:T(8,128)S(1)}, f32[32,16,128]{2,1,0:T(8,128)S(1)}, u32[]{:S(2)}, u32[]{:S(2)}) collective-permute-start(f32[32,16,128]{2,1,0:T(8,128)S(1)} %get-tuple-element.28), channel_id=1, source_target_pairs={{0,1},{1,0},{2,3},{3,2},{4,5},{5,4},{6,7},{7,6},{8,9},{9,8},{10,11... | collective-permute-start | bytes 786440 | tf_op jit(solution)/shard_map/ppermute | solution.py:216
  16.8 0.7 %copy-start.5 = (s32[4,256]{1,0:T(4,128)S(1)}, s32[4,256]{1,0:T(4,128)}, u32[]{:S(2)}) copy-start(s32[4,256]{1,0:T(4,128)} %stoich_ref.1) | copy-start | bytes 12292
  16.8 0.7 %copy-start.6 = (f32[256]{0:T(256)S(1)}, f32[256]{0:T(256)}, u32[]{:S(2)}) copy-start(f32[256]{0:T(256)} %param.12) | copy-start | bytes 3076

commit v5 on v4

--- a/solution.py
+++ b/solution.py
@@ -1,5 +1,3 @@
-import functools
-
 import jax
 import jax.numpy as jnp
 from jax import lax
@@ -7,9 +5,11 @@
 from jax.experimental.pallas import tpu as pltpu
 from jax.sharding import PartitionSpec as P
 
+
 NSUB = 4
 LANES = 128
 GROUP = 12
+DEPTH = 16
 F32 = jnp.float32
 BF16 = jnp.bfloat16
 VMEM = pl.BlockSpec(memory_space=pltpu.VMEM)
@@ -64,9 +64,9 @@
         out_ref[y, data : data + planes, :] = flags_ref[pl.ds(y, planes, stride=rows), :]
 
 
-def halo_kernel(up_ref, pieces_ref, first_ref, second_ref, dif_ref, vel_ref, out_ref):
+def halo_kernel(odd_ref, late_ref, pieces_ref, early_near_ref, across_ref, late_near_ref, dif_ref, vel_ref, out_ref):
     planes, rows, _ = dif_ref.shape
-    species = first_ref.shape[0] // rows
+    species = across_ref.shape[0] // rows
     low = dif_ref[0] + vel_ref[0]
     high = dif_ref[planes - 1]
 
@@ -77,13 +77,15 @@
             out_ref[y, bottom, :] = pieces_ref[y, bottom, :] + low[y : y + 1] * below_ref[at, :]
             out_ref[y, top, :] = pieces_ref[y, top, :] + high[y : y + 1] * above_ref[at, :]
 
-    @pl.when(up_ref[0] == 0)
-    def _():
-        add(first_ref, second_ref)
-
-    @pl.when(up_ref[0] == 1)
-    def _():
-        add(second_ref, first_ref)
+    for late, near_ref in enumerate((early_near_ref, late_near_ref)):
+
+        @pl.when((odd_ref[0] == 0) & (late_ref[0] == late))
+        def _():
+            add(across_ref, near_ref)
+
+        @pl.when((odd_ref[0] == 1) & (late_ref[0] == late))
+        def _():
+            add(near_ref, across_ref)
 
 
 def in_parts(x):
@@ -107,7 +109,7 @@
 
 def chemistry(concent, pairs, partner, squares, produced):
     substep = 1.0 / NSUB
-    for repeat in range(NSUB):
+    for _ in range(NSUB):
         current = factors(concent)
         pair = dot(pairs, current)
         making = dot(produced, jnp.concatenate(in_parts(pair * pair), 0)) - dot(squares, factors(concent * concent))
@@ -203,19 +205,17 @@
     species, planes, rows, width = cells.shape
     data = species * planes
     field = lax.axis_index("field")
-    core, parity = field % 2, block % 2
-    up_first = (parity + core + 1) % 2
-
-    def exchanged(near_core, up):
-        pairs = []
-        for f in range(fields):
-            for i in range(blocks):
-                step = 1 if (i % 2 == 0) == (f % 2 == near_core) else -1
-                pairs.append((f * blocks + i, f * blocks + (i + step) % blocks))
-        plane = lax.dynamic_index_in_dim(cells, up * (planes - 1), 1, False)
-        return lax.ppermute(plane, ("field", "space"), pairs).reshape(species * rows, width)
-
-    first, second = exchanged(0, up_first), exchanged(1, 1 - up_first)
+    odd = block % 2
+    late = (block % DEPTH) // (DEPTH // 2)
+    near_plane = lax.dynamic_index_in_dim(cells, (1 - odd) * (planes - 1), 1, False)
+    across_plane = lax.dynamic_index_in_dim(cells, odd * (planes - 1), 1, False)
+    near_pairs = [(i, i ^ 1) for i in range(blocks)]
+    half = [i % DEPTH < DEPTH // 2 for i in range(blocks)]
+    across_pairs = [(i, (i + 1 if i % 2 else i - 1) % blocks) for i in range(blocks)]
+    early_near = lax.ppermute(near_plane, "space", [p for p in near_pairs if half[p[0]]])
+    across = lax.ppermute(across_plane, "space", across_pairs)
+    late_near = lax.ppermute(near_plane, "space", [p for p in near_pairs if not half[p[0]]])
+    received = [x.reshape(species * rows, width) for x in (early_near, across, late_near)]
     mixing_row = lax.dynamic_index_in_dim(mixing, field, 1, False)
     reactions = rates.shape[0]
     pieces, *tables = pl.pallas_call(
@@ -236,12 +236,12 @@
     pieces = pl.pallas_call(
         halo_kernel,
         out_shape=shape(rows, data + 8, width),
-        in_specs=[SMEM] + [VMEM] * 5,
+        in_specs=[SMEM] * 2 + [VMEM] * 6,
         out_specs=VMEM,
-        input_output_aliases={1: 0},
+        input_output_aliases={2: 0},
         compiler_params=LIMIT,
         name="halo",
-    )(up_first.reshape(1), pieces, first, second, diffusivity, velocity)
+    )(odd.reshape(1), late.reshape(1), pieces, *received, diffusivity, velocity)
     pieces, tables, mixing_row = lax.optimization_barrier((pieces, tables, mixing_row))
     pieces = lax.all_to_all(pieces, "field", 0, 0, tiled=True)
     pieces = pl.pallas_call(

time: 61.1 us -> 62.6 us (1.025)
  waiting for transfers between devices: 2.68 us -> 3.52 us
  starting transfers between devices: 15.6 us -> 16.3 us
    ppermute x2 -> x3, waiting for transfers between devices: 2.68 us -> 3.52 us  [the longest x1 3.52 us: per_device(): across = lax.ppermute(across_plane, 'space', across_pairs)]
    ppermute x2 -> x3, starting transfers between devices: 15.6 us -> 16.3 us  [the longest x1 11.2 us: per_device(): across = lax.ppermute(across_plane, 'space', across_pairs)]
  transfers between devices with their start and end apart: 2 -> 3, of which waited for: 1 -> 1; matrix products, arithmetic and copies ran while one was open for 0% -> 0% of each run, Pallas kernels for 2% -> 2%
where the time goes in v5:
time: 62.6 us; the launch traced here: 62.3 us
  blocking collectives  34.6 us (55%)
  starting transfers between devices  16.3 us (26%)
  Pallas kernels  5.84 us (9%)
  waiting for transfers between devices  3.52 us (6%)
  local copies, waits for them, and re-layouts  1.86 us (3%)
    all_to_all x2, blocking collectives, per_device(): pieces = lax.all_to_all(pieces, 'field', 0, 0, tiled=True)  34.6 us
    ppermute x1, starting transfers between devices, per_device(): across = lax.ppermute(across_plane, 'space', across_pairs)  11.2 us
    ppermute x1, starting transfers between devices, per_device(): lax.ppermute(near_plane, 'space', [p for p in near_pairs if half[p[0]]])  4.36 us
    ppermute x1, waiting for transfers between devices, per_device(): across = lax.ppermute(across_plane, 'space', across_pairs)  3.52 us
    pallas_call x1, Pallas kernels, per_device(): pl.pallas_call(react_kernel, out_shape=shape(fields, data, width), in_spe...  3.19 us
    pallas_call x1, Pallas kernels, per_device(): pl.pallas_call(local_kernel, out_shape=(shape(rows, data + 8, width), jax...  1.34 us
  transfers between devices with their start and end apart: 3, of which 1 were waited for; matrix products, arithmetic and copies ran while one was open for 0% of the time, Pallas kernels for 2%

profile of v5, /device:TPU:1, one launch (start us, length us, event | category | flops | bytes accessed | tf_op | source)
XLA Modules:
  0.0 62.3 jit_solution(2495788134431812376)
XLA Ops:
  0.0 0.0 copy-start
  0.0 1.1 %dynamic-slice_bitcast_fusion = (f32[32,16,128]{2,1,0:T(8,128)S(1)}, f32[32,16,128]{2,1,0:T(8,128)S(1)}) fusion(f32[1,32,2,16,128]{4,3,2,1,0:T(8,128)} %param.8, s32[]{:T(128)S(6)} %select_n.30, s32[]{:T(128)S(6)} %select_n.29), kind=kLoop, calls=%fused_computation | loop fusion | bytes 1048584 | tf_op jit(solution)/shard_map/jit(dynamic_index_in_dim)/squeeze | solution.py:211
  1.1 0.7 %collective-permute-start.2 = (f32[32,16,128]{2,1,0:T(8,128)S(1)}, f32[32,16,128]{2,1,0:T(8,128)S(1)}, u32[]{:S(2)}, u32[]{:S(2)}) collective-permute-start(f32[32,16,128]{2,1,0:T(8,128)S(1)} %get-tuple-element.28), channel_id=1, source_target_pairs={{8,9},{9,8},{10,11},{11,10},{12,13},{13,12},{14,15},{15,14},{24,25... | collective-permute-start | bytes 786440 | tf_op jit(solution)/shard_map/ppermute | solution.py:217
  1.8 4.4 %collective-permute-start = (f32[32,16,128]{2,1,0:T(8,128)S(1)}, f32[32,16,128]{2,1,0:T(8,128)S(1)}, u32[]{:S(2)}, u32[]{:S(2)}) collective-permute-start(f32[32,16,128]{2,1,0:T(8,128)S(1)} %get-tuple-element.28), channel_id=1, source_target_pairs={{0,1},{1,0},{2,3},{3,2},{4,5},{5,4},{6,7},{7,6},{16,17},{17,16},{1... | collective-permute-start | bytes 786440 | tf_op jit(solution)/shard_map/ppermute | solution.py:215
  6.2 11.2 %collective-permute-start.1 = (f32[32,16,128]{2,1,0:T(8,128)S(1)}, f32[32,16,128]{2,1,0:T(8,128)S(1)}, u32[]{:S(2)}, u32[]{:S(2)}) collective-permute-start(f32[32,16,128]{2,1,0:T(8,128)S(1)} %get-tuple-element.27), channel_id=1, source_target_pairs={{0,31},{1,2},{2,1},{3,4},{4,3},{5,6},{6,5},{7,8},{8,7},{9,10},{10,... | collective-permute-start | bytes 786440 | tf_op jit(solution)/shard_map/ppermute | solution.py:216
  17.4 0.0 copy-start.5
  17.4 0.0 copy-start.4
  17.5 0.0 copy-start.6
  17.5 0.0 copy-start.2
  17.5 0.0 copy-start.3
  17.5 0.0 copy-done.1
  17.5 0.6 copy-done.5
  18.1 0.0 copy-done.4
  18.2 0.0 copy-done.2
  18.2 0.0 copy-done.3
  18.2 1.3 %local.1 = (f32[16,72,128]{2,1,0:T(8,128)S(1)}, bf16[256,96]{1,0:T(8,128)(2,1)S(1)}, bf16[32,96]{1,0:T(8,128)(2,1)S(1)}, bf16[32,96]{1,0:T(8,128)(2,1)S(1)}, bf16[32,512]{1,0:T(8,128)(2,1)S(1)}) custom-call(s32[1]{0:T(128)} %bitcast.2.block_ref, f32[32,2,16,128]{3,2,1,0:T(8,128)S(1)} %bitcast.15, f32[2,16,128]{2,1,0:T(8,128)S(1)} %copy-done.2, ...), custom_call_target="tpu_custom_call" | custom-call | tf_op jit(solution)/shard_map/local/pallas_call | solution.py:221
  19.6 0.0 collective-permute-done.2
  19.6 0.0 collective-permute-done
  19.6 3.5 %collective-permute-done.1 = f32[32,16,128]{2,1,0:T(8,128)S(1)} collective-permute-done((f32[32,16,128]{2,1,0:T(8,128)S(1)}, f32[32,16,128]{2,1,0:T(8,128)S(1)}, u32[]{:S(2)}, u32[]{:S(2)}) %collective-permute-start.1) | collective-permute-done | bytes 262176 | tf_op jit(solution)/shard_map/ppermute | solution.py:216
  23.1 0.4 halo.1
  23.6 20.7 %all_to_all.10.in_ref = f32[16,72,128]{2,1,0:T(8,128)S(1)} all-to-all(f32[16,72,128]{2,1,0:T(8,128)S(1)} %halo.1), channel_id=1, replica_groups=mesh['field'=16,'space'=32] {'field'}, dimensions={0} | all-to-all | bytes 1179648 | tf_op jit(solution)/shard_map/all_to_all | solution.py:246
  44.3 3.2 %react.1 = f32[16,64,128]{2,1,0:T(8,128)S(1)} custom-call(f32[16,72,128]{2,1,0:T(8,128)S(1)} %all_to_all.10.in_ref, f32[2,128]{1,0:T(2,128)S(1)} %bitcast.20, bf16[256,96]{1,0:T(8,128)(2,1)S(1)} %get-tuple-element.23.pairs_ref, bf16[32,96]{1,0:T(8,128)(2,1)S(1)} %get-tuple-element.24.partner_ref, bf16[32,96]{1,0:T(8,128)(2,1)S(1)} %get-tuple-element.25.squares_ref, ...), custom_call_target="tpu_custom_call" | custom-call | tf_op jit(solution)/shard_map/react/pallas_call | solution.py:247
  47.5 13.9 %all_to_all.11.in_ref = f32[16,64,128]{2,1,0:T(8,128)S(1)} all-to-all(f32[16,64,128]{2,1,0:T(8,128)S(1)} %react.1), channel_id=1, replica_groups=mesh['field'=16,'space'=32] {'field'}, dimensions={0} | all-to-all | bytes 1048576 | tf_op jit(solution)/shard_map/all_to_all | solution.py:256
  61.4 0.9 %home.1 = f32[1024,128]{1,0:T(8,128)} custom-call(f32[16,64,128]{2,1,0:T(8,128)S(1)} %all_to_all.11.in_ref), custom_call_target="tpu_custom_call" | custom-call | tf_op jit(solution)/shard_map/home/pallas_call | solution.py:257
  (4 shorter events, 0.0 us)
Async XLA Ops:
  0.0 19.6 %copy-start = (f32[2,16,128]{2,1,0:T(8,128)S(1)}, f32[2,16,128]{2,1,0:T(8,128)}, u32[]{:S(2)}) copy-start(f32[2,16,128]{2,1,0:T(8,128)} %param.11) | copy-start | bytes 49156
  0.0 17.5 %copy-start.1 = (f32[1,32,2,16,128]{4,3,2,1,0:T(8,128)S(1)}, f32[1,32,2,16,128]{4,3,2,1,0:T(8,128)}, u32[]{:S(2)}) copy-start(f32[1,32,2,16,128]{4,3,2,1,0:T(8,128)} %param.8) | copy-start | bytes 1572868
  1.1 18.5 %collective-permute-start.2 = (f32[32,16,128]{2,1,0:T(8,128)S(1)}, f32[32,16,128]{2,1,0:T(8,128)S(1)}, u32[]{:S(2)}, u32[]{:S(2)}) collective-permute-start(f32[32,16,128]{2,1,0:T(8,128)S(1)} %get-tuple-element.28), channel_id=1, source_target_pairs={{8,9},{9,8},{10,11},{11,10},{12,13},{13,12},{14,15},{15,14},{24,25... | collective-permute-start | bytes 786440 | tf_op jit(solution)/shard_map/ppermute | solution.py:217
  1.8 17.8 %collective-permute-start = (f32[32,16,128]{2,1,0:T(8,128)S(1)}, f32[32,16,128]{2,1,0:T(8,128)S(1)}, u32[]{:S(2)}, u32[]{:S(2)}) collective-permute-start(f32[32,16,128]{2,1,0:T(8,128)S(1)} %get-tuple-element.28), channel_id=1, source_target_pairs={{0,1},{1,0},{2,3},{3,2},{4,5},{5,4},{6,7},{7,6},{16,17},{17,16},{1... | collective-permute-start | bytes 786440 | tf_op jit(solution)/shard_map/ppermute | solution.py:215
  6.2 16.9 %collective-permute-start.1 = (f32[32,16,128]{2,1,0:T(8,128)S(1)}, f32[32,16,128]{2,1,0:T(8,128)S(1)}, u32[]{:S(2)}, u32[]{:S(2)}) collective-permute-start(f32[32,16,128]{2,1,0:T(8,128)S(1)} %get-tuple-element.27), channel_id=1, source_target_pairs={{0,31},{1,2},{2,1},{3,4},{4,3},{5,6},{6,5},{7,8},{8,7},{9,10},{10,... | collective-permute-start | bytes 786440 | tf_op jit(solution)/shard_map/ppermute | solution.py:216
  17.4 0.7 %copy-start.5 = (s32[4,256]{1,0:T(4,128)S(1)}, s32[4,256]{1,0:T(4,128)}, u32[]{:S(2)}) copy-start(s32[4,256]{1,0:T(4,128)} %stoich_ref.1) | copy-start | bytes 12292
  17.4 0.7 %copy-start.4 = (s32[1,32,32]{2,1,0:T(8,128)S(1)}, s32[1,32,32]{2,1,0:T(8,128)}, u32[]{:S(2)}) copy-start(s32[1,32,32]{2,1,0:T(8,128)} %param.14) | copy-start | bytes 12292
  17.5 0.7 %copy-start.6 = (f32[256]{0:T(256)S(1)}, f32[256]{0:T(256)}, u32[]{:S(2)}) copy-start(f32[256]{0:T(256)} %param.12) | copy-start | bytes 3076
  17.5 0.7 %copy-start.2 = (f32[2,16,128]{2,1,0:T(8,128)S(1)}, f32[2,16,128]{2,1,0:T(8,128)}, u32[]{:S(2)}) copy-start(f32[2,16,128]{2,1,0:T(8,128)} %dif_ref.3) | copy-start | bytes 49156
  17.5 0.7 %copy-start.3 = (f32[2,16,128]{2,1,0:T(8,128)S(1)}, f32[2,16,128]{2,1,0:T(8,128)}, u32[]{:S(2)}) copy-start(f32[2,16,128]{2,1,0:T(8,128)} %vel_ref.3) | copy-start | bytes 49156

commit v6 on v5

--- a/solution.py
+++ b/solution.py
@@ -1,3 +1,5 @@
+import functools
+
 import jax
 import jax.numpy as jnp
 from jax import lax
@@ -10,6 +12,7 @@
 LANES = 128
 GROUP = 12
 DEPTH = 16
+CORES = 2
 F32 = jnp.float32
 BF16 = jnp.bfloat16
 VMEM = pl.BlockSpec(memory_space=pltpu.VMEM)
@@ -58,24 +61,31 @@
 
     lax.fori_loop(0, species, one_species, 0, unroll=4)
     data = species * planes
-    for y in range(rows):
-        out_ref[y, 0:data, :] = rows_ref[pl.ds(y, data, stride=rows), :]
-        out_ref[y, data : data + 8, :] = jnp.zeros((8, LANES), F32)
-        out_ref[y, data : data + planes, :] = flags_ref[pl.ds(y, planes, stride=rows), :]
+    pieces = out_ref.shape[0]
+    share = rows // pieces
+    for piece in range(pieces):
+        out_ref[piece, share * data :, :] = jnp.zeros((8, LANES), F32)
+        for r in range(share):
+            y = piece * share + r
+            out_ref[piece, r * data : (r + 1) * data, :] = rows_ref[pl.ds(y, data, stride=rows), :]
+            flag = share * data + r * planes
+            out_ref[piece, flag : flag + planes, :] = flags_ref[pl.ds(y, planes, stride=rows), :]
 
 
 def halo_kernel(odd_ref, late_ref, pieces_ref, early_near_ref, across_ref, late_near_ref, dif_ref, vel_ref, out_ref):
     planes, rows, _ = dif_ref.shape
     species = across_ref.shape[0] // rows
+    share = rows // out_ref.shape[0]
     low = dif_ref[0] + vel_ref[0]
     high = dif_ref[planes - 1]
 
     def add(below_ref, above_ref):
         for y in range(rows):
             at = pl.ds(y, species, stride=rows)
-            bottom, top = pl.ds(0, species, stride=planes), pl.ds(planes - 1, species, stride=planes)
-            out_ref[y, bottom, :] = pieces_ref[y, bottom, :] + low[y : y + 1] * below_ref[at, :]
-            out_ref[y, top, :] = pieces_ref[y, top, :] + high[y : y + 1] * above_ref[at, :]
+            piece, start = y // share, y % share * species * planes
+            bottom, top = pl.ds(start, species, stride=planes), pl.ds(start + planes - 1, species, stride=planes)
+            out_ref[piece, bottom, :] = pieces_ref[piece, bottom, :] + low[y : y + 1] * below_ref[at, :]
+            out_ref[piece, top, :] = pieces_ref[piece, top, :] + high[y : y + 1] * above_ref[at, :]
 
     for late, near_ref in enumerate((early_near_ref, late_near_ref)):
 
@@ -117,61 +127,76 @@
     return concent
 
 
-def react_kernel(in_ref, mix_ref, pairs_ref, partner_ref, squares_ref, produced_ref, out_ref, list_ref):
-    fields, data, _ = out_ref.shape
-    planes = mix_ref.shape[0]
+def sum_kernel(in_ref, out_ref):
+    @pl.loop(0, out_ref.shape[0] // 8)
+    def _(block):
+        at = pl.ds(pl.multiple_of(block * 8, 8), 8)
+        total = in_ref[0, at, :]
+        for f in range(1, in_ref.shape[0]):
+            total = total + in_ref[f, at, :]
+        out_ref[at, :] = total
+
+
+def react_kernel(
+    in_ref, own_ref, other_ref, mix_ref, pairs_ref, partner_ref, squares_ref, produced_ref, out_ref, list_ref
+):
+    fields, size, _ = out_ref.shape
+    planes, share, _ = mix_ref.shape
+    data = size // share
     species = data // planes
     even = lax.broadcasted_iota(jnp.int32, (8, LANES), 0) % planes == 0
-    mixing = jnp.where(even, mix_ref[0:1, :], mix_ref[1:2, :])
-
-    def one_block(block, carry):
-        at = pl.ds(pl.multiple_of(block * 8, 8), 8)
-        cells = [in_ref[f, at, :] for f in range(fields)]
-        total = cells[0]
-        for f in range(1, fields):
-            total = total + cells[f]
-        ensemble = total * (1.0 / fields)
-        for f in range(fields):
-            out_ref[f, at, :] = cells[f] - mixing * (cells[f] - ensemble)
-        return carry
-
-    lax.fori_loop(0, data // 8, one_block, 0)
+    for r in range(share):
+        mixing = jnp.where(even, mix_ref[0, r : r + 1, :], mix_ref[1, r : r + 1, :])
+
+        def one_block(block, carry):
+            at = pl.ds(pl.multiple_of(r * data + block * 8, 8), 8)
+            ensemble = (own_ref[at, :] + other_ref[at, :]) * (0.5 / fields)
+            for f in range(fields):
+                cells = in_ref[f, at, :]
+                out_ref[f, at, :] = cells - mixing * (cells - ensemble)
+            return carry
+
+        lax.fori_loop(0, data // 8, one_block, 0)
     marks = jnp.zeros((8, LANES), F32)
     for f in range(fields):
-        marks = marks + in_ref[f, data : data + 8, :] * float(2**f)
-    code = [jnp.max(marks[z : z + 1, :]).astype(jnp.int32) for z in range(planes)]
+        marks = marks + in_ref[f, size : size + 8, :] * float(2**f)
     count = jnp.int32(0)
-    for z in range(planes):
+    for start in range(share * planes):
+        code = jnp.max(marks[start : start + 1, :]).astype(jnp.int32)
         for f in range(fields):
-            list_ref[count] = f * planes + z
-            count = count + ((code[z] >> f) & 1)
+            list_ref[count] = f * share * planes + start
+            count = count + ((code >> f) & 1)
     tables = [ref[...] for ref in (pairs_ref, partner_ref, squares_ref, produced_ref)]
 
     @pl.loop(0, pl.cdiv(count, GROUP))
     def _(group):
         first = group * GROUP
-        entries = [list_ref[jnp.minimum(first + j, count - 1)] for j in range(GROUP)]
-        places = [(lax.div(e, planes), lax.rem(e, planes)) for e in entries]
-        concent = jnp.concatenate([out_ref[f, pl.ds(z, species, stride=planes), :] for f, z in places], 1)
+        places = []
+        for j in range(GROUP):
+            entry = list_ref[jnp.minimum(first + j, count - 1)]
+            f, rest = lax.div(entry, share * planes), lax.rem(entry, share * planes)
+            places.append((f, lax.div(rest, planes) * data + lax.rem(rest, planes)))
+        concent = jnp.concatenate([out_ref[f, pl.ds(start, species, stride=planes), :] for f, start in places], 1)
         concent = chemistry(concent, *tables)
-        for j, (f, z) in enumerate(places):
+        for j, (f, start) in enumerate(places):
 
             @pl.when(first + j < count)
             def _():
-                out_ref[f, pl.ds(z, species, stride=planes), :] = concent[:, j * LANES : (j + 1) * LANES]
-
-
-def home_kernel(in_ref, out_ref, rows_ref, sems):
-    pieces, data, _ = in_ref.shape
+                out_ref[f, pl.ds(start, species, stride=planes), :] = concent[:, j * LANES : (j + 1) * LANES]
+
+
+def home_kernel(rows, in_ref, out_ref, rows_ref, sems):
+    pieces, size, _ = in_ref.shape
+    share = rows // pieces
+    data = size // share
     steps = sems.shape[0]
     part = data // steps
     copies = []
     for step in range(steps):
-        size = part * pieces
-        for y in range(pieces):
-            at = pl.ds(step * size + y, part, stride=pieces)
-            rows_ref[at, :] = in_ref[y, step * part : (step + 1) * part, :]
-        at = pl.ds(step * size, size)
+        for y in range(rows):
+            start = y % share * data + step * part
+            rows_ref[pl.ds(step * part * rows + y, part, stride=rows), :] = in_ref[y // share, start : start + part, :]
+        at = pl.ds(step * part * rows, part * rows)
         copies.append(pltpu.make_async_copy(rows_ref.at[at], out_ref.at[at], sems.at[step]))
         copies[-1].start()
     for copy in copies:
@@ -216,12 +241,16 @@
     across = lax.ppermute(across_plane, "space", across_pairs)
     late_near = lax.ppermute(near_plane, "space", [p for p in near_pairs if not half[p[0]]])
     received = [x.reshape(species * rows, width) for x in (early_near, across, late_near)]
-    mixing_row = lax.dynamic_index_in_dim(mixing, field, 1, False)
+    chips = fields // CORES
+    share = rows // chips
+    groups = [[chip * CORES + core for chip in range(chips)] for core in range(CORES)]
+    partners = [(i, i ^ 1) for i in range(fields)]
+    mixing_rows = lax.dynamic_slice_in_dim(mixing, field // CORES * share, share, 1)
     reactions = rates.shape[0]
     pieces, *tables = pl.pallas_call(
         local_kernel,
         out_shape=(
-            shape(rows, data + 8, width),
+            shape(chips, share * data + 8, width),
             jax.ShapeDtypeStruct((reactions, 3 * species), BF16),
             jax.ShapeDtypeStruct((species, 3 * species), BF16),
             jax.ShapeDtypeStruct((species, 3 * species), BF16),
@@ -235,27 +264,36 @@
     )(block.reshape(1), cells, diffusivity, velocity, burn_tile[0], stoich, rates[None])
     pieces = pl.pallas_call(
         halo_kernel,
-        out_shape=shape(rows, data + 8, width),
+        out_shape=shape(chips, share * data + 8, width),
         in_specs=[SMEM] * 2 + [VMEM] * 6,
         out_specs=VMEM,
         input_output_aliases={2: 0},
         compiler_params=LIMIT,
         name="halo",
     )(odd.reshape(1), late.reshape(1), pieces, *received, diffusivity, velocity)
-    pieces, tables, mixing_row = lax.optimization_barrier((pieces, tables, mixing_row))
-    pieces = lax.all_to_all(pieces, "field", 0, 0, tiled=True)
+    pieces, tables, mixing_rows = lax.optimization_barrier((pieces, tables, mixing_rows))
+    pieces = lax.all_to_all(pieces, "field", 0, 0, axis_index_groups=groups, tiled=True)
+    own = pl.pallas_call(
+        sum_kernel,
+        out_shape=shape(share * data, width),
+        in_specs=[VMEM],
+        out_specs=VMEM,
+        compiler_params=LIMIT,
+        name="sum",
+    )(pieces)
+    other = lax.ppermute(own, "field", partners)
     pieces = pl.pallas_call(
         react_kernel,
-        out_shape=shape(fields, data, width),
-        in_specs=[VMEM] * 6,
+        out_shape=shape(chips, share * data, width),
+        in_specs=[VMEM] * 8,
         out_specs=VMEM,
-        scratch_shapes=[pltpu.SMEM((fields * planes + 1,), jnp.int32)],
+        scratch_shapes=[pltpu.SMEM((chips * share * planes + 1,), jnp.int32)],
         compiler_params=LIMIT,
         name="react",
-    )(pieces, mixing_row, *tables)
-    pieces = lax.all_to_all(pieces, "field", 0, 0, tiled=True)
+    )(pieces, own, other, mixing_rows, *tables)
+    pieces = lax.all_to_all(pieces, "field", 0, 0, axis_index_groups=groups, tiled=True)
     updated = pl.pallas_call(
-        home_kernel,
+        functools.partial(home_kernel, rows),
         out_shape=shape(data * rows, width),
         in_specs=[VMEM],
         out_specs=pl.BlockSpec(memory_space=pltpu.HBM),

time: 62.6 us -> 64.3 us (1.027)
  starting transfers between devices: 16.3 us -> 20.6 us
  blocking collectives: 34.6 us -> 31 us
  waiting for transfers between devices: 3.52 us -> 4.39 us
    ppermute x0 -> x1, starting transfers between devices: none -> 4.29 us  [per_device(): other = lax.ppermute(own, 'field', partners)]
    all_to_all x2, blocking collectives: 34.6 us -> 31 us  [per_device(): lax.all_to_all(pieces, 'field', 0, 0, axis_index_groups=groups, tiled=True)]
    ppermute x0 -> x1, waiting for transfers between devices: none -> 0.88 us  [per_device(): other = lax.ppermute(own, 'field', partners)]
    pallas_call x4 -> x5, Pallas kernels: 5.84 us -> 5.9 us  [the longest x1 3.11 us: per_device(): pl.pallas_call(react_kernel, out_shape=shape(chips, share * data, width),...]
  transfers between devices with their start and end apart: 3 -> 4, of which waited for: 1 -> 2; matrix products, arithmetic and copies ran while one was open for 0% -> 0% of each run, Pallas kernels for 2% -> 2%
where the time goes in v6:
time: 64.3 us; the launch traced here: 63.9 us
  blocking collectives  31 us (48%)
  starting transfers between devices  20.6 us (32%)
  Pallas kernels  5.9 us (9%)
  waiting for transfers between devices  4.39 us (7%)
  local copies, waits for them, and re-layouts  1.86 us (3%)
    all_to_all x2, blocking collectives, per_device(): lax.all_to_all(pieces, 'field', 0, 0, axis_index_groups=groups, tiled=True)  31 us
    ppermute x1, starting transfers between devices, per_device(): across = lax.ppermute(across_plane, 'space', across_pairs)  11.2 us
    ppermute x1, starting transfers between devices, per_device(): lax.ppermute(near_plane, 'space', [p for p in near_pairs if half[p[0]]])  4.36 us
    ppermute x1, starting transfers between devices, per_device(): other = lax.ppermute(own, 'field', partners)  4.29 us
    ppermute x1, waiting for transfers between devices, per_device(): across = lax.ppermute(across_plane, 'space', across_pairs)  3.51 us
    pallas_call x1, Pallas kernels, per_device(): pl.pallas_call(react_kernel, out_shape=shape(chips, share * data, width),...  3.11 us
    pallas_call x1, Pallas kernels, per_device(): pl.pallas_call(local_kernel, out_shape=(shape(chips, share * data + 8, wi...  1.34 us
  transfers between devices with their start and end apart: 4, of which 2 were waited for; matrix products, arithmetic and copies ran while one was open for 0% of the time, Pallas kernels for 2%

profile of v6, /device:TPU:1, one launch (start us, length us, event | category | flops | bytes accessed | tf_op | source)
XLA Modules:
  0.0 63.9 jit_solution(12227052041430621497)
XLA Ops:
  0.0 1.1 %dynamic-slice_bitcast_fusion = (f32[32,16,128]{2,1,0:T(8,128)S(1)}, f32[32,16,128]{2,1,0:T(8,128)S(1)}) fusion(f32[1,32,2,16,128]{4,3,2,1,0:T(8,128)} %param.8, s32[]{:T(128)S(6)} %select_n.32, s32[]{:T(128)S(6)} %select_n.31), kind=kLoop, calls=%fused_computation | loop fusion | bytes 1048584 | tf_op jit(solution)/shard_map/jit(dynamic_index_in_dim)/squeeze | solution.py:236
  1.1 0.7 %collective-permute-start.2 = (f32[32,16,128]{2,1,0:T(8,128)S(1)}, f32[32,16,128]{2,1,0:T(8,128)S(1)}, u32[]{:S(2)}, u32[]{:S(2)}) collective-permute-start(f32[32,16,128]{2,1,0:T(8,128)S(1)} %get-tuple-element.28), channel_id=1, source_target_pairs={{8,9},{9,8},{10,11},{11,10},{12,13},{13,12},{14,15},{15,14},{24,25... | collective-permute-start | bytes 786440 | tf_op jit(solution)/shard_map/ppermute | solution.py:242
  1.8 4.4 %collective-permute-start = (f32[32,16,128]{2,1,0:T(8,128)S(1)}, f32[32,16,128]{2,1,0:T(8,128)S(1)}, u32[]{:S(2)}, u32[]{:S(2)}) collective-permute-start(f32[32,16,128]{2,1,0:T(8,128)S(1)} %get-tuple-element.28), channel_id=1, source_target_pairs={{0,1},{1,0},{2,3},{3,2},{4,5},{5,4},{6,7},{7,6},{16,17},{17,16},{1... | collective-permute-start | bytes 786440 | tf_op jit(solution)/shard_map/ppermute | solution.py:240
  6.2 11.2 %collective-permute-start.1 = (f32[32,16,128]{2,1,0:T(8,128)S(1)}, f32[32,16,128]{2,1,0:T(8,128)S(1)}, u32[]{:S(2)}, u32[]{:S(2)}) collective-permute-start(f32[32,16,128]{2,1,0:T(8,128)S(1)} %get-tuple-element.27), channel_id=1, source_target_pairs={{0,31},{1,2},{2,1},{3,4},{4,3},{5,6},{6,5},{7,8},{8,7},{9,10},{10,... | collective-permute-start | bytes 786440 | tf_op jit(solution)/shard_map/ppermute | solution.py:241
  17.4 0.0 copy-start.6
  17.5 0.0 copy-start.5
  17.5 0.0 copy-start.4
  17.5 0.0 copy-start.2
  17.5 0.0 copy-start.3
  17.5 0.6 copy-done.6
  18.1 0.0 copy-done.5
  18.2 0.0 copy-done.4
  18.2 0.0 copy-done.2
  18.2 0.0 copy-done.3
  18.2 1.3 %local.1 = (f32[8,136,128]{2,1,0:T(8,128)S(1)}, bf16[256,96]{1,0:T(8,128)(2,1)S(1)}, bf16[32,96]{1,0:T(8,128)(2,1)S(1)}, bf16[32,96]{1,0:T(8,128)(2,1)S(1)}, bf16[32,512]{1,0:T(8,128)(2,1)S(1)}) custom-call(s32[1]{0:T(128)} %bitcast.2.block_ref, f32[32,2,16,128]{3,2,1,0:T(8,128)S(1)} %bitcast.14, f32[2,16,128]{2,1,0:T(8,128)S(1)} %copy-done.2, ...), custom_call_target="tpu_custom_call" | custom-call | tf_op jit(solution)/shard_map/local/pallas_call | solution.py:250
  19.6 3.5 %collective-permute-done.1 = f32[32,16,128]{2,1,0:T(8,128)S(1)} collective-permute-done((f32[32,16,128]{2,1,0:T(8,128)S(1)}, f32[32,16,128]{2,1,0:T(8,128)S(1)}, u32[]{:S(2)}, u32[]{:S(2)}) %collective-permute-start.1) | collective-permute-done | bytes 262176 | tf_op jit(solution)/shard_map/ppermute | solution.py:241
  23.1 0.4 halo.1
  23.6 16.9 %all_to_all.10.in_ref = f32[8,136,128]{2,1,0:T(8,128)S(1)} all-to-all(f32[8,136,128]{2,1,0:T(8,128)S(1)} %halo.1), channel_id=1, replica_groups={{0,64,128,192,256,320,384,448},{32,96,160,224,288,352,416,480},{1,65,12..., dimensions={0} | all-to-all | bytes 1114112 | tf_op jit(solution)/shard_map/all_to_all | solution.py:275
  40.5 0.1 sum.1.own_ref
  40.6 4.3 %collective-permute-start.3 = (f32[128,128]{1,0:T(8,128)S(1)}, f32[128,128]{1,0:T(8,128)S(1)}, u32[]{:S(2)}, u32[]{:S(2)}) collective-permute-start(f32[128,128]{1,0:T(8,128)S(1)} %sum.1.own_ref), channel_id=1, source_target_pairs={{0,32},{32,0},{64,96},{96,64},{128,160},{160,128},{192,224},{224,1... | collective-permute-start | bytes 196616 | tf_op jit(solution)/shard_map/ppermute | solution.py:284
  44.9 0.9 %collective-permute-done.3.other_ref = f32[128,128]{1,0:T(8,128)S(1)} collective-permute-done((f32[128,128]{1,0:T(8,128)S(1)}, f32[128,128]{1,0:T(8,128)S(1)}, u32[]{:S(2)}, u32[]{:S(2)}) %collective-permute-start.3) | collective-permute-done | bytes 65568 | tf_op jit(solution)/shard_map/ppermute | solution.py:284
  45.8 3.1 %react.1 = f32[8,128,128]{2,1,0:T(8,128)S(1)} custom-call(f32[8,136,128]{2,1,0:T(8,128)S(1)} %all_to_all.10.in_ref, f32[128,128]{1,0:T(8,128)S(1)} %sum.1.own_ref, f32[128,128]{1,0:T(8,128)S(1)} %collective-permute-done.3.other_ref, f32[2,2,128]{2,1,0:T(2,128)S(1)} %constant_dynamic-slice_fusion.mix_ref, bf16[256,96]{1,0:T(8,128)(2,1)S(1)} %get-tuple-element.23.pairs_ref, ...), custom_call_target="tpu_custom_call" | custom-call | tf_op jit(solution)/shard_map/react/pallas_call | solution.py:285
  48.9 14.1 %all_to_all.11.in_ref = f32[8,128,128]{2,1,0:T(8,128)S(1)} all-to-all(f32[8,128,128]{2,1,0:T(8,128)S(1)} %react.1), channel_id=1, replica_groups={{0,64,128,192,256,320,384,448},{32,96,160,224,288,352,416,480},{1,65,12..., dimensions={0} | all-to-all | bytes 1048576 | tf_op jit(solution)/shard_map/all_to_all | solution.py:294
  63.1 0.9 %home.1 = f32[1024,128]{1,0:T(8,128)} custom-call(f32[8,128,128]{2,1,0:T(8,128)S(1)} %all_to_all.11.in_ref), custom_call_target="tpu_custom_call" | custom-call | tf_op jit(solution)/shard_map/home/pallas_call | solution.py:295
  (7 shorter events, 0.0 us)
Async XLA Ops:
  0.0 19.6 %copy-start = (f32[2,16,128]{2,1,0:T(8,128)S(1)}, f32[2,16,128]{2,1,0:T(8,128)}, u32[]{:S(2)}) copy-start(f32[2,16,128]{2,1,0:T(8,128)} %param.11) | copy-start | bytes 49156
  0.0 17.5 %copy-start.1 = (f32[1,32,2,16,128]{4,3,2,1,0:T(8,128)S(1)}, f32[1,32,2,16,128]{4,3,2,1,0:T(8,128)}, u32[]{:S(2)}) copy-start(f32[1,32,2,16,128]{4,3,2,1,0:T(8,128)} %param.8) | copy-start | bytes 1572868
  1.1 18.5 %collective-permute-start.2 = (f32[32,16,128]{2,1,0:T(8,128)S(1)}, f32[32,16,128]{2,1,0:T(8,128)S(1)}, u32[]{:S(2)}, u32[]{:S(2)}) collective-permute-start(f32[32,16,128]{2,1,0:T(8,128)S(1)} %get-tuple-element.28), channel_id=1, source_target_pairs={{8,9},{9,8},{10,11},{11,10},{12,13},{13,12},{14,15},{15,14},{24,25... | collective-permute-start | bytes 786440 | tf_op jit(solution)/shard_map/ppermute | solution.py:242
  1.8 17.8 %collective-permute-start = (f32[32,16,128]{2,1,0:T(8,128)S(1)}, f32[32,16,128]{2,1,0:T(8,128)S(1)}, u32[]{:S(2)}, u32[]{:S(2)}) collective-permute-start(f32[32,16,128]{2,1,0:T(8,128)S(1)} %get-tuple-element.28), channel_id=1, source_target_pairs={{0,1},{1,0},{2,3},{3,2},{4,5},{5,4},{6,7},{7,6},{16,17},{17,16},{1... | collective-permute-start | bytes 786440 | tf_op jit(solution)/shard_map/ppermute | solution.py:240
  6.2 16.9 %collective-permute-start.1 = (f32[32,16,128]{2,1,0:T(8,128)S(1)}, f32[32,16,128]{2,1,0:T(8,128)S(1)}, u32[]{:S(2)}, u32[]{:S(2)}) collective-permute-start(f32[32,16,128]{2,1,0:T(8,128)S(1)} %get-tuple-element.27), channel_id=1, source_target_pairs={{0,31},{1,2},{2,1},{3,4},{4,3},{5,6},{6,5},{7,8},{8,7},{9,10},{10,... | collective-permute-start | bytes 786440 | tf_op jit(solution)/shard_map/ppermute | solution.py:241
  17.4 0.7 %copy-start.6 = (f32[256]{0:T(256)S(1)}, f32[256]{0:T(256)}, u32[]{:S(2)}) copy-start(f32[256]{0:T(256)} %param.12) | copy-start | bytes 3076
  17.5 0.7 %copy-start.5 = (s32[4,256]{1,0:T(4,128)S(1)}, s32[4,256]{1,0:T(4,128)}, u32[]{:S(2)}) copy-start(s32[4,256]{1,0:T(4,128)} %stoich_ref.1) | copy-start | bytes 12292
  17.5 0.7 %copy-start.4 = (s32[1,32,32]{2,1,0:T(8,128)S(1)}, s32[1,32,32]{2,1,0:T(8,128)}, u32[]{:S(2)}) copy-start(s32[1,32,32]{2,1,0:T(8,128)} %param.14) | copy-start | bytes 12292
  17.5 0.7 %copy-start.2 = (f32[2,16,128]{2,1,0:T(8,128)S(1)}, f32[2,16,128]{2,1,0:T(8,128)}, u32[]{:S(2)}) copy-start(f32[2,16,128]{2,1,0:T(8,128)} %dif_ref.3) | copy-start | bytes 49156
  17.5 0.7 %copy-start.3 = (f32[2,16,128]{2,1,0:T(8,128)S(1)}, f32[2,16,128]{2,1,0:T(8,128)}, u32[]{:S(2)}) copy-start(f32[2,16,128]{2,1,0:T(8,128)} %vel_ref.3) | copy-start | bytes 49156
  40.6 5.2 %collective-permute-start.3 = (f32[128,128]{1,0:T(8,128)S(1)}, f32[128,128]{1,0:T(8,128)S(1)}, u32[]{:S(2)}, u32[]{:S(2)}) collective-permute-start(f32[128,128]{1,0:T(8,128)S(1)} %sum.1.own_ref), channel_id=1, source_target_pairs={{0,32},{32,0},{64,96},{96,64},{128,160},{160,128},{192,224},{224,1... | collective-permute-start | bytes 196616 | tf_op jit(solution)/shard_map/ppermute | solution.py:284

commit v7 on v5

--- a/solution.py
+++ b/solution.py
@@ -8,7 +8,7 @@
 
 NSUB = 4
 LANES = 128
-GROUP = 12
+GROUPS = 10, 12
 DEPTH = 16
 F32 = jnp.float32
 BF16 = jnp.bfloat16
@@ -76,6 +76,7 @@
             bottom, top = pl.ds(0, species, stride=planes), pl.ds(planes - 1, species, stride=planes)
             out_ref[y, bottom, :] = pieces_ref[y, bottom, :] + low[y : y + 1] * below_ref[at, :]
             out_ref[y, top, :] = pieces_ref[y, top, :] + high[y : y + 1] * above_ref[at, :]
+            out_ref[y, species * planes :, :] = pieces_ref[y, species * planes :, :]
 
     for late, near_ref in enumerate((early_near_ref, late_near_ref)):
 
@@ -147,18 +148,29 @@
             count = count + ((code[z] >> f) & 1)
     tables = [ref[...] for ref in (pairs_ref, partner_ref, squares_ref, produced_ref)]
 
-    @pl.loop(0, pl.cdiv(count, GROUP))
-    def _(group):
-        first = group * GROUP
-        entries = [list_ref[jnp.minimum(first + j, count - 1)] for j in range(GROUP)]
-        places = [(lax.div(e, planes), lax.rem(e, planes)) for e in entries]
-        concent = jnp.concatenate([out_ref[f, pl.ds(z, species, stride=planes), :] for f, z in places], 1)
-        concent = chemistry(concent, *tables)
-        for j, (f, z) in enumerate(places):
-
-            @pl.when(first + j < count)
-            def _():
-                out_ref[f, pl.ds(z, species, stride=planes), :] = concent[:, j * LANES : (j + 1) * LANES]
+    def react(size):
+        @pl.loop(0, pl.cdiv(count, size))
+        def _(group):
+            first = group * size
+            entries = [list_ref[jnp.minimum(first + j, count - 1)] for j in range(size)]
+            places = [(lax.div(e, planes), lax.rem(e, planes)) for e in entries]
+            concent = jnp.concatenate([out_ref[f, pl.ds(z, species, stride=planes), :] for f, z in places], 1)
+            concent = chemistry(concent, *tables)
+            for j, (f, z) in enumerate(places):
+
+                @pl.when(first + j < count)
+                def _():
+                    out_ref[f, pl.ds(z, species, stride=planes), :] = concent[:, j * LANES : (j + 1) * LANES]
+
+    small, large = GROUPS
+
+    @pl.when(count <= small)
+    def _():
+        react(small)
+
+    @pl.when(count > small)
+    def _():
+        react(large)
 
 
 def home_kernel(in_ref, out_ref, rows_ref, sems):

time: 62.6 us -> 62.1 us (level)
  no operation moved by 1% of the time
where the time goes in v7:
time: 62.1 us; the launch traced here: 61.8 us
  blocking collectives  34.6 us (56%)
  starting transfers between devices  16.3 us (26%)
  Pallas kernels  5.37 us (9%)
  waiting for transfers between devices  3.52 us (6%)
  local copies, waits for them, and re-layouts  1.86 us (3%)
    all_to_all x2, blocking collectives, per_device(): pieces = lax.all_to_all(pieces, 'field', 0, 0, tiled=True)  34.6 us
    ppermute x1, starting transfers between devices, per_device(): across = lax.ppermute(across_plane, 'space', across_pairs)  11.2 us
    ppermute x1, starting transfers between devices, per_device(): lax.ppermute(near_plane, 'space', [p for p in near_pairs if half[p[0]]])  4.36 us
    ppermute x1, waiting for transfers between devices, per_device(): across = lax.ppermute(across_plane, 'space', across_pairs)  3.52 us
    pallas_call x1, Pallas kernels, per_device(): pl.pallas_call(react_kernel, out_shape=shape(fields, data, width), in_spe...  2.74 us
    pallas_call x1, Pallas kernels, per_device(): pl.pallas_call(local_kernel, out_shape=(shape(rows, data + 8, width), jax...  1.34 us
  transfers between devices with their start and end apart: 3, of which 1 were waited for; matrix products, arithmetic and copies ran while one was open for 0% of the time, Pallas kernels for 2%

profile of v7, /device:TPU:1, one launch (start us, length us, event | category | flops | bytes accessed | tf_op | source)
XLA Modules:
  0.0 61.8 jit_solution(6059378045699354827)
XLA Ops:
  0.0 0.0 copy-start
  0.0 1.1 %dynamic-slice_bitcast_fusion = (f32[32,16,128]{2,1,0:T(8,128)S(1)}, f32[32,16,128]{2,1,0:T(8,128)S(1)}) fusion(f32[1,32,2,16,128]{4,3,2,1,0:T(8,128)} %param.8, s32[]{:T(128)S(6)} %select_n.30, s32[]{:T(128)S(6)} %select_n.29), kind=kLoop, calls=%fused_computation | loop fusion | bytes 1048584 | tf_op jit(solution)/shard_map/jit(dynamic_index_in_dim)/squeeze | solution.py:223
  1.1 0.7 %collective-permute-start.2 = (f32[32,16,128]{2,1,0:T(8,128)S(1)}, f32[32,16,128]{2,1,0:T(8,128)S(1)}, u32[]{:S(2)}, u32[]{:S(2)}) collective-permute-start(f32[32,16,128]{2,1,0:T(8,128)S(1)} %get-tuple-element.28), channel_id=1, source_target_pairs={{8,9},{9,8},{10,11},{11,10},{12,13},{13,12},{14,15},{15,14},{24,25... | collective-permute-start | bytes 786440 | tf_op jit(solution)/shard_map/ppermute | solution.py:229
  1.8 4.4 %collective-permute-start = (f32[32,16,128]{2,1,0:T(8,128)S(1)}, f32[32,16,128]{2,1,0:T(8,128)S(1)}, u32[]{:S(2)}, u32[]{:S(2)}) collective-permute-start(f32[32,16,128]{2,1,0:T(8,128)S(1)} %get-tuple-element.28), channel_id=1, source_target_pairs={{0,1},{1,0},{2,3},{3,2},{4,5},{5,4},{6,7},{7,6},{16,17},{17,16},{1... | collective-permute-start | bytes 786440 | tf_op jit(solution)/shard_map/ppermute | solution.py:227
  6.2 11.2 %collective-permute-start.1 = (f32[32,16,128]{2,1,0:T(8,128)S(1)}, f32[32,16,128]{2,1,0:T(8,128)S(1)}, u32[]{:S(2)}, u32[]{:S(2)}) collective-permute-start(f32[32,16,128]{2,1,0:T(8,128)S(1)} %get-tuple-element.27), channel_id=1, source_target_pairs={{0,31},{1,2},{2,1},{3,4},{4,3},{5,6},{6,5},{7,8},{8,7},{9,10},{10,... | collective-permute-start | bytes 786440 | tf_op jit(solution)/shard_map/ppermute | solution.py:228
  17.4 0.0 copy-start.5
  17.4 0.0 copy-start.4
  17.5 0.0 copy-start.6
  17.5 0.0 copy-start.2
  17.5 0.0 copy-start.3
  17.5 0.0 copy-done.1
  17.5 0.6 copy-done.5
  18.1 0.0 copy-done.4
  18.2 0.0 copy-done.2
  18.2 0.0 copy-done.3
  18.2 1.3 %local.1 = (f32[16,72,128]{2,1,0:T(8,128)S(1)}, bf16[256,96]{1,0:T(8,128)(2,1)S(1)}, bf16[32,96]{1,0:T(8,128)(2,1)S(1)}, bf16[32,96]{1,0:T(8,128)(2,1)S(1)}, bf16[32,512]{1,0:T(8,128)(2,1)S(1)}) custom-call(s32[1]{0:T(128)} %bitcast.2.block_ref, f32[32,2,16,128]{3,2,1,0:T(8,128)S(1)} %bitcast.15, f32[2,16,128]{2,1,0:T(8,128)S(1)} %copy-done.2, ...), custom_call_target="tpu_custom_call" | custom-call | tf_op jit(solution)/shard_map/local/pallas_call | solution.py:233
  19.6 0.0 collective-permute-done.2
  19.6 0.0 collective-permute-done
  19.6 3.5 %collective-permute-done.1 = f32[32,16,128]{2,1,0:T(8,128)S(1)} collective-permute-done((f32[32,16,128]{2,1,0:T(8,128)S(1)}, f32[32,16,128]{2,1,0:T(8,128)S(1)}, u32[]{:S(2)}, u32[]{:S(2)}) %collective-permute-start.1) | collective-permute-done | bytes 262176 | tf_op jit(solution)/shard_map/ppermute | solution.py:228
  23.1 0.4 halo.1
  23.6 20.7 %all_to_all.10.in_ref = f32[16,72,128]{2,1,0:T(8,128)S(1)} all-to-all(f32[16,72,128]{2,1,0:T(8,128)S(1)} %halo.1), channel_id=1, replica_groups=mesh['field'=16,'space'=32] {'field'}, dimensions={0} | all-to-all | bytes 1179648 | tf_op jit(solution)/shard_map/all_to_all | solution.py:258
  44.3 2.7 %react.1 = f32[16,64,128]{2,1,0:T(8,128)S(1)} custom-call(f32[16,72,128]{2,1,0:T(8,128)S(1)} %all_to_all.10.in_ref, f32[2,128]{1,0:T(2,128)S(1)} %bitcast.20, bf16[256,96]{1,0:T(8,128)(2,1)S(1)} %get-tuple-element.23.pairs_ref, bf16[32,96]{1,0:T(8,128)(2,1)S(1)} %get-tuple-element.24.partner_ref, bf16[32,96]{1,0:T(8,128)(2,1)S(1)} %get-tuple-element.25.squares_ref, ...), custom_call_target="tpu_custom_call" | custom-call | tf_op jit(solution)/shard_map/react/pallas_call | solution.py:259
  47.0 13.9 %all_to_all.11.in_ref = f32[16,64,128]{2,1,0:T(8,128)S(1)} all-to-all(f32[16,64,128]{2,1,0:T(8,128)S(1)} %react.1), channel_id=1, replica_groups=mesh['field'=16,'space'=32] {'field'}, dimensions={0} | all-to-all | bytes 1048576 | tf_op jit(solution)/shard_map/all_to_all | solution.py:268
  60.9 0.9 %home.1 = f32[1024,128]{1,0:T(8,128)} custom-call(f32[16,64,128]{2,1,0:T(8,128)S(1)} %all_to_all.11.in_ref), custom_call_target="tpu_custom_call" | custom-call | tf_op jit(solution)/shard_map/home/pallas_call | solution.py:269
  (4 shorter events, 0.0 us)
Async XLA Ops:
  0.0 19.6 %copy-start = (f32[2,16,128]{2,1,0:T(8,128)S(1)}, f32[2,16,128]{2,1,0:T(8,128)}, u32[]{:S(2)}) copy-start(f32[2,16,128]{2,1,0:T(8,128)} %param.11) | copy-start | bytes 49156
  0.0 17.5 %copy-start.1 = (f32[1,32,2,16,128]{4,3,2,1,0:T(8,128)S(1)}, f32[1,32,2,16,128]{4,3,2,1,0:T(8,128)}, u32[]{:S(2)}) copy-start(f32[1,32,2,16,128]{4,3,2,1,0:T(8,128)} %param.8) | copy-start | bytes 1572868
  1.1 18.5 %collective-permute-start.2 = (f32[32,16,128]{2,1,0:T(8,128)S(1)}, f32[32,16,128]{2,1,0:T(8,128)S(1)}, u32[]{:S(2)}, u32[]{:S(2)}) collective-permute-start(f32[32,16,128]{2,1,0:T(8,128)S(1)} %get-tuple-element.28), channel_id=1, source_target_pairs={{8,9},{9,8},{10,11},{11,10},{12,13},{13,12},{14,15},{15,14},{24,25... | collective-permute-start | bytes 786440 | tf_op jit(solution)/shard_map/ppermute | solution.py:229
  1.8 17.8 %collective-permute-start = (f32[32,16,128]{2,1,0:T(8,128)S(1)}, f32[32,16,128]{2,1,0:T(8,128)S(1)}, u32[]{:S(2)}, u32[]{:S(2)}) collective-permute-start(f32[32,16,128]{2,1,0:T(8,128)S(1)} %get-tuple-element.28), channel_id=1, source_target_pairs={{0,1},{1,0},{2,3},{3,2},{4,5},{5,4},{6,7},{7,6},{16,17},{17,16},{1... | collective-permute-start | bytes 786440 | tf_op jit(solution)/shard_map/ppermute | solution.py:227
  6.2 16.9 %collective-permute-start.1 = (f32[32,16,128]{2,1,0:T(8,128)S(1)}, f32[32,16,128]{2,1,0:T(8,128)S(1)}, u32[]{:S(2)}, u32[]{:S(2)}) collective-permute-start(f32[32,16,128]{2,1,0:T(8,128)S(1)} %get-tuple-element.27), channel_id=1, source_target_pairs={{0,31},{1,2},{2,1},{3,4},{4,3},{5,6},{6,5},{7,8},{8,7},{9,10},{10,... | collective-permute-start | bytes 786440 | tf_op jit(solution)/shard_map/ppermute | solution.py:228
  17.4 0.7 %copy-start.5 = (s32[4,256]{1,0:T(4,128)S(1)}, s32[4,256]{1,0:T(4,128)}, u32[]{:S(2)}) copy-start(s32[4,256]{1,0:T(4,128)} %stoich_ref.1) | copy-start | bytes 12292
  17.4 0.7 %copy-start.4 = (s32[1,32,32]{2,1,0:T(8,128)S(1)}, s32[1,32,32]{2,1,0:T(8,128)}, u32[]{:S(2)}) copy-start(s32[1,32,32]{2,1,0:T(8,128)} %param.14) | copy-start | bytes 12292
  17.5 0.7 %copy-start.6 = (f32[256]{0:T(256)S(1)}, f32[256]{0:T(256)}, u32[]{:S(2)}) copy-start(f32[256]{0:T(256)} %param.12) | copy-start | bytes 3076
  17.5 0.7 %copy-start.2 = (f32[2,16,128]{2,1,0:T(8,128)S(1)}, f32[2,16,128]{2,1,0:T(8,128)}, u32[]{:S(2)}) copy-start(f32[2,16,128]{2,1,0:T(8,128)} %dif_ref.3) | copy-start | bytes 49156
  17.5 0.7 %copy-start.3 = (f32[2,16,128]{2,1,0:T(8,128)S(1)}, f32[2,16,128]{2,1,0:T(8,128)}, u32[]{:S(2)}) copy-start(f32[2,16,128]{2,1,0:T(8,128)} %vel_ref.3) | copy-start | bytes 49156

commit v8 on v7

--- a/solution.py
+++ b/solution.py
@@ -218,15 +218,16 @@
     data = species * planes
     field = lax.axis_index("field")
     odd = block % 2
-    late = (block % DEPTH) // (DEPTH // 2)
+    place = block % DEPTH
+    late = ((place >= DEPTH // 2) & (place < DEPTH - 1)).astype(jnp.int32)
     near_plane = lax.dynamic_index_in_dim(cells, (1 - odd) * (planes - 1), 1, False)
     across_plane = lax.dynamic_index_in_dim(cells, odd * (planes - 1), 1, False)
     near_pairs = [(i, i ^ 1) for i in range(blocks)]
-    half = [i % DEPTH < DEPTH // 2 for i in range(blocks)]
+    early_pairs = [p for p in near_pairs if p[0] % DEPTH < DEPTH // 2 or p[1] % DEPTH == DEPTH - 1]
     across_pairs = [(i, (i + 1 if i % 2 else i - 1) % blocks) for i in range(blocks)]
-    early_near = lax.ppermute(near_plane, "space", [p for p in near_pairs if half[p[0]]])
+    early_near = lax.ppermute(near_plane, "space", early_pairs)
     across = lax.ppermute(across_plane, "space", across_pairs)
-    late_near = lax.ppermute(near_plane, "space", [p for p in near_pairs if not half[p[0]]])
+    late_near = lax.ppermute(near_plane, "space", [p for p in near_pairs if p not in early_pairs])
     received = [x.reshape(species * rows, width) for x in (early_near, across, late_near)]
     mixing_row = lax.dynamic_index_in_dim(mixing, field, 1, False)
     reactions = rates.shape[0]

time: 62.1 us -> 62.8 us (1.011)
  no operation moved by 1% of the time
where the time goes in v8:
time: 62.8 us; the launch traced here: 62.4 us
  blocking collectives  34.6 us (55%)
  starting transfers between devices  16.9 us (27%)
  Pallas kernels  5.36 us (9%)
  waiting for transfers between devices  3.56 us (6%)
  local copies, waits for them, and re-layouts  1.84 us (3%)
    all_to_all x2, blocking collectives, per_device(): pieces = lax.all_to_all(pieces, 'field', 0, 0, tiled=True)  34.6 us
    ppermute x1, starting transfers between devices, per_device(): across = lax.ppermute(across_plane, 'space', across_pairs)  11.9 us
    ppermute x1, starting transfers between devices, per_device(): early_near = lax.ppermute(near_plane, 'space', early_pairs)  4.36 us
    ppermute x1, waiting for transfers between devices, per_device(): across = lax.ppermute(across_plane, 'space', across_pairs)  3.56 us
    pallas_call x1, Pallas kernels, per_device(): pl.pallas_call(react_kernel, out_shape=shape(fields, data, width), in_spe...  2.74 us
    pallas_call x1, Pallas kernels, per_device(): pl.pallas_call(local_kernel, out_shape=(shape(rows, data + 8, width), jax...  1.34 us
  transfers between devices with their start and end apart: 3, of which 1 were waited for; matrix products, arithmetic and copies ran while one was open for 0% of the time, Pallas kernels for 2%

profile of v8, /device:TPU:1, one launch (start us, length us, event | category | flops | bytes accessed | tf_op | source)
XLA Modules:
  0.0 62.4 jit_solution(12918104380309361002)
XLA Ops:
  0.0 0.0 copy-start
  0.0 0.0 copy-start.6
  0.0 1.1 %dynamic-slice_bitcast_fusion = (f32[32,16,128]{2,1,0:T(8,128)S(1)}, f32[32,16,128]{2,1,0:T(8,128)S(1)}) fusion(f32[1,32,2,16,128]{4,3,2,1,0:T(8,128)} %param.8, s32[]{:T(128)S(6)} %select_n.25, s32[]{:T(128)S(6)} %select_n.24), kind=kLoop, calls=%fused_computation | loop fusion | bytes 1048584 | tf_op jit(solution)/shard_map/jit(dynamic_index_in_dim)/squeeze | solution.py:224
  1.2 0.7 %collective-permute-start.2 = (f32[32,16,128]{2,1,0:T(8,128)S(1)}, f32[32,16,128]{2,1,0:T(8,128)S(1)}, u32[]{:S(2)}, u32[]{:S(2)}) collective-permute-start(f32[32,16,128]{2,1,0:T(8,128)S(1)} %get-tuple-element.28), channel_id=1, source_target_pairs={{8,9},{9,8},{10,11},{11,10},{12,13},{13,12},{15,14},{24,25},{25,24... | collective-permute-start | bytes 786440 | tf_op jit(solution)/shard_map/ppermute | solution.py:230
  1.8 4.4 %collective-permute-start = (f32[32,16,128]{2,1,0:T(8,128)S(1)}, f32[32,16,128]{2,1,0:T(8,128)S(1)}, u32[]{:S(2)}, u32[]{:S(2)}) collective-permute-start(f32[32,16,128]{2,1,0:T(8,128)S(1)} %get-tuple-element.28), channel_id=1, source_target_pairs={{0,1},{1,0},{2,3},{3,2},{4,5},{5,4},{6,7},{7,6},{14,15},{16,17},{1... | collective-permute-start | bytes 786440 | tf_op jit(solution)/shard_map/ppermute | solution.py:228
  6.2 11.9 %collective-permute-start.1 = (f32[32,16,128]{2,1,0:T(8,128)S(1)}, f32[32,16,128]{2,1,0:T(8,128)S(1)}, u32[]{:S(2)}, u32[]{:S(2)}) collective-permute-start(f32[32,16,128]{2,1,0:T(8,128)S(1)} %get-tuple-element.27), channel_id=1, source_target_pairs={{0,31},{1,2},{2,1},{3,4},{4,3},{5,6},{6,5},{7,8},{8,7},{9,10},{10,... | collective-permute-start | bytes 786440 | tf_op jit(solution)/shard_map/ppermute | solution.py:229
  18.1 0.0 copy-start.5
  18.1 0.0 copy-start.2
  18.1 0.0 copy-start.3
  18.1 0.0 copy-done.1
  18.1 0.0 copy-done.4
  18.2 0.6 copy-done.5
  18.8 0.0 copy-done.2
  18.8 0.0 copy-done.3
  18.8 1.3 %local.1 = (f32[16,72,128]{2,1,0:T(8,128)S(1)}, bf16[256,96]{1,0:T(8,128)(2,1)S(1)}, bf16[32,96]{1,0:T(8,128)(2,1)S(1)}, bf16[32,96]{1,0:T(8,128)(2,1)S(1)}, bf16[32,512]{1,0:T(8,128)(2,1)S(1)}) custom-call(s32[1]{0:T(128)} %bitcast.2.block_ref, f32[32,2,16,128]{3,2,1,0:T(8,128)S(1)} %bitcast.15, f32[2,16,128]{2,1,0:T(8,128)S(1)} %copy-done.2, ...), custom_call_target="tpu_custom_call" | custom-call | tf_op jit(solution)/shard_map/local/pallas_call | solution.py:234
  20.2 0.0 copy-done
  20.2 0.0 collective-permute-done.2
  20.2 0.0 collective-permute-done
  20.2 3.6 %collective-permute-done.1 = f32[32,16,128]{2,1,0:T(8,128)S(1)} collective-permute-done((f32[32,16,128]{2,1,0:T(8,128)S(1)}, f32[32,16,128]{2,1,0:T(8,128)S(1)}, u32[]{:S(2)}, u32[]{:S(2)}) %collective-permute-start.1) | collective-permute-done | bytes 262176 | tf_op jit(solution)/shard_map/ppermute | solution.py:229
  23.8 0.4 halo.1
  24.2 20.7 %all_to_all.10.in_ref = f32[16,72,128]{2,1,0:T(8,128)S(1)} all-to-all(f32[16,72,128]{2,1,0:T(8,128)S(1)} %halo.1), channel_id=1, replica_groups=mesh['field'=16,'space'=32] {'field'}, dimensions={0} | all-to-all | bytes 1179648 | tf_op jit(solution)/shard_map/all_to_all | solution.py:259
  44.9 2.7 %react.1 = f32[16,64,128]{2,1,0:T(8,128)S(1)} custom-call(f32[16,72,128]{2,1,0:T(8,128)S(1)} %all_to_all.10.in_ref, f32[2,128]{1,0:T(2,128)S(1)} %bitcast.20, bf16[256,96]{1,0:T(8,128)(2,1)S(1)} %get-tuple-element.23.pairs_ref, bf16[32,96]{1,0:T(8,128)(2,1)S(1)} %get-tuple-element.24.partner_ref, bf16[32,96]{1,0:T(8,128)(2,1)S(1)} %get-tuple-element.25.squares_ref, ...), custom_call_target="tpu_custom_call" | custom-call | tf_op jit(solution)/shard_map/react/pallas_call | solution.py:260
  47.7 13.9 %all_to_all.11.in_ref = f32[16,64,128]{2,1,0:T(8,128)S(1)} all-to-all(f32[16,64,128]{2,1,0:T(8,128)S(1)} %react.1), channel_id=1, replica_groups=mesh['field'=16,'space'=32] {'field'}, dimensions={0} | all-to-all | bytes 1048576 | tf_op jit(solution)/shard_map/all_to_all | solution.py:269
  61.6 0.9 %home.1 = f32[1024,128]{1,0:T(8,128)} custom-call(f32[16,64,128]{2,1,0:T(8,128)S(1)} %all_to_all.11.in_ref), custom_call_target="tpu_custom_call" | custom-call | tf_op jit(solution)/shard_map/home/pallas_call | solution.py:270
  (4 shorter events, 0.0 us)
Async XLA Ops:
  0.0 20.2 %copy-start = (f32[2,16,128]{2,1,0:T(8,128)S(1)}, f32[2,16,128]{2,1,0:T(8,128)}, u32[]{:S(2)}) copy-start(f32[2,16,128]{2,1,0:T(8,128)} %param.11) | copy-start | bytes 49156
  0.0 18.1 %copy-start.1 = (f32[1,32,2,16,128]{4,3,2,1,0:T(8,128)S(1)}, f32[1,32,2,16,128]{4,3,2,1,0:T(8,128)}, u32[]{:S(2)}) copy-start(f32[1,32,2,16,128]{4,3,2,1,0:T(8,128)} %param.8) | copy-start | bytes 1572868
  0.0 18.1 %copy-start.4 = (s32[1,32,32]{2,1,0:T(8,128)S(1)}, s32[1,32,32]{2,1,0:T(8,128)}, u32[]{:S(2)}) copy-start(s32[1,32,32]{2,1,0:T(8,128)} %param.14) | copy-start | bytes 12292
  0.0 18.1 %copy-start.6 = (f32[256]{0:T(256)S(1)}, f32[256]{0:T(256)}, u32[]{:S(2)}) copy-start(f32[256]{0:T(256)} %param.12) | copy-start | bytes 3076
  1.2 19.1 %collective-permute-start.2 = (f32[32,16,128]{2,1,0:T(8,128)S(1)}, f32[32,16,128]{2,1,0:T(8,128)S(1)}, u32[]{:S(2)}, u32[]{:S(2)}) collective-permute-start(f32[32,16,128]{2,1,0:T(8,128)S(1)} %get-tuple-element.28), channel_id=1, source_target_pairs={{8,9},{9,8},{10,11},{11,10},{12,13},{13,12},{15,14},{24,25},{25,24... | collective-permute-start | bytes 786440 | tf_op jit(solution)/shard_map/ppermute | solution.py:230
  1.8 18.4 %collective-permute-start = (f32[32,16,128]{2,1,0:T(8,128)S(1)}, f32[32,16,128]{2,1,0:T(8,128)S(1)}, u32[]{:S(2)}, u32[]{:S(2)}) collective-permute-start(f32[32,16,128]{2,1,0:T(8,128)S(1)} %get-tuple-element.28), channel_id=1, source_target_pairs={{0,1},{1,0},{2,3},{3,2},{4,5},{5,4},{6,7},{7,6},{14,15},{16,17},{1... | collective-permute-start | bytes 786440 | tf_op jit(solution)/shard_map/ppermute | solution.py:228
  6.2 17.6 %collective-permute-start.1 = (f32[32,16,128]{2,1,0:T(8,128)S(1)}, f32[32,16,128]{2,1,0:T(8,128)S(1)}, u32[]{:S(2)}, u32[]{:S(2)}) collective-permute-start(f32[32,16,128]{2,1,0:T(8,128)S(1)} %get-tuple-element.27), channel_id=1, source_target_pairs={{0,31},{1,2},{2,1},{3,4},{4,3},{5,6},{6,5},{7,8},{8,7},{9,10},{10,... | collective-permute-start | bytes 786440 | tf_op jit(solution)/shard_map/ppermute | solution.py:229
  18.1 0.7 %copy-start.5 = (s32[4,256]{1,0:T(4,128)S(1)}, s32[4,256]{1,0:T(4,128)}, u32[]{:S(2)}) copy-start(s32[4,256]{1,0:T(4,128)} %stoich_ref.1) | copy-start | bytes 12292
  18.1 0.7 %copy-start.2 = (f32[2,16,128]{2,1,0:T(8,128)S(1)}, f32[2,16,128]{2,1,0:T(8,128)}, u32[]{:S(2)}) copy-start(f32[2,16,128]{2,1,0:T(8,128)} %dif_ref.3) | copy-start | bytes 49156
  18.1 0.7 %copy-start.3 = (f32[2,16,128]{2,1,0:T(8,128)S(1)}, f32[2,16,128]{2,1,0:T(8,128)}, u32[]{:S(2)}) copy-start(f32[2,16,128]{2,1,0:T(8,128)} %vel_ref.3) | copy-start | bytes 49156

commit v9 on v7

--- a/solution.py
+++ b/solution.py
@@ -64,29 +64,34 @@
         out_ref[y, data : data + planes, :] = flags_ref[pl.ds(y, planes, stride=rows), :]
 
 
-def halo_kernel(odd_ref, late_ref, pieces_ref, early_near_ref, across_ref, late_near_ref, dif_ref, vel_ref, out_ref):
+def halo_kernel(
+    odd_ref, late_ref, pieces_ref, early_near_ref, across_ref, late_near_ref, dif_ref, vel_ref, out_ref, full_ref, sems
+):
     planes, rows, _ = dif_ref.shape
     species = across_ref.shape[0] // rows
     low = dif_ref[0] + vel_ref[0]
     high = dif_ref[planes - 1]
-
-    def add(below_ref, above_ref):
-        for y in range(rows):
-            at = pl.ds(y, species, stride=rows)
-            bottom, top = pl.ds(0, species, stride=planes), pl.ds(planes - 1, species, stride=planes)
-            out_ref[y, bottom, :] = pieces_ref[y, bottom, :] + low[y : y + 1] * below_ref[at, :]
-            out_ref[y, top, :] = pieces_ref[y, top, :] + high[y : y + 1] * above_ref[at, :]
-            out_ref[y, species * planes :, :] = pieces_ref[y, species * planes :, :]
-
-    for late, near_ref in enumerate((early_near_ref, late_near_ref)):
-
-        @pl.when((odd_ref[0] == 0) & (late_ref[0] == late))
-        def _():
-            add(across_ref, near_ref)
-
-        @pl.when((odd_ref[0] == 1) & (late_ref[0] == late))
-        def _():
-            add(near_ref, across_ref)
+    steps = sems.shape[0]
+    part = rows // steps
+
+    def copy_of(step):
+        at = pl.ds(step * part, part)
+        return pltpu.make_async_copy(full_ref.at[at], out_ref.at[at], sems.at[step])
+
+    odd, late = odd_ref[0] == 1, late_ref[0] == 1
+    bottom, top = pl.ds(0, species, stride=planes), pl.ds(planes - 1, species, stride=planes)
+    for y in range(rows):
+        at = pl.ds(y, species, stride=rows)
+        near = jnp.where(late, late_near_ref[at, :], early_near_ref[at, :])
+        across = across_ref[at, :]
+        below, above = jnp.where(odd, near, across), jnp.where(odd, across, near)
+        full_ref[y, bottom, :] = pieces_ref[y, bottom, :] + low[y : y + 1] * below
+        full_ref[y, top, :] = pieces_ref[y, top, :] + high[y : y + 1] * above
+        full_ref[y, species * planes :, :] = pieces_ref[y, species * planes :, :]
+        if y % part == part - 1:
+            copy_of(y // part).start()
+    for step in range(steps):
+        copy_of(step).wait()
 
 
 def in_parts(x):
@@ -228,7 +233,6 @@
     across = lax.ppermute(across_plane, "space", across_pairs)
     late_near = lax.ppermute(near_plane, "space", [p for p in near_pairs if not half[p[0]]])
     received = [x.reshape(species * rows, width) for x in (early_near, across, late_near)]
-    mixing_row = lax.dynamic_index_in_dim(mixing, field, 1, False)
     reactions = rates.shape[0]
     pieces, *tables = pl.pallas_call(
         local_kernel,
@@ -245,16 +249,18 @@
         compiler_params=LIMIT,
         name="local",
     )(block.reshape(1), cells, diffusivity, velocity, burn_tile[0], stoich, rates[None])
+    pieces = pltpu.with_memory_space_constraint(pieces, pltpu.VMEM)
     pieces = pl.pallas_call(
         halo_kernel,
         out_shape=shape(rows, data + 8, width),
         in_specs=[SMEM] * 2 + [VMEM] * 6,
-        out_specs=VMEM,
-        input_output_aliases={2: 0},
+        out_specs=pl.BlockSpec(memory_space=pltpu.HBM),
+        scratch_shapes=[pltpu.VMEM((rows, data + 8, width), F32), pltpu.SemaphoreType.DMA((4,))],
         compiler_params=LIMIT,
         name="halo",
     )(odd.reshape(1), late.reshape(1), pieces, *received, diffusivity, velocity)
-    pieces, tables, mixing_row = lax.optimization_barrier((pieces, tables, mixing_row))
+    pieces, mixing = lax.optimization_barrier((pieces, mixing))
+    mixing_row = lax.dynamic_index_in_dim(mixing, field, 1, False)
     pieces = lax.all_to_all(pieces, "field", 0, 0, tiled=True)
     pieces = pl.pallas_call(
         react_kernel,

time: 62.1 us -> 63.8 us (1.027)
  blocking collectives: 34.6 us -> 15 us
  waiting for transfers between devices: 3.52 us -> 16.4 us
  starting transfers between devices: 16.3 us -> 24 us
    all_to_all x2 -> x1, blocking collectives: 34.6 us -> 15 us  [per_device(): pieces = lax.all_to_all(pieces, 'field', 0, 0, tiled=True)]
    all_to_all x0 -> x1, waiting for transfers between devices: none -> 11.6 us  [per_device(): pieces = lax.all_to_all(pieces, 'field', 0, 0, tiled=True)]
    all_to_all x0 -> x1, starting transfers between devices: none -> 8.47 us  [per_device(): pieces = lax.all_to_all(pieces, 'field', 0, 0, tiled=True)]
    ppermute x1, waiting for transfers between devices: 0.01 us -> 3.49 us  [per_device(): lax.ppermute(near_plane, 'space', [p for p in near_pairs if half[p[0]]])]
    ppermute x1, starting transfers between devices: 4.36 us -> 1.92 us  [per_device(): lax.ppermute(near_plane, 'space', [p for p in near_pairs if half[p[0]]])]
    ppermute x1, waiting for transfers between devices: 3.52 us -> 1.25 us  [per_device(): across = lax.ppermute(across_plane, 'space', across_pairs)]
    ppermute x1, starting transfers between devices: 11.2 us -> 13 us  [per_device(): across = lax.ppermute(across_plane, 'space', across_pairs)]
  transfers between devices with their start and end apart: 3 -> 4, of which waited for: 1 -> 3; matrix products, arithmetic and copies ran while one was open for 0% -> 0% of each run, Pallas kernels for 2% -> 2%
where the time goes in v9:
time: 63.8 us; the launch traced here: 63.4 us
  starting transfers between devices  24 us (38%)
  waiting for transfers between devices  16.4 us (26%)
  blocking collectives  15 us (24%)
  Pallas kernels  5.95 us (9%)
  local copies, waits for them, and re-layouts  1.85 us (3%)
    all_to_all x1, blocking collectives, per_device(): pieces = lax.all_to_all(pieces, 'field', 0, 0, tiled=True)  15 us
    ppermute x1, starting transfers between devices, per_device(): across = lax.ppermute(across_plane, 'space', across_pairs)  13 us
    all_to_all x1, waiting for transfers between devices, per_device(): pieces = lax.all_to_all(pieces, 'field', 0, 0, tiled=True)  11.6 us
    all_to_all x1, starting transfers between devices, per_device(): pieces = lax.all_to_all(pieces, 'field', 0, 0, tiled=True)  8.47 us
    ppermute x1, waiting for transfers between devices, per_device(): lax.ppermute(near_plane, 'space', [p for p in near_pairs if half[p[0]]])  3.49 us
    pallas_call x1, Pallas kernels, per_device(): pl.pallas_call(react_kernel, out_shape=shape(fields, data, width), in_spe...  2.74 us
    ppermute x1, starting transfers between devices, per_device(): lax.ppermute(near_plane, 'space', [p for p in near_pairs if half[p[0]]])  1.92 us
    pallas_call x1, Pallas kernels, per_device(): pl.pallas_call(local_kernel, out_shape=(shape(rows, data + 8, width), jax...  1.34 us
  transfers between devices with their start and end apart: 4, of which 3 were waited for; matrix products, arithmetic and copies ran while one was open for 0% of the time, Pallas kernels for 2%

profile of v9, /device:TPU:1, one launch (start us, length us, event | category | flops | bytes accessed | tf_op | source)
XLA Modules:
  0.0 63.4 jit_solution(4627914461659252960)
XLA Ops:
  0.0 0.0 copy-start
  0.0 1.1 %dynamic-slice_bitcast_fusion = (f32[32,16,128]{2,1,0:T(8,128)S(1)}, f32[32,16,128]{2,1,0:T(8,128)S(1)}) fusion(f32[1,32,2,16,128]{4,3,2,1,0:T(8,128)} %param.8, s32[]{:T(128)S(6)} %select_n.30, s32[]{:T(128)S(6)} %select_n.29), kind=kLoop, calls=%fused_computation | loop fusion | bytes 1048584 | tf_op jit(solution)/shard_map/jit(dynamic_index_in_dim)/squeeze | solution.py:228
  1.2 13.0 %collective-permute-start.1 = (f32[32,16,128]{2,1,0:T(8,128)S(1)}, f32[32,16,128]{2,1,0:T(8,128)S(1)}, u32[]{:S(2)}, u32[]{:S(2)}) collective-permute-start(f32[32,16,128]{2,1,0:T(8,128)S(1)} %get-tuple-element.19), channel_id=1, source_target_pairs={{0,31},{1,2},{2,1},{3,4},{4,3},{5,6},{6,5},{7,8},{8,7},{9,10},{10,... | collective-permute-start | bytes 786440 | tf_op jit(solution)/shard_map/ppermute | solution.py:233
  14.1 0.7 %collective-permute-start.2 = (f32[32,16,128]{2,1,0:T(8,128)S(1)}, f32[32,16,128]{2,1,0:T(8,128)S(1)}, u32[]{:S(2)}, u32[]{:S(2)}) collective-permute-start(f32[32,16,128]{2,1,0:T(8,128)S(1)} %get-tuple-element.20), channel_id=1, source_target_pairs={{8,9},{9,8},{10,11},{11,10},{12,13},{13,12},{14,15},{15,14},{24,25... | collective-permute-start | bytes 786440 | tf_op jit(solution)/shard_map/ppermute | solution.py:234
  14.8 1.9 %collective-permute-start = (f32[32,16,128]{2,1,0:T(8,128)S(1)}, f32[32,16,128]{2,1,0:T(8,128)S(1)}, u32[]{:S(2)}, u32[]{:S(2)}) collective-permute-start(f32[32,16,128]{2,1,0:T(8,128)S(1)} %get-tuple-element.20), channel_id=1, source_target_pairs={{0,1},{1,0},{2,3},{3,2},{4,5},{5,4},{6,7},{7,6},{16,17},{17,16},{1... | collective-permute-start | bytes 786440 | tf_op jit(solution)/shard_map/ppermute | solution.py:232
  16.7 0.0 copy-start.4
  16.7 0.0 copy-start.6
  16.8 0.0 copy-start.2
  16.8 0.0 copy-start.3
  16.8 0.0 copy-done.1
  16.8 0.6 copy-done.4
  17.5 0.0 copy-done.6
  17.5 0.0 copy-done.2
  17.5 0.0 copy-done.3
  17.5 1.3 %local.1 = (f32[16,72,128]{2,1,0:T(8,128)S(1)}, bf16[256,96]{1,0:T(8,128)(2,1)S(1)}, bf16[32,96]{1,0:T(8,128)(2,1)S(1)}, bf16[32,96]{1,0:T(8,128)(2,1)S(1)}, bf16[32,512]{1,0:T(8,128)(2,1)S(1)}) custom-call(s32[1]{0:T(128)} %bitcast.2.block_ref, f32[32,2,16,128]{3,2,1,0:T(8,128)S(1)} %bitcast.15, f32[2,16,128]{2,1,0:T(8,128)S(1)} %copy-done.2, ...), custom_call_target="tpu_custom_call" | custom-call | tf_op jit(solution)/shard_map/local/pallas_call | solution.py:237
  18.9 1.3 %collective-permute-done.1 = f32[32,16,128]{2,1,0:T(8,128)S(1)} collective-permute-done((f32[32,16,128]{2,1,0:T(8,128)S(1)}, f32[32,16,128]{2,1,0:T(8,128)S(1)}, u32[]{:S(2)}, u32[]{:S(2)}) %collective-permute-start.1) | collective-permute-done | bytes 262176 | tf_op jit(solution)/shard_map/ppermute | solution.py:233
  20.1 0.0 collective-permute-done.2
  20.1 3.5 %collective-permute-done = f32[32,16,128]{2,1,0:T(8,128)S(1)} collective-permute-done((f32[32,16,128]{2,1,0:T(8,128)S(1)}, f32[32,16,128]{2,1,0:T(8,128)S(1)}, u32[]{:S(2)}, u32[]{:S(2)}) %collective-permute-start) | collective-permute-done | bytes 262176 | tf_op jit(solution)/shard_map/ppermute | solution.py:232
  23.6 1.0 %halo.1 = f32[16,72,128]{2,1,0:T(8,128)} custom-call(s32[1]{0:T(128)} %bitcast.odd_ref, s32[1]{0:T(128)} %bitcast.1.late_ref, f32[16,72,128]{2,1,0:T(8,128)S(1)} %get-tuple-element.12.pieces_ref, f32[512,128]{1,0:T(8,128)S(1)} %bitcast.18, f32[512,128]{1,0:T(8,128)S(1)} %bitcast.16, f32[512,128]{1,0:T(8,128)S(1)} %bitcast.17, f32[2,16,128]{2,1,0:T(8,128)S(1)} %copy-done.2, ...), custom_call_target="tpu_custom_call" | custom-call | tf_op jit(solution)/shard_map/halo/pallas_call | solution.py:253
  24.6 8.5 %all-to-all-start = ((f32[16,72,128]{2,1,0:T(8,128)}), f32[16,72,128]{2,1,0:T(8,128)S(1)}, u32[]{:S(2)}, u32[]{:S(2)}) async-start(f32[16,72,128]{2,1,0:T(8,128)} %halo.1), calls=%async_computation | async-start | bytes 1179648 | tf_op jit(solution)/shard_map/all_to_all | solution.py:264
  33.1 11.6 %all-to-all-done.in_ref = f32[16,72,128]{2,1,0:T(8,128)S(1)} async-done(((f32[16,72,128]{2,1,0:T(8,128)}), f32[16,72,128]{2,1,0:T(8,128)S(1)}, u32[]{:S(2)}, u32[]{:S(2)}) %all-to-all-start) | async-done | bytes 589856 | tf_op jit(solution)/shard_map/all_to_all | solution.py:264
  44.7 2.7 %react.1 = f32[16,64,128]{2,1,0:T(8,128)S(1)} custom-call(f32[16,72,128]{2,1,0:T(8,128)S(1)} %all-to-all-done.in_ref, f32[2,128]{1,0:T(2,128)S(1)} %bitcast.20, bf16[256,96]{1,0:T(8,128)(2,1)S(1)} %get-tuple-element.15.pairs_ref, bf16[32,96]{1,0:T(8,128)(2,1)S(1)} %get-tuple-element.16.partner_ref, bf16[32,96]{1,0:T(8,128)(2,1)S(1)} %get-tuple-element.17.squares_ref, ...), custom_call_target="tpu_custom_call" | custom-call | tf_op jit(solution)/shard_map/react/pallas_call | solution.py:265
  47.5 15.0 %all_to_all.10.in_ref = f32[16,64,128]{2,1,0:T(8,128)S(1)} all-to-all(f32[16,64,128]{2,1,0:T(8,128)S(1)} %react.1), channel_id=1, replica_groups=mesh['field'=16,'space'=32] {'field'}, dimensions={0} | all-to-all | bytes 1048576 | tf_op jit(solution)/shard_map/all_to_all | solution.py:274
  62.5 0.9 %home.1 = f32[1024,128]{1,0:T(8,128)} custom-call(f32[16,64,128]{2,1,0:T(8,128)S(1)} %all_to_all.10.in_ref), custom_call_target="tpu_custom_call" | custom-call | tf_op jit(solution)/shard_map/home/pallas_call | solution.py:275
  (5 shorter events, 0.0 us)
Async XLA Ops:
  0.0 33.1 %copy-start = (f32[2,16,128]{2,1,0:T(8,128)S(1)}, f32[2,16,128]{2,1,0:T(8,128)}, u32[]{:S(2)}) copy-start(f32[2,16,128]{2,1,0:T(8,128)} %param.11) | copy-start | bytes 49156
  0.0 16.8 %copy-start.1 = (f32[1,32,2,16,128]{4,3,2,1,0:T(8,128)S(1)}, f32[1,32,2,16,128]{4,3,2,1,0:T(8,128)}, u32[]{:S(2)}) copy-start(f32[1,32,2,16,128]{4,3,2,1,0:T(8,128)} %param.8) | copy-start | bytes 1572868
  0.0 16.8 %copy-start.5 = (s32[4,256]{1,0:T(4,128)S(1)}, s32[4,256]{1,0:T(4,128)}, u32[]{:S(2)}) copy-start(s32[4,256]{1,0:T(4,128)} %stoich_ref.1) | copy-start | bytes 12292
  1.2 19.0 %collective-permute-start.1 = (f32[32,16,128]{2,1,0:T(8,128)S(1)}, f32[32,16,128]{2,1,0:T(8,128)S(1)}, u32[]{:S(2)}, u32[]{:S(2)}) collective-permute-start(f32[32,16,128]{2,1,0:T(8,128)S(1)} %get-tuple-element.19), channel_id=1, source_target_pairs={{0,31},{1,2},{2,1},{3,4},{4,3},{5,6},{6,5},{7,8},{8,7},{9,10},{10,... | collective-permute-start | bytes 786440 | tf_op jit(solution)/shard_map/ppermute | solution.py:233
  14.1 6.0 %collective-permute-start.2 = (f32[32,16,128]{2,1,0:T(8,128)S(1)}, f32[32,16,128]{2,1,0:T(8,128)S(1)}, u32[]{:S(2)}, u32[]{:S(2)}) collective-permute-start(f32[32,16,128]{2,1,0:T(8,128)S(1)} %get-tuple-element.20), channel_id=1, source_target_pairs={{8,9},{9,8},{10,11},{11,10},{12,13},{13,12},{14,15},{15,14},{24,25... | collective-permute-start | bytes 786440 | tf_op jit(solution)/shard_map/ppermute | solution.py:234
  14.8 8.8 %collective-permute-start = (f32[32,16,128]{2,1,0:T(8,128)S(1)}, f32[32,16,128]{2,1,0:T(8,128)S(1)}, u32[]{:S(2)}, u32[]{:S(2)}) collective-permute-start(f32[32,16,128]{2,1,0:T(8,128)S(1)} %get-tuple-element.20), channel_id=1, source_target_pairs={{0,1},{1,0},{2,3},{3,2},{4,5},{5,4},{6,7},{7,6},{16,17},{17,16},{1... | collective-permute-start | bytes 786440 | tf_op jit(solution)/shard_map/ppermute | solution.py:232
  16.7 0.7 %copy-start.4 = (s32[1,32,32]{2,1,0:T(8,128)S(1)}, s32[1,32,32]{2,1,0:T(8,128)}, u32[]{:S(2)}) copy-start(s32[1,32,32]{2,1,0:T(8,128)} %param.14) | copy-start | bytes 12292
  16.7 0.7 %copy-start.6 = (f32[256]{0:T(256)S(1)}, f32[256]{0:T(256)}, u32[]{:S(2)}) copy-start(f32[256]{0:T(256)} %param.12) | copy-start | bytes 3076
  16.8 0.7 %copy-start.2 = (f32[2,16,128]{2,1,0:T(8,128)S(1)}, f32[2,16,128]{2,1,0:T(8,128)}, u32[]{:S(2)}) copy-start(f32[2,16,128]{2,1,0:T(8,128)} %dif_ref.3) | copy-start | bytes 49156
  16.8 0.7 %copy-start.3 = (f32[2,16,128]{2,1,0:T(8,128)S(1)}, f32[2,16,128]{2,1,0:T(8,128)}, u32[]{:S(2)}) copy-start(f32[2,16,128]{2,1,0:T(8,128)} %vel_ref.3) | copy-start | bytes 49156
  24.6 20.1 %all-to-all-start = ((f32[16,72,128]{2,1,0:T(8,128)}), f32[16,72,128]{2,1,0:T(8,128)S(1)}, u32[]{:S(2)}, u32[]{:S(2)}) async-start(f32[16,72,128]{2,1,0:T(8,128)} %halo.1), calls=%async_computation | async-start | bytes 1179648 | tf_op jit(solution)/shard_map/all_to_all | solution.py:264

commit v10 on v7

--- a/solution.py
+++ b/solution.py
@@ -10,6 +10,7 @@
 LANES = 128
 GROUPS = 10, 12
 DEPTH = 16
+ORDER = (13, 1, 8, 3, 6, 10, 9, 5, 14, 15, 11, 0, 4, 12, 7, 2)
 F32 = jnp.float32
 BF16 = jnp.bfloat16
 VMEM = pl.BlockSpec(memory_space=pltpu.VMEM)
@@ -228,7 +229,8 @@
     across = lax.ppermute(across_plane, "space", across_pairs)
     late_near = lax.ppermute(near_plane, "space", [p for p in near_pairs if not half[p[0]]])
     received = [x.reshape(species * rows, width) for x in (early_near, across, late_near)]
-    mixing_row = lax.dynamic_index_in_dim(mixing, field, 1, False)
+    owned = sum(jnp.where(field == member, place, 0) for place, member in enumerate(ORDER))
+    mixing_row = lax.dynamic_index_in_dim(mixing, owned, 1, False)
     reactions = rates.shape[0]
     pieces, *tables = pl.pallas_call(
         local_kernel,
@@ -255,7 +257,7 @@
         name="halo",
     )(odd.reshape(1), late.reshape(1), pieces, *received, diffusivity, velocity)
     pieces, tables, mixing_row = lax.optimization_barrier((pieces, tables, mixing_row))
-    pieces = lax.all_to_all(pieces, "field", 0, 0, tiled=True)
+    pieces = lax.all_to_all(pieces, "field", 0, 0, axis_index_groups=[list(ORDER)], tiled=True)
     pieces = pl.pallas_call(
         react_kernel,
         out_shape=shape(fields, data, width),
@@ -265,7 +267,7 @@
         compiler_params=LIMIT,
         name="react",
     )(pieces, mixing_row, *tables)
-    pieces = lax.all_to_all(pieces, "field", 0, 0, tiled=True)
+    pieces = lax.all_to_all(pieces, "field", 0, 0, axis_index_groups=[list(ORDER)], tiled=True)
     updated = pl.pallas_call(
         home_kernel,
         out_shape=shape(data * rows, width),

time: 62.1 us -> 58.5 us (0.942)
  blocking collectives: 34.6 us -> 31 us
    all_to_all x2, blocking collectives: 34.6 us -> 31 us  [per_device(): lax.all_to_all(pieces, 'field', 0, 0, axis_index_groups=[list(ORDER)], ti...]
where the time goes in v10:
time: 58.5 us; the launch traced here: 58.1 us
  blocking collectives  31 us (53%)
  starting transfers between devices  16.3 us (28%)
  Pallas kernels  5.37 us (9%)
  waiting for transfers between devices  3.46 us (6%)
  local copies, waits for them, and re-layouts  1.86 us (3%)
    all_to_all x2, blocking collectives, per_device(): lax.all_to_all(pieces, 'field', 0, 0, axis_index_groups=[list(ORDER)], ti...  31 us
    ppermute x1, starting transfers between devices, per_device(): across = lax.ppermute(across_plane, 'space', across_pairs)  11.2 us
    ppermute x1, starting transfers between devices, per_device(): lax.ppermute(near_plane, 'space', [p for p in near_pairs if half[p[0]]])  4.36 us
    ppermute x1, waiting for transfers between devices, per_device(): across = lax.ppermute(across_plane, 'space', across_pairs)  3.46 us
    pallas_call x1, Pallas kernels, per_device(): pl.pallas_call(react_kernel, out_shape=shape(fields, data, width), in_spe...  2.74 us
    pallas_call x1, Pallas kernels, per_device(): pl.pallas_call(local_kernel, out_shape=(shape(rows, data + 8, width), jax...  1.34 us
  transfers between devices with their start and end apart: 3, of which 1 were waited for; matrix products, arithmetic and copies ran while one was open for 0% of the time, Pallas kernels for 2%

profile of v10, /device:TPU:1, one launch (start us, length us, event | category | flops | bytes accessed | tf_op | source)
XLA Modules:
  0.0 58.1 jit_solution(14084641752459262821)
XLA Ops:
  0.0 0.0 copy-start
  0.0 1.1 %dynamic-slice_bitcast_fusion = (f32[32,16,128]{2,1,0:T(8,128)S(1)}, f32[32,16,128]{2,1,0:T(8,128)S(1)}) fusion(f32[1,32,2,16,128]{4,3,2,1,0:T(8,128)} %param.8, s32[]{:T(128)S(6)} %select_n.77, s32[]{:T(128)S(6)} %select_n.76), kind=kLoop, calls=%fused_computation | loop fusion | bytes 1048584 | tf_op jit(solution)/shard_map/jit(dynamic_index_in_dim)/squeeze | solution.py:224
  1.1 0.7 %collective-permute-start.2 = (f32[32,16,128]{2,1,0:T(8,128)S(1)}, f32[32,16,128]{2,1,0:T(8,128)S(1)}, u32[]{:S(2)}, u32[]{:S(2)}) collective-permute-start(f32[32,16,128]{2,1,0:T(8,128)S(1)} %get-tuple-element.28), channel_id=1, source_target_pairs={{8,9},{9,8},{10,11},{11,10},{12,13},{13,12},{14,15},{15,14},{24,25... | collective-permute-start | bytes 786440 | tf_op jit(solution)/shard_map/ppermute | solution.py:230
  1.8 4.4 %collective-permute-start = (f32[32,16,128]{2,1,0:T(8,128)S(1)}, f32[32,16,128]{2,1,0:T(8,128)S(1)}, u32[]{:S(2)}, u32[]{:S(2)}) collective-permute-start(f32[32,16,128]{2,1,0:T(8,128)S(1)} %get-tuple-element.28), channel_id=1, source_target_pairs={{0,1},{1,0},{2,3},{3,2},{4,5},{5,4},{6,7},{7,6},{16,17},{17,16},{1... | collective-permute-start | bytes 786440 | tf_op jit(solution)/shard_map/ppermute | solution.py:228
  6.2 11.2 %collective-permute-start.1 = (f32[32,16,128]{2,1,0:T(8,128)S(1)}, f32[32,16,128]{2,1,0:T(8,128)S(1)}, u32[]{:S(2)}, u32[]{:S(2)}) collective-permute-start(f32[32,16,128]{2,1,0:T(8,128)S(1)} %get-tuple-element.27), channel_id=1, source_target_pairs={{0,31},{1,2},{2,1},{3,4},{4,3},{5,6},{6,5},{7,8},{8,7},{9,10},{10,... | collective-permute-start | bytes 786440 | tf_op jit(solution)/shard_map/ppermute | solution.py:229
  17.5 0.0 copy-start.5
  17.5 0.0 copy-start.4
  17.5 0.0 copy-start.6
  17.5 0.0 copy-start.2
  17.6 0.0 copy-start.3
  17.6 0.0 copy-done.1
  17.6 0.6 %copy-done.5 = s32[4,256]{1,0:T(4,128)S(1)} copy-done((s32[4,256]{1,0:T(4,128)S(1)}, s32[4,256]{1,0:T(4,128)}, u32[]{:S(2)}) %copy-start.5) | copy-done | bytes 4120
  18.2 0.0 copy-done.4
  18.2 0.0 copy-done.2
  18.3 0.0 copy-done.3
  18.3 1.3 %local.1 = (f32[16,72,128]{2,1,0:T(8,128)S(1)}, bf16[256,96]{1,0:T(8,128)(2,1)S(1)}, bf16[32,96]{1,0:T(8,128)(2,1)S(1)}, bf16[32,96]{1,0:T(8,128)(2,1)S(1)}, bf16[32,512]{1,0:T(8,128)(2,1)S(1)}) custom-call(s32[1]{0:T(128)} %bitcast.2.block_ref, f32[32,2,16,128]{3,2,1,0:T(8,128)S(1)} %bitcast.15, f32[2,16,128]{2,1,0:T(8,128)S(1)} %copy-done.2, ...), custom_call_target="tpu_custom_call" | custom-call | tf_op jit(solution)/shard_map/local/pallas_call | solution.py:235
  19.7 0.0 collective-permute-done.2
  19.7 0.0 collective-permute-done
  19.7 3.5 %collective-permute-done.1 = f32[32,16,128]{2,1,0:T(8,128)S(1)} collective-permute-done((f32[32,16,128]{2,1,0:T(8,128)S(1)}, f32[32,16,128]{2,1,0:T(8,128)S(1)}, u32[]{:S(2)}, u32[]{:S(2)}) %collective-permute-start.1) | collective-permute-done | bytes 262176 | tf_op jit(solution)/shard_map/ppermute | solution.py:229
  23.1 0.4 halo.1
  23.6 16.6 %all_to_all.10.in_ref = f32[16,72,128]{2,1,0:T(8,128)S(1)} all-to-all(f32[16,72,128]{2,1,0:T(8,128)S(1)} %halo.1), channel_id=1, replica_groups={{416,32,256,96,192,320,288,160,448,480,352,0,128,384,224,64},{417,33,25..., dimensions={0} | all-to-all | bytes 1179648 | tf_op jit(solution)/shard_map/all_to_all | solution.py:260
  40.1 2.7 %react.1 = f32[16,64,128]{2,1,0:T(8,128)S(1)} custom-call(f32[16,72,128]{2,1,0:T(8,128)S(1)} %all_to_all.10.in_ref, f32[2,128]{1,0:T(2,128)S(1)} %bitcast.20, bf16[256,96]{1,0:T(8,128)(2,1)S(1)} %get-tuple-element.23.pairs_ref, bf16[32,96]{1,0:T(8,128)(2,1)S(1)} %get-tuple-element.24.partner_ref, bf16[32,96]{1,0:T(8,128)(2,1)S(1)} %get-tuple-element.25.squares_ref, ...), custom_call_target="tpu_custom_call" | custom-call | tf_op jit(solution)/shard_map/react/pallas_call | solution.py:261
  42.9 14.4 %all_to_all.11.in_ref = f32[16,64,128]{2,1,0:T(8,128)S(1)} all-to-all(f32[16,64,128]{2,1,0:T(8,128)S(1)} %react.1), channel_id=1, replica_groups={{416,32,256,96,192,320,288,160,448,480,352,0,128,384,224,64},{417,33,25..., dimensions={0} | all-to-all | bytes 1048576 | tf_op jit(solution)/shard_map/all_to_all | solution.py:270
  57.3 0.9 %home.1 = f32[1024,128]{1,0:T(8,128)} custom-call(f32[16,64,128]{2,1,0:T(8,128)S(1)} %all_to_all.11.in_ref), custom_call_target="tpu_custom_call" | custom-call | tf_op jit(solution)/shard_map/home/pallas_call | solution.py:271
  (4 shorter events, 0.0 us)
Async XLA Ops:
  0.0 19.6 %copy-start = (f32[2,16,128]{2,1,0:T(8,128)S(1)}, f32[2,16,128]{2,1,0:T(8,128)}, u32[]{:S(2)}) copy-start(f32[2,16,128]{2,1,0:T(8,128)} %param.11) | copy-start | bytes 49156
  0.0 17.6 %copy-start.1 = (f32[1,32,2,16,128]{4,3,2,1,0:T(8,128)S(1)}, f32[1,32,2,16,128]{4,3,2,1,0:T(8,128)}, u32[]{:S(2)}) copy-start(f32[1,32,2,16,128]{4,3,2,1,0:T(8,128)} %param.8) | copy-start | bytes 1572868
  1.1 18.5 %collective-permute-start.2 = (f32[32,16,128]{2,1,0:T(8,128)S(1)}, f32[32,16,128]{2,1,0:T(8,128)S(1)}, u32[]{:S(2)}, u32[]{:S(2)}) collective-permute-start(f32[32,16,128]{2,1,0:T(8,128)S(1)} %get-tuple-element.28), channel_id=1, source_target_pairs={{8,9},{9,8},{10,11},{11,10},{12,13},{13,12},{14,15},{15,14},{24,25... | collective-permute-start | bytes 786440 | tf_op jit(solution)/shard_map/ppermute | solution.py:230
  1.8 17.9 %collective-permute-start = (f32[32,16,128]{2,1,0:T(8,128)S(1)}, f32[32,16,128]{2,1,0:T(8,128)S(1)}, u32[]{:S(2)}, u32[]{:S(2)}) collective-permute-start(f32[32,16,128]{2,1,0:T(8,128)S(1)} %get-tuple-element.28), channel_id=1, source_target_pairs={{0,1},{1,0},{2,3},{3,2},{4,5},{5,4},{6,7},{7,6},{16,17},{17,16},{1... | collective-permute-start | bytes 786440 | tf_op jit(solution)/shard_map/ppermute | solution.py:228
  6.2 16.9 %collective-permute-start.1 = (f32[32,16,128]{2,1,0:T(8,128)S(1)}, f32[32,16,128]{2,1,0:T(8,128)S(1)}, u32[]{:S(2)}, u32[]{:S(2)}) collective-permute-start(f32[32,16,128]{2,1,0:T(8,128)S(1)} %get-tuple-element.27), channel_id=1, source_target_pairs={{0,31},{1,2},{2,1},{3,4},{4,3},{5,6},{6,5},{7,8},{8,7},{9,10},{10,... | collective-permute-start | bytes 786440 | tf_op jit(solution)/shard_map/ppermute | solution.py:229
  17.5 0.7 %copy-start.5 = (s32[4,256]{1,0:T(4,128)S(1)}, s32[4,256]{1,0:T(4,128)}, u32[]{:S(2)}) copy-start(s32[4,256]{1,0:T(4,128)} %stoich_ref.1) | copy-start | bytes 12292
  17.5 0.7 %copy-start.4 = (s32[1,32,32]{2,1,0:T(8,128)S(1)}, s32[1,32,32]{2,1,0:T(8,128)}, u32[]{:S(2)}) copy-start(s32[1,32,32]{2,1,0:T(8,128)} %param.14) | copy-start | bytes 12292
  17.5 0.7 %copy-start.6 = (f32[256]{0:T(256)S(1)}, f32[256]{0:T(256)}, u32[]{:S(2)}) copy-start(f32[256]{0:T(256)} %param.12) | copy-start | bytes 3076
  17.5 0.7 %copy-start.2 = (f32[2,16,128]{2,1,0:T(8,128)S(1)}, f32[2,16,128]{2,1,0:T(8,128)}, u32[]{:S(2)}) copy-start(f32[2,16,128]{2,1,0:T(8,128)} %dif_ref.3) | copy-start | bytes 49156
  17.6 0.7 %copy-start.3 = (f32[2,16,128]{2,1,0:T(8,128)S(1)}, f32[2,16,128]{2,1,0:T(8,128)}, u32[]{:S(2)}) copy-start(f32[2,16,128]{2,1,0:T(8,128)} %vel_ref.3) | copy-start | bytes 49156

commit v11 on v10

--- a/solution.py
+++ b/solution.py
@@ -8,7 +8,7 @@
 
 NSUB = 4
 LANES = 128
-GROUPS = 10, 12
+GROUPS = 8, 10, 12
 DEPTH = 16
 ORDER = (13, 1, 8, 3, 6, 10, 9, 5, 14, 15, 11, 0, 4, 12, 7, 2)
 F32 = jnp.float32
@@ -163,15 +163,17 @@
                 def _():
                     out_ref[f, pl.ds(z, species, stride=planes), :] = concent[:, j * LANES : (j + 1) * LANES]
 
-    small, large = GROUPS
-
-    @pl.when(count <= small)
-    def _():
-        react(small)
-
-    @pl.when(count > small)
-    def _():
-        react(large)
+    below = -1
+    for size in GROUPS:
+        fits = count > below
+        if size != GROUPS[-1]:
+            fits &= count <= size
+
+        @pl.when(fits)
+        def _():
+            react(size)
+
+        below = size
 
 
 def home_kernel(in_ref, out_ref, rows_ref, sems):
@@ -273,7 +275,7 @@
         out_shape=shape(data * rows, width),
         in_specs=[VMEM],
         out_specs=pl.BlockSpec(memory_space=pltpu.HBM),
-        scratch_shapes=[pltpu.VMEM((data * rows, width), F32), pltpu.SemaphoreType.DMA((4,))],
+        scratch_shapes=[pltpu.VMEM((data * rows, width), F32), pltpu.SemaphoreType.DMA((8,))],
         compiler_params=LIMIT,
         name="home",
     )(pieces)

time: 58.5 us -> 58.4 us (level)
  no operation moved by 1% of the time
where the time goes in v11:
time: 58.4 us; the launch traced here: 58.1 us
  blocking collectives  31 us (53%)
  starting transfers between devices  16.3 us (28%)
  Pallas kernels  5.29 us (9%)
  waiting for transfers between devices  3.46 us (6%)
  local copies, waits for them, and re-layouts  1.86 us (3%)
    all_to_all x2, blocking collectives, per_device(): lax.all_to_all(pieces, 'field', 0, 0, axis_index_groups=[list(ORDER)], ti...  31 us
    ppermute x1, starting transfers between devices, per_device(): across = lax.ppermute(across_plane, 'space', across_pairs)  11.2 us
    ppermute x1, starting transfers between devices, per_device(): lax.ppermute(near_plane, 'space', [p for p in near_pairs if half[p[0]]])  4.36 us
    ppermute x1, waiting for transfers between devices, per_device(): across = lax.ppermute(across_plane, 'space', across_pairs)  3.46 us
    pallas_call x1, Pallas kernels, per_device(): pl.pallas_call(react_kernel, out_shape=shape(fields, data, width), in_spe...  2.66 us
    pallas_call x1, Pallas kernels, per_device(): pl.pallas_call(local_kernel, out_shape=(shape(rows, data + 8, width), jax...  1.34 us
  transfers between devices with their start and end apart: 3, of which 1 were waited for; matrix products, arithmetic and copies ran while one was open for 0% of the time, Pallas kernels for 2%

profile of v11, /device:TPU:1, one launch (start us, length us, event | category | flops | bytes accessed | tf_op | source)
XLA Modules:
  0.0 58.1 jit_solution(13302680456947931065)
XLA Ops:
  0.0 0.0 copy-start
  0.0 1.1 %dynamic-slice_bitcast_fusion = (f32[32,16,128]{2,1,0:T(8,128)S(1)}, f32[32,16,128]{2,1,0:T(8,128)S(1)}) fusion(f32[1,32,2,16,128]{4,3,2,1,0:T(8,128)} %param.8, s32[]{:T(128)S(6)} %select_n.77, s32[]{:T(128)S(6)} %select_n.76), kind=kLoop, calls=%fused_computation | loop fusion | bytes 1048584 | tf_op jit(solution)/shard_map/jit(dynamic_index_in_dim)/squeeze | solution.py:226
  1.1 0.7 %collective-permute-start.2 = (f32[32,16,128]{2,1,0:T(8,128)S(1)}, f32[32,16,128]{2,1,0:T(8,128)S(1)}, u32[]{:S(2)}, u32[]{:S(2)}) collective-permute-start(f32[32,16,128]{2,1,0:T(8,128)S(1)} %get-tuple-element.28), channel_id=1, source_target_pairs={{8,9},{9,8},{10,11},{11,10},{12,13},{13,12},{14,15},{15,14},{24,25... | collective-permute-start | bytes 786440 | tf_op jit(solution)/shard_map/ppermute | solution.py:232
  1.8 4.4 %collective-permute-start = (f32[32,16,128]{2,1,0:T(8,128)S(1)}, f32[32,16,128]{2,1,0:T(8,128)S(1)}, u32[]{:S(2)}, u32[]{:S(2)}) collective-permute-start(f32[32,16,128]{2,1,0:T(8,128)S(1)} %get-tuple-element.28), channel_id=1, source_target_pairs={{0,1},{1,0},{2,3},{3,2},{4,5},{5,4},{6,7},{7,6},{16,17},{17,16},{1... | collective-permute-start | bytes 786440 | tf_op jit(solution)/shard_map/ppermute | solution.py:230
  6.2 11.2 %collective-permute-start.1 = (f32[32,16,128]{2,1,0:T(8,128)S(1)}, f32[32,16,128]{2,1,0:T(8,128)S(1)}, u32[]{:S(2)}, u32[]{:S(2)}) collective-permute-start(f32[32,16,128]{2,1,0:T(8,128)S(1)} %get-tuple-element.27), channel_id=1, source_target_pairs={{0,31},{1,2},{2,1},{3,4},{4,3},{5,6},{6,5},{7,8},{8,7},{9,10},{10,... | collective-permute-start | bytes 786440 | tf_op jit(solution)/shard_map/ppermute | solution.py:231
  17.5 0.0 copy-start.5
  17.5 0.0 copy-start.4
  17.5 0.0 copy-start.6
  17.5 0.0 copy-start.2
  17.6 0.0 copy-start.3
  17.6 0.0 copy-done.1
  17.6 0.6 %copy-done.5 = s32[4,256]{1,0:T(4,128)S(1)} copy-done((s32[4,256]{1,0:T(4,128)S(1)}, s32[4,256]{1,0:T(4,128)}, u32[]{:S(2)}) %copy-start.5) | copy-done | bytes 4120
  18.2 0.0 copy-done.4
  18.2 0.0 copy-done.2
  18.3 0.0 copy-done.3
  18.3 1.3 %local.1 = (f32[16,72,128]{2,1,0:T(8,128)S(1)}, bf16[256,96]{1,0:T(8,128)(2,1)S(1)}, bf16[32,96]{1,0:T(8,128)(2,1)S(1)}, bf16[32,96]{1,0:T(8,128)(2,1)S(1)}, bf16[32,512]{1,0:T(8,128)(2,1)S(1)}) custom-call(s32[1]{0:T(128)} %bitcast.2.block_ref, f32[32,2,16,128]{3,2,1,0:T(8,128)S(1)} %bitcast.15, f32[2,16,128]{2,1,0:T(8,128)S(1)} %copy-done.2, ...), custom_call_target="tpu_custom_call" | custom-call | tf_op jit(solution)/shard_map/local/pallas_call | solution.py:237
  19.7 0.0 collective-permute-done.2
  19.7 0.0 collective-permute-done
  19.7 3.5 %collective-permute-done.1 = f32[32,16,128]{2,1,0:T(8,128)S(1)} collective-permute-done((f32[32,16,128]{2,1,0:T(8,128)S(1)}, f32[32,16,128]{2,1,0:T(8,128)S(1)}, u32[]{:S(2)}, u32[]{:S(2)}) %collective-permute-start.1) | collective-permute-done | bytes 262176 | tf_op jit(solution)/shard_map/ppermute | solution.py:231
  23.1 0.4 halo.1
  23.6 16.6 %all_to_all.10.in_ref = f32[16,72,128]{2,1,0:T(8,128)S(1)} all-to-all(f32[16,72,128]{2,1,0:T(8,128)S(1)} %halo.1), channel_id=1, replica_groups={{416,32,256,96,192,320,288,160,448,480,352,0,128,384,224,64},{417,33,25..., dimensions={0} | all-to-all | bytes 1179648 | tf_op jit(solution)/shard_map/all_to_all | solution.py:262
  40.1 2.7 %react.1 = f32[16,64,128]{2,1,0:T(8,128)S(1)} custom-call(f32[16,72,128]{2,1,0:T(8,128)S(1)} %all_to_all.10.in_ref, f32[2,128]{1,0:T(2,128)S(1)} %bitcast.20, bf16[256,96]{1,0:T(8,128)(2,1)S(1)} %get-tuple-element.23.pairs_ref, bf16[32,96]{1,0:T(8,128)(2,1)S(1)} %get-tuple-element.24.partner_ref, bf16[32,96]{1,0:T(8,128)(2,1)S(1)} %get-tuple-element.25.squares_ref, ...), custom_call_target="tpu_custom_call" | custom-call | tf_op jit(solution)/shard_map/react/pallas_call | solution.py:263
  42.8 14.4 %all_to_all.11.in_ref = f32[16,64,128]{2,1,0:T(8,128)S(1)} all-to-all(f32[16,64,128]{2,1,0:T(8,128)S(1)} %react.1), channel_id=1, replica_groups={{416,32,256,96,192,320,288,160,448,480,352,0,128,384,224,64},{417,33,25..., dimensions={0} | all-to-all | bytes 1048576 | tf_op jit(solution)/shard_map/all_to_all | solution.py:272
  57.2 0.9 %home.1 = f32[1024,128]{1,0:T(8,128)} custom-call(f32[16,64,128]{2,1,0:T(8,128)S(1)} %all_to_all.11.in_ref), custom_call_target="tpu_custom_call" | custom-call | tf_op jit(solution)/shard_map/home/pallas_call | solution.py:273
  (4 shorter events, 0.0 us)
Async XLA Ops:
  0.0 19.6 %copy-start = (f32[2,16,128]{2,1,0:T(8,128)S(1)}, f32[2,16,128]{2,1,0:T(8,128)}, u32[]{:S(2)}) copy-start(f32[2,16,128]{2,1,0:T(8,128)} %param.11) | copy-start | bytes 49156
  0.0 17.6 %copy-start.1 = (f32[1,32,2,16,128]{4,3,2,1,0:T(8,128)S(1)}, f32[1,32,2,16,128]{4,3,2,1,0:T(8,128)}, u32[]{:S(2)}) copy-start(f32[1,32,2,16,128]{4,3,2,1,0:T(8,128)} %param.8) | copy-start | bytes 1572868
  1.1 18.5 %collective-permute-start.2 = (f32[32,16,128]{2,1,0:T(8,128)S(1)}, f32[32,16,128]{2,1,0:T(8,128)S(1)}, u32[]{:S(2)}, u32[]{:S(2)}) collective-permute-start(f32[32,16,128]{2,1,0:T(8,128)S(1)} %get-tuple-element.28), channel_id=1, source_target_pairs={{8,9},{9,8},{10,11},{11,10},{12,13},{13,12},{14,15},{15,14},{24,25... | collective-permute-start | bytes 786440 | tf_op jit(solution)/shard_map/ppermute | solution.py:232
  1.8 17.9 %collective-permute-start = (f32[32,16,128]{2,1,0:T(8,128)S(1)}, f32[32,16,128]{2,1,0:T(8,128)S(1)}, u32[]{:S(2)}, u32[]{:S(2)}) collective-permute-start(f32[32,16,128]{2,1,0:T(8,128)S(1)} %get-tuple-element.28), channel_id=1, source_target_pairs={{0,1},{1,0},{2,3},{3,2},{4,5},{5,4},{6,7},{7,6},{16,17},{17,16},{1... | collective-permute-start | bytes 786440 | tf_op jit(solution)/shard_map/ppermute | solution.py:230
  6.2 16.9 %collective-permute-start.1 = (f32[32,16,128]{2,1,0:T(8,128)S(1)}, f32[32,16,128]{2,1,0:T(8,128)S(1)}, u32[]{:S(2)}, u32[]{:S(2)}) collective-permute-start(f32[32,16,128]{2,1,0:T(8,128)S(1)} %get-tuple-element.27), channel_id=1, source_target_pairs={{0,31},{1,2},{2,1},{3,4},{4,3},{5,6},{6,5},{7,8},{8,7},{9,10},{10,... | collective-permute-start | bytes 786440 | tf_op jit(solution)/shard_map/ppermute | solution.py:231
  17.5 0.7 %copy-start.5 = (s32[4,256]{1,0:T(4,128)S(1)}, s32[4,256]{1,0:T(4,128)}, u32[]{:S(2)}) copy-start(s32[4,256]{1,0:T(4,128)} %stoich_ref.1) | copy-start | bytes 12292
  17.5 0.7 %copy-start.4 = (s32[1,32,32]{2,1,0:T(8,128)S(1)}, s32[1,32,32]{2,1,0:T(8,128)}, u32[]{:S(2)}) copy-start(s32[1,32,32]{2,1,0:T(8,128)} %param.14) | copy-start | bytes 12292
  17.5 0.7 %copy-start.6 = (f32[256]{0:T(256)S(1)}, f32[256]{0:T(256)}, u32[]{:S(2)}) copy-start(f32[256]{0:T(256)} %param.12) | copy-start | bytes 3076
  17.5 0.7 %copy-start.2 = (f32[2,16,128]{2,1,0:T(8,128)S(1)}, f32[2,16,128]{2,1,0:T(8,128)}, u32[]{:S(2)}) copy-start(f32[2,16,128]{2,1,0:T(8,128)} %dif_ref.3) | copy-start | bytes 49156
  17.6 0.7 %copy-start.3 = (f32[2,16,128]{2,1,0:T(8,128)S(1)}, f32[2,16,128]{2,1,0:T(8,128)}, u32[]{:S(2)}) copy-start(f32[2,16,128]{2,1,0:T(8,128)} %vel_ref.3) | copy-start | bytes 49156

commit v12 on v11

--- a/solution.py
+++ b/solution.py
@@ -111,11 +111,14 @@
 
 def chemistry(concent, pairs, partner, squares, produced):
     substep = 1.0 / NSUB
+    species = concent.shape[0]
+    both = jnp.concatenate([partner, pairs], 0)
+    made = jnp.concatenate([produced, -squares], 1)
     for _ in range(NSUB):
-        current = factors(concent)
-        pair = dot(pairs, current)
-        making = dot(produced, jnp.concatenate(in_parts(pair * pair), 0)) - dot(squares, factors(concent * concent))
-        concent = (concent + substep * making) / (1.0 + substep * dot(partner, current))
+        picked = dot(both, factors(concent))
+        pair = picked[species:]
+        making = dot(made, jnp.concatenate([*in_parts(pair * pair), factors(concent * concent)], 0))
+        concent = (concent + substep * making) / (1.0 + substep * picked[:species])
     return concent
 
 

time: 58.4 us -> 58 us (level)
  no operation moved by 1% of the time
where the time goes in v12:
time: 58 us; the launch traced here: 57.7 us
  blocking collectives  31 us (53%)
  starting transfers between devices  16.3 us (28%)
  Pallas kernels  4.9 us (8%)
  waiting for transfers between devices  3.46 us (6%)
  local copies, waits for them, and re-layouts  1.86 us (3%)
    all_to_all x2, blocking collectives, per_device(): lax.all_to_all(pieces, 'field', 0, 0, axis_index_groups=[list(ORDER)], ti...  31 us
    ppermute x1, starting transfers between devices, per_device(): across = lax.ppermute(across_plane, 'space', across_pairs)  11.2 us
    ppermute x1, starting transfers between devices, per_device(): lax.ppermute(near_plane, 'space', [p for p in near_pairs if half[p[0]]])  4.36 us
    ppermute x1, waiting for transfers between devices, per_device(): across = lax.ppermute(across_plane, 'space', across_pairs)  3.46 us
    pallas_call x1, Pallas kernels, per_device(): pl.pallas_call(react_kernel, out_shape=shape(fields, data, width), in_spe...  2.27 us
    pallas_call x1, Pallas kernels, per_device(): pl.pallas_call(local_kernel, out_shape=(shape(rows, data + 8, width), jax...  1.34 us
  transfers between devices with their start and end apart: 3, of which 1 were waited for; matrix products, arithmetic and copies ran while one was open for 0% of the time, Pallas kernels for 2%

profile of v12, /device:TPU:1, one launch (start us, length us, event | category | flops | bytes accessed | tf_op | source)
XLA Modules:
  0.0 57.7 jit_solution(15296373997550730506)
XLA Ops:
  0.0 0.0 copy-start
  0.0 1.1 %dynamic-slice_bitcast_fusion = (f32[32,16,128]{2,1,0:T(8,128)S(1)}, f32[32,16,128]{2,1,0:T(8,128)S(1)}) fusion(f32[1,32,2,16,128]{4,3,2,1,0:T(8,128)} %param.8, s32[]{:T(128)S(6)} %select_n.77, s32[]{:T(128)S(6)} %select_n.76), kind=kLoop, calls=%fused_computation | loop fusion | bytes 1048584 | tf_op jit(solution)/shard_map/jit(dynamic_index_in_dim)/squeeze | solution.py:229
  1.1 0.7 %collective-permute-start.2 = (f32[32,16,128]{2,1,0:T(8,128)S(1)}, f32[32,16,128]{2,1,0:T(8,128)S(1)}, u32[]{:S(2)}, u32[]{:S(2)}) collective-permute-start(f32[32,16,128]{2,1,0:T(8,128)S(1)} %get-tuple-element.28), channel_id=1, source_target_pairs={{8,9},{9,8},{10,11},{11,10},{12,13},{13,12},{14,15},{15,14},{24,25... | collective-permute-start | bytes 786440 | tf_op jit(solution)/shard_map/ppermute | solution.py:235
  1.8 4.4 %collective-permute-start = (f32[32,16,128]{2,1,0:T(8,128)S(1)}, f32[32,16,128]{2,1,0:T(8,128)S(1)}, u32[]{:S(2)}, u32[]{:S(2)}) collective-permute-start(f32[32,16,128]{2,1,0:T(8,128)S(1)} %get-tuple-element.28), channel_id=1, source_target_pairs={{0,1},{1,0},{2,3},{3,2},{4,5},{5,4},{6,7},{7,6},{16,17},{17,16},{1... | collective-permute-start | bytes 786440 | tf_op jit(solution)/shard_map/ppermute | solution.py:233
  6.2 11.2 %collective-permute-start.1 = (f32[32,16,128]{2,1,0:T(8,128)S(1)}, f32[32,16,128]{2,1,0:T(8,128)S(1)}, u32[]{:S(2)}, u32[]{:S(2)}) collective-permute-start(f32[32,16,128]{2,1,0:T(8,128)S(1)} %get-tuple-element.27), channel_id=1, source_target_pairs={{0,31},{1,2},{2,1},{3,4},{4,3},{5,6},{6,5},{7,8},{8,7},{9,10},{10,... | collective-permute-start | bytes 786440 | tf_op jit(solution)/shard_map/ppermute | solution.py:234
  17.5 0.0 copy-start.5
  17.5 0.0 copy-start.4
  17.5 0.0 copy-start.6
  17.5 0.0 copy-start.2
  17.6 0.0 copy-start.3
  17.6 0.0 copy-done.1
  17.6 0.6 %copy-done.5 = s32[4,256]{1,0:T(4,128)S(1)} copy-done((s32[4,256]{1,0:T(4,128)S(1)}, s32[4,256]{1,0:T(4,128)}, u32[]{:S(2)}) %copy-start.5) | copy-done | bytes 4120
  18.2 0.0 copy-done.4
  18.2 0.0 copy-done.2
  18.3 0.0 copy-done.3
  18.3 1.3 %local.1 = (f32[16,72,128]{2,1,0:T(8,128)S(1)}, bf16[256,96]{1,0:T(8,128)(2,1)S(1)}, bf16[32,96]{1,0:T(8,128)(2,1)S(1)}, bf16[32,96]{1,0:T(8,128)(2,1)S(1)}, bf16[32,512]{1,0:T(8,128)(2,1)S(1)}) custom-call(s32[1]{0:T(128)} %bitcast.2.block_ref, f32[32,2,16,128]{3,2,1,0:T(8,128)S(1)} %bitcast.15, f32[2,16,128]{2,1,0:T(8,128)S(1)} %copy-done.2, ...), custom_call_target="tpu_custom_call" | custom-call | tf_op jit(solution)/shard_map/local/pallas_call | solution.py:240
  19.7 0.0 collective-permute-done.2
  19.7 0.0 collective-permute-done
  19.7 3.5 %collective-permute-done.1 = f32[32,16,128]{2,1,0:T(8,128)S(1)} collective-permute-done((f32[32,16,128]{2,1,0:T(8,128)S(1)}, f32[32,16,128]{2,1,0:T(8,128)S(1)}, u32[]{:S(2)}, u32[]{:S(2)}) %collective-permute-start.1) | collective-permute-done | bytes 262176 | tf_op jit(solution)/shard_map/ppermute | solution.py:234
  23.1 0.4 halo.1
  23.6 16.6 %all_to_all.10.in_ref = f32[16,72,128]{2,1,0:T(8,128)S(1)} all-to-all(f32[16,72,128]{2,1,0:T(8,128)S(1)} %halo.1), channel_id=1, replica_groups={{416,32,256,96,192,320,288,160,448,480,352,0,128,384,224,64},{417,33,25..., dimensions={0} | all-to-all | bytes 1179648 | tf_op jit(solution)/shard_map/all_to_all | solution.py:265
  40.1 2.3 %react.1 = f32[16,64,128]{2,1,0:T(8,128)S(1)} custom-call(f32[16,72,128]{2,1,0:T(8,128)S(1)} %all_to_all.10.in_ref, f32[2,128]{1,0:T(2,128)S(1)} %bitcast.20, bf16[256,96]{1,0:T(8,128)(2,1)S(1)} %get-tuple-element.23.pairs_ref, bf16[32,96]{1,0:T(8,128)(2,1)S(1)} %get-tuple-element.24.partner_ref, bf16[32,96]{1,0:T(8,128)(2,1)S(1)} %get-tuple-element.25.squares_ref, ...), custom_call_target="tpu_custom_call" | custom-call | tf_op jit(solution)/shard_map/react/pallas_call | solution.py:266
  42.4 14.4 %all_to_all.11.in_ref = f32[16,64,128]{2,1,0:T(8,128)S(1)} all-to-all(f32[16,64,128]{2,1,0:T(8,128)S(1)} %react.1), channel_id=1, replica_groups={{416,32,256,96,192,320,288,160,448,480,352,0,128,384,224,64},{417,33,25..., dimensions={0} | all-to-all | bytes 1048576 | tf_op jit(solution)/shard_map/all_to_all | solution.py:275
  56.8 0.9 %home.1 = f32[1024,128]{1,0:T(8,128)} custom-call(f32[16,64,128]{2,1,0:T(8,128)S(1)} %all_to_all.11.in_ref), custom_call_target="tpu_custom_call" | custom-call | tf_op jit(solution)/shard_map/home/pallas_call | solution.py:276
  (4 shorter events, 0.0 us)
Async XLA Ops:
  0.0 19.6 %copy-start = (f32[2,16,128]{2,1,0:T(8,128)S(1)}, f32[2,16,128]{2,1,0:T(8,128)}, u32[]{:S(2)}) copy-start(f32[2,16,128]{2,1,0:T(8,128)} %param.11) | copy-start | bytes 49156
  0.0 17.6 %copy-start.1 = (f32[1,32,2,16,128]{4,3,2,1,0:T(8,128)S(1)}, f32[1,32,2,16,128]{4,3,2,1,0:T(8,128)}, u32[]{:S(2)}) copy-start(f32[1,32,2,16,128]{4,3,2,1,0:T(8,128)} %param.8) | copy-start | bytes 1572868
  1.1 18.5 %collective-permute-start.2 = (f32[32,16,128]{2,1,0:T(8,128)S(1)}, f32[32,16,128]{2,1,0:T(8,128)S(1)}, u32[]{:S(2)}, u32[]{:S(2)}) collective-permute-start(f32[32,16,128]{2,1,0:T(8,128)S(1)} %get-tuple-element.28), channel_id=1, source_target_pairs={{8,9},{9,8},{10,11},{11,10},{12,13},{13,12},{14,15},{15,14},{24,25... | collective-permute-start | bytes 786440 | tf_op jit(solution)/shard_map/ppermute | solution.py:235
  1.8 17.9 %collective-permute-start = (f32[32,16,128]{2,1,0:T(8,128)S(1)}, f32[32,16,128]{2,1,0:T(8,128)S(1)}, u32[]{:S(2)}, u32[]{:S(2)}) collective-permute-start(f32[32,16,128]{2,1,0:T(8,128)S(1)} %get-tuple-element.28), channel_id=1, source_target_pairs={{0,1},{1,0},{2,3},{3,2},{4,5},{5,4},{6,7},{7,6},{16,17},{17,16},{1... | collective-permute-start | bytes 786440 | tf_op jit(solution)/shard_map/ppermute | solution.py:233
  6.2 16.9 %collective-permute-start.1 = (f32[32,16,128]{2,1,0:T(8,128)S(1)}, f32[32,16,128]{2,1,0:T(8,128)S(1)}, u32[]{:S(2)}, u32[]{:S(2)}) collective-permute-start(f32[32,16,128]{2,1,0:T(8,128)S(1)} %get-tuple-element.27), channel_id=1, source_target_pairs={{0,31},{1,2},{2,1},{3,4},{4,3},{5,6},{6,5},{7,8},{8,7},{9,10},{10,... | collective-permute-start | bytes 786440 | tf_op jit(solution)/shard_map/ppermute | solution.py:234
  17.5 0.7 %copy-start.5 = (s32[4,256]{1,0:T(4,128)S(1)}, s32[4,256]{1,0:T(4,128)}, u32[]{:S(2)}) copy-start(s32[4,256]{1,0:T(4,128)} %stoich_ref.1) | copy-start | bytes 12292
  17.5 0.7 %copy-start.4 = (s32[1,32,32]{2,1,0:T(8,128)S(1)}, s32[1,32,32]{2,1,0:T(8,128)}, u32[]{:S(2)}) copy-start(s32[1,32,32]{2,1,0:T(8,128)} %param.14) | copy-start | bytes 12292
  17.5 0.7 %copy-start.6 = (f32[256]{0:T(256)S(1)}, f32[256]{0:T(256)}, u32[]{:S(2)}) copy-start(f32[256]{0:T(256)} %param.12) | copy-start | bytes 3076
  17.5 0.7 %copy-start.2 = (f32[2,16,128]{2,1,0:T(8,128)S(1)}, f32[2,16,128]{2,1,0:T(8,128)}, u32[]{:S(2)}) copy-start(f32[2,16,128]{2,1,0:T(8,128)} %dif_ref.3) | copy-start | bytes 49156
  17.6 0.7 %copy-start.3 = (f32[2,16,128]{2,1,0:T(8,128)S(1)}, f32[2,16,128]{2,1,0:T(8,128)}, u32[]{:S(2)}) copy-start(f32[2,16,128]{2,1,0:T(8,128)} %vel_ref.3) | copy-start | bytes 49156
